TPU v7x, 32 devices: a whole 2x2x4 slice. The times are simulated.
32 devices in a mesh: dp: 8 (over z, y), tensor: 4 (over x, core).
Axes of the slice: x: 2, y: 2, z: 4, core: 2. Of those that a mesh axis runs over, the one named last changes fastest.
Arguments:
- inputs: bfloat16 [25088, 512], P(('dp', 'tensor')), may hold values from -6 to 6
- image_count: int32 [8], P('dp'), may hold values from 15 to 16, as said below
- rel_index: int32 [49, 49], replicated, may hold values from 0 to 168, as said below
- rel_table: float32 [169, 16], P(None, 'tensor'), may hold values from -8 to 400
- norm1_gain: float32 [512], replicated, may hold values from 0.5 to 1.5
- norm1_shift: float32 [512], replicated, may hold values from -3 to 3
- w_qkv: bfloat16 [3, 512, 512], P(None, None, 'tensor'), may hold values from -0.25 to 0.25
- bias_qv: float32 [2, 512], P(None, 'tensor'), may hold values from -3 to 3
- w_proj: bfloat16 [512, 512], P('tensor'), may hold values from -0.625 to 0.625
- b_proj: float32 [512], replicated, may hold values from -2 to 2
- norm2_gain: float32 [512], replicated, may hold values from 0.5 to 1.5
- norm2_shift: float32 [512], replicated, may hold values from -3 to 3
- w_fc1: bfloat16 [512, 2048], P(None, 'tensor'), may hold values from -0.25 to 0.25
- b_fc1: float32 [2048], P('tensor'), may hold values from -3 to 3
- w_fc2: bfloat16 [2048, 512], P('tensor'), may hold values from -0.1875 to 0.1875
- b_fc2: float32 [512], replicated, may hold values from -2 to 2
- out_grad: bfloat16 [25088, 512], P(('dp', 'tensor')), may hold values from -6 to 6
Outputs:
- outputs: bfloat16 [25088, 512], P(('dp', 'tensor'))
- in_grad: bfloat16 [25088, 512], P(('dp', 'tensor'))
- g_table: float32 [169, 16], P(None, 'tensor')
- g_norm1_gain: float32 [512], replicated
- g_norm1_shift: float32 [512], replicated
- g_qkv: float32 [3, 512, 512], P(None, None, 'tensor')
- g_bias_qv: float32 [2, 512], P(None, 'tensor')
- g_proj: float32 [512, 512], P('tensor')
- g_b_proj: float32 [512], replicated
- g_norm2_gain: float32 [512], replicated
- g_norm2_shift: float32 [512], replicated
- g_fc1: float32 [512, 2048], P(None, 'tensor')
- g_b_fc1: float32 [2048], P('tensor')
- g_fc2: float32 [2048, 512], P('tensor')
- g_b_fc2: float32 [512], replicated
Inputs may be any that keep to these rules, and one draw needn't show every extreme that they name: `image_count`: each value is 15 or 16; both occur in every draw. `rel_index`: entries for equal offsets between query and key position are equal, unequal offsets give unequal entries.
All inputs are finite; a program needn't handle non-finite values.
Results may differ from a plain program's by a relative error of at most 0.015.
Values may be sent and summed in bfloat16 or wider, within the bound.
No kernel may reach another device: no remote copies, remote signals or barrier semaphores. Data moves between devices by JAX's collectives and lax.ppermute only.
A program may use at most 128 MiB of HBM per device.

v0:
```python
import jax
import jax.numpy as jnp
from jax import lax
from jax.sharding import PartitionSpec as P

HEAD_DIM = 32
WINDOW = 49
OFFSETS = 169
IMG_TOKENS = 196


eps = 1e-05


def norm_forward(values, gain, shift):
    mean = jnp.mean(values, axis=-1, keepdims=True)
    centred = values - mean
    var = jnp.mean(centred * centred, axis=-1, keepdims=True)
    scale_inv = lax.rsqrt(var + eps)
    normed = centred * scale_inv
    return (normed * gain + shift, normed, scale_inv)


def norm_backward(grad, normed, scale_inv, gain):
    scaled = grad * gain
    return scale_inv * (
        scaled
        - jnp.mean(scaled, axis=-1, keepdims=True)
        - normed * jnp.mean(scaled * normed, axis=-1, keepdims=True)
    )


def gelu_parts(pre):
    cdf = 0.5 * (1.0 + lax.erf(pre * 0.7071067811865476))
    dens = jnp.exp(-0.5 * pre * pre) * 0.3989422804014327
    return (pre * cdf, cdf + pre * dens)


def outer_dot(left, right):
    return lax.dot_general(
        left, right, (((0,), (0,)), ((), ())), preferred_element_type=jnp.float32
    )


def inner_t(left, right):
    return lax.dot_general(
        left, right, (((1,), (1,)), ((), ())), preferred_element_type=jnp.float32
    )


def project_qkv(normed_rows, weights, biases, scale):
    qs = (
        (jnp.dot(normed_rows, weights[0], preferred_element_type=jnp.float32) + biases[0]) * scale
    ).astype(jnp.bfloat16)
    kk = jnp.dot(normed_rows, weights[1], preferred_element_type=jnp.float32).astype(jnp.bfloat16)
    vv = (jnp.dot(normed_rows, weights[2], preferred_element_type=jnp.float32) + biases[1]).astype(
        jnp.bfloat16
    )
    return (qs, kk, vv)


def window_attention(qs, kk, vv, bias, windows, heads):
    qw = qs.reshape(windows, WINDOW, heads, HEAD_DIM)
    kw = kk.reshape(windows, WINDOW, heads, HEAD_DIM)
    vw = vv.reshape(windows, WINDOW, heads, HEAD_DIM)
    scores = jnp.einsum("nqhe,nkhe->nhqk", qw, kw, preferred_element_type=jnp.float32) + bias[None]
    top = jnp.max(scores, axis=-1, keepdims=True)
    lse = top + jnp.log(jnp.sum(jnp.exp(scores - top), axis=-1, keepdims=True))
    pb = jnp.exp(scores - lse).astype(jnp.bfloat16)
    att = jnp.einsum("nhqk,nkhe->nqhe", pb, vw, preferred_element_type=jnp.float32)
    att_out = att.reshape(windows * WINDOW, heads * HEAD_DIM).astype(jnp.bfloat16)
    return (att_out, lse, qw, kw, vw)


def window_backward(datt, qw, kw, vw, bias, lse, onehot, scale):
    windows = qw.shape[0]
    heads = qw.shape[2]
    rows = windows * WINDOW
    width = heads * HEAD_DIM
    dw = datt.reshape(windows, WINDOW, heads, HEAD_DIM)
    probs_again = jnp.exp(
        jnp.einsum("nqhe,nkhe->nhqk", qw, kw, preferred_element_type=jnp.float32) + bias[None] - lse
    )
    pb_again = probs_again.astype(jnp.bfloat16)
    dvv = jnp.einsum("nhqk,nqhe->nkhe", pb_again, dw, preferred_element_type=jnp.float32)
    dprobs = jnp.einsum("nqhe,nkhe->nhqk", dw, vw, preferred_element_type=jnp.float32)
    dscores = probs_again * (dprobs - jnp.sum(probs_again * dprobs, axis=-1, keepdims=True))
    g_tab = jnp.einsum(
        "qkt,hqk->th", onehot, jnp.sum(dscores, axis=0), precision=lax.Precision.HIGHEST
    )
    dsb = dscores.astype(jnp.bfloat16)
    dq = (
        jnp.einsum("nhqk,nkhe->nqhe", dsb, kw, preferred_element_type=jnp.float32) * scale
    ).reshape(rows, width)
    dk = jnp.einsum("nhqk,nqhe->nkhe", dsb, qw, preferred_element_type=jnp.float32).reshape(
        rows, width
    )
    dv = dvv.reshape(rows, width)
    g_bqv = jnp.stack([jnp.sum(dq, axis=0), jnp.sum(dv, axis=0)])
    dqkv = jnp.stack([dq, dk, dv]).astype(jnp.bfloat16)
    return (g_tab, g_bqv, dqkv)


def local(
    inputs,
    image_count,
    rel_index,
    rel_table,
    norm1_gain,
    norm1_shift,
    w_qkv,
    bias_qv,
    w_proj,
    b_proj,
    norm2_gain,
    norm2_shift,
    w_fc1,
    b_fc1,
    w_fc2,
    b_fc2,
    out_grad,
):
    local_rows = inputs.shape[0]
    scale = HEAD_DIM ** (-0.5)
    row_ids = lax.axis_index("tensor") * local_rows + jnp.arange(local_rows, dtype=jnp.int32)
    live = (row_ids // IMG_TOKENS < image_count[0]).astype(jnp.float32)[:, None]
    onehot = (rel_index[:, :, None] == jnp.arange(OFFSETS, dtype=jnp.int32)[None, None, :]).astype(
        jnp.float32
    )
    x32 = inputs.astype(jnp.float32)
    xn1f, normed1, rs1 = norm_forward(x32, norm1_gain, norm1_shift)
    xn1_local = xn1f.astype(jnp.bfloat16)
    gout = out_grad.astype(jnp.float32) * live
    gout_local = gout.astype(jnp.bfloat16)
    g_b_fc2 = jnp.sum(gout, axis=0)
    local_heads = rel_table.shape[1]
    group_rows = local_rows * lax.axis_size("tensor")
    bias = jnp.einsum("qkt,th->hqk", onehot, rel_table, precision=lax.Precision.HIGHEST)
    xn1 = lax.all_gather(xn1_local, "tensor", axis=0, tiled=True)
    qs, kk, vv = project_qkv(xn1, w_qkv, bias_qv, scale)
    att_out, lse, qw, kw, vw = window_attention(qs, kk, vv, bias, group_rows // WINDOW, local_heads)
    rows = att_out
    attn_part = lax.psum_scatter(
        jnp.dot(rows, w_proj, preferred_element_type=jnp.float32),
        "tensor",
        scatter_dimension=0,
        tiled=True,
    )
    mid = x32 + (attn_part + b_proj)
    xn2f, normed2, rs2 = norm_forward(mid, norm2_gain, norm2_shift)
    xn2 = lax.all_gather(xn2f.astype(jnp.bfloat16), "tensor", axis=0, tiled=True)
    pre = jnp.dot(xn2, w_fc1, preferred_element_type=jnp.float32) + b_fc1
    act, slope = gelu_parts(pre)
    hidden = act.astype(jnp.bfloat16)
    rows = hidden
    mlp_part = lax.psum_scatter(
        jnp.dot(rows, w_fc2, preferred_element_type=jnp.float32).astype(jnp.bfloat16),
        "tensor",
        scatter_dimension=0,
        tiled=True,
    ).astype(jnp.float32)
    outputs = (live * (mid + mlp_part + b_fc2)).astype(jnp.bfloat16)
    gout_rows = lax.all_gather(gout_local, "tensor", axis=0, tiled=True)
    g_fc2 = outer_dot(hidden, gout_rows)
    dpre = inner_t(gout_rows, w_fc2) * slope
    g_b_fc1 = jnp.sum(dpre, axis=0)
    dpre_b = dpre.astype(jnp.bfloat16)
    g_fc1 = outer_dot(xn2, dpre_b)
    rows = dpre_b
    dxn2 = lax.psum_scatter(inner_t(rows, w_fc1), "tensor", scatter_dimension=0, tiled=True)
    g_n2g = jnp.sum(dxn2 * normed2, axis=0)
    g_n2s = jnp.sum(dxn2, axis=0)
    dmid = gout + norm_backward(dxn2, normed2, rs2, norm2_gain)
    g_bp = jnp.sum(dmid, axis=0)
    dmid_rows = lax.all_gather(dmid.astype(jnp.bfloat16), "tensor", axis=0, tiled=True)
    g_proj = outer_dot(att_out, dmid_rows)
    datt = inner_t(dmid_rows, w_proj).astype(jnp.bfloat16)
    g_tab, g_bqv, dqkv = window_backward(datt, qw, kw, vw, bias, lse, onehot, scale)
    g_qkv = jnp.einsum("rd,cre->cde", xn1, dqkv, preferred_element_type=jnp.float32)
    rows = dqkv
    dxn1 = lax.psum_scatter(
        jnp.einsum("cre,cde->rd", rows, w_qkv, preferred_element_type=jnp.float32).astype(
            jnp.bfloat16
        ),
        "tensor",
        scatter_dimension=0,
        tiled=True,
    ).astype(jnp.float32)
    g_n1g = jnp.sum(dxn1 * normed1, axis=0)
    g_n1s = jnp.sum(dxn1, axis=0)
    in_grad = (dmid + norm_backward(dxn1, normed1, rs1, norm1_gain)).astype(jnp.bfloat16)
    g_tab, g_qkv, g_bqv, g_proj, g_fc1, g_b_fc1, g_fc2 = (
        lax.psum(g_tab.astype(jnp.bfloat16), "dp").astype(jnp.float32),
        lax.psum(g_qkv.astype(jnp.bfloat16), "dp").astype(jnp.float32),
        lax.psum(g_bqv.astype(jnp.bfloat16), "dp").astype(jnp.float32),
        lax.psum(g_proj.astype(jnp.bfloat16), "dp").astype(jnp.float32),
        lax.psum(g_fc1.astype(jnp.bfloat16), "dp").astype(jnp.float32),
        lax.psum(g_b_fc1.astype(jnp.bfloat16), "dp").astype(jnp.float32),
        lax.psum(g_fc2.astype(jnp.bfloat16), "dp").astype(jnp.float32),
    )
    g_n1g, g_n1s, g_bp, g_n2g, g_n2s, g_b_fc2 = lax.psum(
        (g_n1g, g_n1s, g_bp, g_n2g, g_n2s, g_b_fc2), ("dp", "tensor")
    )
    return (
        outputs,
        in_grad,
        g_tab,
        g_n1g,
        g_n1s,
        g_qkv,
        g_bqv,
        g_proj,
        g_bp,
        g_n2g,
        g_n2s,
        g_fc1,
        g_b_fc1,
        g_fc2,
        g_b_fc2,
    )


def solution(mesh):
    placed = (
        P(("dp", "tensor"), None),
        P("dp"),
        P(),
        P(None, "tensor"),
        P(),
        P(),
        P(None, None, "tensor"),
        P(None, "tensor"),
        P("tensor", None),
        P(),
        P(),
        P(),
        P(None, "tensor"),
        P("tensor"),
        P("tensor", None),
        P(),
        P(("dp", "tensor"), None),
    )
    return jax.shard_map(
        local,
        mesh=mesh,
        in_specs=placed,
        out_specs=(
            P(("dp", "tensor"), None),
            P(("dp", "tensor"), None),
            P(None, "tensor"),
            P(),
            P(),
            P(None, None, "tensor"),
            P(None, "tensor"),
            P("tensor", None),
            P(),
            P(),
            P(),
            P(None, "tensor"),
            P("tensor"),
            P("tensor", None),
            P(),
        ),
        check_vma=False,
    )
```

profile of v0, /device:TPU:0, one launch (start us, length us, event | category | flops | bytes accessed | tf_op | source)
XLA Modules:
  0.0 638.7 jit_solution(3990552281167432014)
XLA Ops:
  10.8 2.4 fusion.24
  13.4 2.0 fusion.49
  15.4 29.6 %all-gather.5.cloned.1.call-done = bf16[3136,512]{1,0:T(8,128)(2,1)} async-done(((bf16[784,512]{1,0:T(8,128)(2,1)}), bf16[3136,512]{1,0:T(8,128)(2,1)}) %all-gather.5.cloned.1.call-update) | async-done | bytes 3211280 | tf_op jit(solution)/shard_map/all_gather | solution.py:139
  45.0 2.9 convolution_convert_fusion.2
  47.9 2.7 reshape.136
  50.6 5.7 copy.106
  56.3 3.7 fusion.7
  59.9 2.5 reshape.134
  62.4 5.8 copy.109
  68.2 2.9 fusion.6
  71.2 2.5 reshape.135
  73.7 5.8 copy.105
  79.5 3.7 add_reduce_fusion
  83.2 2.4 exponential_reduce_fusion
  89.4 3.5 convert_element_type.131
  93.0 4.8 fusion.70
  97.9 59.8 %reduce-scatter.5.cloned.1.call-done = f32[784,512]{1,0:T(8,128)} async-done(((f32[3136,512]{1,0:T(8,128)}), f32[784,512]{1,0:T(8,128)}) %reduce-scatter.5.cloned.1.call-update) | async-done | bytes 1605648 | tf_op jit(solution)/shard_map/reduce_scatter | solution.py:143
  157.7 1.7 fusion.68
  161.8 2.3 fusion.37
  164.1 26.0 %all-gather.7.cloned.1.call-done = bf16[3136,512]{1,0:T(8,128)(2,1)} async-done(((bf16[784,512]{1,0:T(8,128)(2,1)}), bf16[3136,512]{1,0:T(8,128)(2,1)}) %all-gather.7.cloned.1.call-update) | async-done | bytes 3211280 | tf_op jit(solution)/shard_map/all_gather | solution.py:151
  190.1 6.7 %multiply_convert_fusion = (bf16[3136,512]{1,0:T(8,128)(2,1)}, f32[3136,512]{1,0:T(8,128)}) fusion(f32[512]{0:T(512)S(1)} %copy-done.46, bf16[3136,512]{1,0:T(8,128)(2,1)} %all-gather.7.cloned.1.call-done, bf16[512,512]{1,0:T(8,128)(2,1)S(1)} %copy-done), kind=kOutput, calls=%fused_computation.13 | convolution fusion | flops 1653800960 | bytes 13371392 | tf_op jit(solution)/shard_map/dot_general | solution.py:152
  196.8 24.2 %all-gather.9.cloned.1.call-done = bf16[3136,512]{1,0:T(8,128)(2,1)} async-done(((bf16[784,512]{1,0:T(8,128)(2,1)}), bf16[3136,512]{1,0:T(8,128)(2,1)}) %all-gather.9.cloned.1.call-update) | async-done | bytes 3211280 | tf_op jit(solution)/shard_map/all_gather | solution.py:163
  221.0 7.0 %fusion.69 = (bf16[512]{0:T(512)(128)(2,1)S(1)}, bf16[3136,512]{1,0:T(8,128)(2,1)S(1)}) fusion(f32[3136,512]{1,0:T(8,128)} %get-tuple-element.109, bf16[3136,512]{1,0:T(8,128)(2,1)} %all-gather.9.cloned.1.call-done, bf16[512,512]{1,0:T(8,128)(2,1)} %param.31), kind=kOutput, calls=%fused_computation.120 | convolution fusion | flops 1661828608 | bytes 13370368 | tf_op jit(solution)/shard_map/dot_general | solution.py:46
  228.0 1.6 copy-done.17
  229.7 4.6 fusion.34
  235.3 5.7 convolution_convert_fusion
  241.1 53.1 %reduce-scatter.9.cloned.1.call-done = f32[784,512]{1,0:T(8,128)} async-done(((f32[3136,512]{1,0:T(8,128)}), f32[784,512]{1,0:T(8,128)}) %reduce-scatter.9.cloned.1.call-update) | async-done | bytes 1605648 | tf_op jit(solution)/shard_map/reduce_scatter | solution.py:170
  294.2 2.8 multiply_reduce_fusion.1
  297.0 37.9 %reduce-scatter.7.cloned.1.call-done = bf16[784,512]{1,0:T(8,128)(2,1)} async-done(((bf16[3136,512]{1,0:T(8,128)(2,1)}), bf16[784,512]{1,0:T(8,128)(2,1)}) %reduce-scatter.7.cloned.1.call-update) | async-done | bytes 802832 | tf_op jit(solution)/shard_map/reduce_scatter | solution.py:156
  335.0 3.8 fusion.66
  341.0 5.8 convolution_convert_fusion.3
  346.8 2.7 fusion.40
  349.5 20.5 %all-gather.11.cloned.1.call-done = bf16[3136,512]{1,0:T(8,128)(2,1)} async-done(((bf16[784,512]{1,0:T(8,128)(2,1)}), bf16[3136,512]{1,0:T(8,128)(2,1)}) %all-gather.11.cloned.1.call-update) | async-done | bytes 3211280 | tf_op jit(solution)/shard_map/all_gather | solution.py:175
  370.0 2.9 convolution_convert_fusion.1
  372.9 2.7 reshape.137
  375.6 5.8 copy.113
  381.5 8.0 %fusion.52 = f32[64,4,32,49]{3,2,1,0:T(8,128)} fusion(bf16[64,49,4,32]{1,3,2,0:T(8,128)(2,1)} %copy.113, f32[64,4,49,49]{2,3,1,0:T(8,128)} %copy-done.2, f32[64,4,49]{2,1,0:T(4,128)S(1)} %bitcast.91, f32[4,49,49]{1,2,0:T(8,128)S(1)} %copy.108), kind=kOutput, calls=%fused_computation.86 | convolution fusion | flops 41181952 | bytes 4955664 | tf_op jit(solution)/shard_map/nhqk,nqhe->nkhe/dot_general | solution.py:85
  389.5 6.2 multiply_reduce_fusion
  395.7 2.7 fusion.67
  398.4 3.4 convert_bitcast_fusion
  401.9 3.1 fusion.21
  405.0 6.4 copy.124
  411.4 2.4 bitcast_convert_fusion
  413.7 4.3 copy.137
  418.0 4.7 reshape.133
  422.8 6.6 %copy.117 = f32[64,4,32,49]{0,2,1,3:T(8,128)} copy(f32[64,4,32,49]{3,2,1,0:T(8,128)} %fusion.21) | data formatting | bytes 3211264 | tf_op jit(solution)/shard_map/nhqk,nkhe->nqhe/dot_general | solution.py:93
  429.4 2.4 bitcast_convert_fusion.1
  431.8 5.9 copy.136
  437.7 4.7 reshape.132
  442.4 4.3 copy.135
  446.7 4.9 reshape.131
  455.4 2.3 fusion.46
  457.7 5.2 fusion.4
  463.0 2.4 bitcast_reduce_fusion
  465.4 2.4 bitcast_reduce_fusion.1
  469.0 22.1 %all-reduce.1 = (bf16[169,4]{0,1:T(4,128)(2,1)S(1)}, bf16[2,128]{1,0:T(2,128)(2,1)S(1)}, bf16[512]{0:T(512)(128)(2,1)S(1)}) all-reduce(bf16[169,4]{0,1:T(4,128)(2,1)S(1)} %fusion.51, bf16[2,128]{1,0:T(2,128)(2,1)S(1)} %pad_maximum_fusion, bf16[512]{0:T(512)(128)(2,1)S(1)} %get-tuple-element.112), channel_id=1, replica_groups=mesh['dp'=8,'tensor'=4] {'dp'}, use_global_device_ids=true, to_apply=%region_16.17 | all-reduce | flops 1444 | bytes 5776 | tf_op jit(solution)/shard_map/psum | solution.py:193
  492.9 54.7 %all-reduce.5.cloned.1.call-done = (bf16[3,512,128]{1,2,0:T(8,128)(2,1)}, bf16[128,512]{1,0:T(8,128)(2,1)}, bf16[512,512]{1,0:T(8,128)(2,1)}, bf16[512,512]{1,0:T(8,128)(2,1)}) async-done(((bf16[3,512,128]{1,2,0:T(8,128)(2,1)}, bf16[128,512]{1,0:T(8,128)(2,1)}, bf16[512,512]{1,0:T(8,128)(2,1)}, bf16[512,512]{1,0:T(8,128)(2,1)}), (bf16[3,512,128]{1,2,0:T(8,128)(2,1)}, bf16[128,512]{1,0:T(8,128)(2,1)}, ...) | async-done | bytes 1572880 | tf_op jit(solution)/shard_map/psum | solution.py:194
  547.5 1.7 convert_element_type.153
  549.2 2.0 copy.130
  551.3 2.1 convert_element_type.155
  554.5 33.1 %reduce-scatter.11.cloned.1.call-done = bf16[784,512]{1,0:T(8,128)(2,1)} async-done(((bf16[3136,512]{1,0:T(8,128)(2,1)}), bf16[784,512]{1,0:T(8,128)(2,1)}) %reduce-scatter.11.cloned.1.call-update) | async-done | bytes 802832 | tf_op jit(solution)/shard_map/reduce_scatter | solution.py:181
  587.7 2.1 fusion.31
  589.8 39.5 %all-reduce = (f32[512]{0:T(512)}, f32[512]{0:T(512)}, f32[512]{0:T(512)}, f32[512]{0:T(512)}, f32[512]{0:T(512)}, /*index=5*/f32[512]{0:T(512)}) all-reduce(f32[512]{0:T(512)S(1)} %get-tuple-element.77, f32[512]{0:T(512)S(1)} %get-tuple-element.82, f32[512]{0:T(512)S(1)} %copy-done.37, ...), channel_id=1, replica_groups=mesh['dp'=8,'tensor'=4] {'dp','tensor'}, use_global_device_ids=true, to_apply=%region_18.19 | all-reduce | flops 3072 | bytes 24576 | tf_op jit(solution)/shard_map/psum | solution.py:201
  629.3 2.6 fusion.28
  (147 shorter events, 20.7 us)
Async XLA Ops:
  7.2 182.9 %copy-start = (bf16[512,512]{1,0:T(8,128)(2,1)S(1)}, bf16[512,512]{1,0:T(8,128)(2,1)}, u32[]{:S(2)}) copy-start(bf16[512,512]{1,0:T(8,128)(2,1)} %param.29) | copy-start | bytes 1572868
  7.2 6.1 copy-start.30
  7.2 6.2 copy-start.45
  7.2 8.2 %copy-start.42 = (f32[2,128]{1,0:T(2,128)S(1)}, f32[2,128]{1,0:T(2,128)}, u32[]{:S(2)}) copy-start(f32[2,128]{1,0:T(2,128)} %param.24) | copy-start | bytes 3076
  7.2 37.8 %all-gather.5.cloned.1.call-start = ((), (), s32[]{:S(2)}) async-start(), calls=%async_computation.4 | async-start | bytes 4014080 | tf_op jit(solution)/shard_map/all_gather | solution.py:139
  8.7 1.5 copy-start.26
  10.2 0.6 copy-start.28
  13.2 144.5 %reduce-scatter.5.cloned.1.call-start = ((), (), s32[]{:S(2)}) async-start(), calls=%async_computation.5 | async-start | bytes 8028160 | tf_op jit(solution)/shard_map/reduce_scatter | solution.py:143
  13.4 2.0 copy-start.31
  56.3 23.2 %copy-start.6 = (bf16[64,49,4,32]{1,3,2,0:T(8,128)(2,1)}, bf16[64,49,4,32]{1,3,2,0:T(8,128)(2,1)S(1)}, u32[]{:S(2)}) copy-start(bf16[64,49,4,32]{1,3,2,0:T(8,128)(2,1)S(1)} %copy.106) | copy-start | bytes 2408452
  83.2 3.2 copy-start.2
  83.2 3.2 copy-start.9
  85.7 2.4 copy-start.19
  93.0 4.8 copy-start.14
  97.8 59.9 %copy-start.4 = (bf16[784,512]{1,0:T(8,128)(2,1)S(1)}, bf16[784,512]{1,0:T(8,128)(2,1)}, u32[]{:S(2)}) copy-start(bf16[784,512]{1,0:T(8,128)(2,1)} %param.17) | copy-start | bytes 2408452
  97.8 59.9 %copy-start.39 = (f32[512]{0:T(512)S(1)}, f32[512]{0:T(512)}, u32[]{:S(2)}) copy-start(f32[512]{0:T(512)} %param.26) | copy-start | bytes 6148
  97.8 62.0 %copy-start.34 = (f32[512]{0:T(512)S(1)}, f32[512]{0:T(512)}, u32[]{:S(2)}) copy-start(f32[512]{0:T(512)} %param.27) | copy-start | bytes 6148
  97.8 62.0 %copy-start.40 = (f32[512]{0:T(512)S(1)}, f32[512]{0:T(512)}, u32[]{:S(2)}) copy-start(f32[512]{0:T(512)} %param.28) | copy-start | bytes 6148
  97.9 92.3 %all-gather.7.cloned.1.call-start = ((), (), s32[]{:S(2)}) async-start(), calls=%async_computation.6 | async-start | bytes 4014080 | tf_op jit(solution)/shard_map/all_gather | solution.py:151
  159.8 30.3 %copy-start.46 = (f32[512]{0:T(512)S(1)}, f32[512]{0:T(512)}, u32[]{:S(2)}) copy-start(f32[512]{0:T(512)} %param.30) | copy-start | bytes 6148
  161.1 59.9 %all-gather.9.cloned.1.call-start = ((), (), s32[]{:S(2)}) async-start(), calls=%async_computation.8 | async-start | bytes 4014080 | tf_op jit(solution)/shard_map/all_gather | solution.py:163
  164.1 130.1 %reduce-scatter.9.cloned.1.call-start = ((), (), s32[]{:S(2)}) async-start(), calls=%async_computation.9 | async-start | bytes 8028160 | tf_op jit(solution)/shard_map/reduce_scatter | solution.py:170
  228.0 1.7 copy-start.17
  234.3 1.0 copy-start.44
  234.3 100.7 %reduce-scatter.7.cloned.1.call-start = ((), (), s32[]{:S(2)}) async-start(), calls=%async_computation.7 | async-start | bytes 4014080 | tf_op jit(solution)/shard_map/reduce_scatter | solution.py:156
  241.0 94.0 %copy-start.41 = (f32[512]{0:T(512)S(1)}, f32[512]{0:T(512)}, u32[]{:S(2)}) copy-start(f32[512]{0:T(512)} %param.32) | copy-start | bytes 6148
  241.0 129.0 %all-gather.11.cloned.1.call-start = ((), (), s32[]{:S(2)}) async-start(), calls=%async_computation.10 | async-start | bytes 4014080 | tf_op jit(solution)/shard_map/all_gather | solution.py:175
  338.8 1.2 copy-start.12
  340.9 206.6 %all-reduce.5.cloned.1.call-start = ((), (), s32[]{:S(2)}) async-start(), calls=%async_computation.12 | async-start | bytes 3145728 | tf_op jit(solution)/shard_map/psum | solution.py:194
  341.0 5.8 copy-start.18
  341.0 5.8 copy-start.43
  346.8 23.2 %copy-start.23 = (bf16[128,512]{1,0:T(8,128)(2,1)S(1)}, bf16[128,512]{1,0:T(8,128)(2,1)}, u32[]{:S(2)}) copy-start(bf16[128,512]{1,0:T(8,128)(2,1)} %param.25) | copy-start | bytes 393220
  375.6 5.8 copy-start.20
  381.5 8.0 %copy-start.10 = (bf16[64,49,4,32]{1,3,2,0:T(8,128)(2,1)S(1)}, bf16[64,49,4,32]{1,3,2,0:T(8,128)(2,1)}, u32[]{:S(2)}) copy-start(bf16[64,49,4,32]{1,3,2,0:T(8,128)(2,1)} %copy.109) | copy-start | bytes 2408452
  381.5 8.0 %copy-start.11 = (bf16[64,49,4,32]{1,3,2,0:T(8,128)(2,1)S(1)}, bf16[64,49,4,32]{1,3,2,0:T(8,128)(2,1)}, u32[]{:S(2)}) copy-start(bf16[64,49,4,32]{1,3,2,0:T(8,128)(2,1)} %copy.113) | copy-start | bytes 2408452
  381.5 14.2 %slice-start = ((s8[7340032]{0:T(1024)(128)(4,1)}), s8[4194304]{0:T(1024)(128)(4,1)S(1)}, s32[]{:S(2)}) async-start(s8[7340032]{0:T(1024)(128)(4,1)} %bitcast.88), calls=%async_computation.13 | async-start | bytes 8388608
  389.4 6.2 slice-start.1
  395.7 2.7 copy-start.8
  398.4 3.5 copy-start.7
  446.7 6.2 copy-start.22
  446.7 6.3 copy-start.21
  451.6 2.1 copy-start.5
  451.6 2.3 copy-start.15
  453.0 2.3 copy-start.3
  453.9 1.5 copy-start.16
  455.4 2.3 copy-start.25
  457.7 130.0 %reduce-scatter.11.cloned.1.call-start = ((), (), s32[]{:S(2)}) async-start(), calls=%async_computation.11 | async-start | bytes 4014080 | tf_op jit(solution)/shard_map/reduce_scatter | solution.py:181
  463.0 5.0 copy-start.32
  467.8 119.9 %copy-start.27 = (f32[784]{0:T(1024)S(1)}, f32[784]{0:T(1024)}, u32[]{:S(2)}) copy-start(f32[784]{0:T(1024)} %copy-done.26) | copy-start | bytes 9412
  467.8 119.9 %copy-start.29 = (f32[784]{0:T(1024)S(1)}, f32[784]{0:T(1024)}, u32[]{:S(2)}) copy-start(f32[784]{0:T(1024)} %copy-done.28) | copy-start | bytes 9412
  467.8 119.9 %copy-start.33 = (f32[512]{0:T(512)S(1)}, f32[512]{0:T(512)}, u32[]{:S(2)}) copy-start(f32[512]{0:T(512)} %param.21) | copy-start | bytes 6148
  468.9 120.8 %copy-start.35 = (f32[512]{0:T(512)S(1)}, f32[512]{0:T(512)}, u32[]{:S(2)}) copy-start(f32[512]{0:T(512)} %get-tuple-element.75) | copy-start | bytes 6148
  468.9 120.8 %copy-start.36 = (f32[512]{0:T(512)S(1)}, f32[512]{0:T(512)}, u32[]{:S(2)}) copy-start(f32[512]{0:T(512)} %get-tuple-element.80) | copy-start | bytes 6148
  469.0 120.8 %copy-start.37 = (f32[512]{0:T(512)S(1)}, f32[512]{0:T(512)}, u32[]{:S(2)}) copy-start(f32[512]{0:T(512)} %get-tuple-element.96) | copy-start | bytes 6148
  469.0 120.8 %copy-start.38 = (f32[512]{0:T(512)S(1)}, f32[512]{0:T(512)}, u32[]{:S(2)}) copy-start(f32[512]{0:T(512)} %get-tuple-element.103) | copy-start | bytes 6148
  469.0 160.3 %copy-start.13 = (f32[784,512]{1,0:T(8,128)S(1)}, f32[784,512]{1,0:T(8,128)}, u32[]{:S(2)}) copy-start(f32[784,512]{1,0:T(8,128)} %copy-done.12) | copy-start | bytes 4816900
  547.5 5.9 copy-start.24
  553.4 78.5 %copy-start.1 = (bf16[512,512]{1,0:T(8,128)(2,1)S(1)}, bf16[512,512]{1,0:T(8,128)(2,1)}, u32[]{:S(2)}) copy-start(bf16[512,512]{1,0:T(8,128)(2,1)} %param.29) | copy-start | bytes 1572868
Sparse Core Ops, SparseCore 0:
  13.4 31.5 all-gather.4
  97.9 59.7 reduce-scatter.4
  161.2 28.8 all-gather.6
  192.1 28.8 all-gather.8
  234.4 59.7 reduce-scatter.8
  296.6 38.2 reduce-scatter.6
  341.1 28.9 all-gather.10
  457.8 89.7 all-reduce.4
  550.1 37.5 reduce-scatter.10
where the time goes:
time: 644 us; the launch traced here: 639 us
  waiting for transfers between devices  339 us (53%)
  local copies, waits for them, and re-layouts  90.1 us (14%)
  matrix products  87.7 us (14%)
  blocking collectives  61.6 us (10%)
  other arithmetic  44.5 us (7%)
  between operations  15.3 us (2%)
    reduce_scatter x1, waiting for transfers between devices, local(): lax.psum_scatter(jnp.dot(rows, w_proj, preferred_element_type=jnp.float32...  59.8 us
    psum x1, waiting for transfers between devices, local(): lax.psum(g_qkv.astype(jnp.bfloat16), 'dp').astype(jnp.float32)  54.7 us
    reduce_scatter x1, waiting for transfers between devices, local(): lax.psum_scatter(inner_t(rows, w_fc1), 'tensor', scatter_dimension=0, til...  53.1 us
    psum x1, blocking collectives, local(): lax.psum((g_n1g, g_n1s, g_bp, g_n2g, g_n2s, g_b_fc2), ('dp', 'tensor'))  39.5 us
    reduce_scatter x1, waiting for transfers between devices, local(): lax.psum_scatter(jnp.dot(rows, w_fc2, preferred_element_type=jnp.float32)...  37.9 us
    reduce_scatter x1, waiting for transfers between devices, local(): lax.psum_scatter(jnp.einsum('cre,cde->rd', rows, w_qkv, preferred_element...  33.1 us
    all_gather x1, waiting for transfers between devices, local(): xn1 = lax.all_gather(xn1_local, 'tensor', axis=0, tiled=True)  29.6 us
    another operation x7, local copies, waits for them, and re-layouts, window_backward(): dqkv = jnp.stack([dq, dk, dv]).astype(jnp.bfloat16)  28.9 us
  transfers between devices with their start and end apart: 9, of which 9 were waited for; matrix products, arithmetic and copies ran while one was open for 8% of the time, Pallas kernels for 0%

commit v1 on v0

v1 whole, which is shorter than its diff:
```python
import functools

import jax
import jax.numpy as jnp
from jax import lax
from jax.experimental import pallas as pl
from jax.experimental.pallas import tpu as pltpu
from jax.sharding import PartitionSpec as P


IMG_TOKENS = 196
ROW_TILE = 16
CHUNK = 256
FAR_BELOW = -1e30

eps = 1e-05
f32 = jnp.float32
bf16 = jnp.bfloat16


def norm_forward(values, gain, shift):
    mean = jnp.mean(values, axis=-1, keepdims=True)
    centred = values - mean
    var = jnp.mean(centred * centred, axis=-1, keepdims=True)
    scale_inv = lax.rsqrt(var + eps)
    normed = centred * scale_inv
    return (normed * gain + shift, normed, scale_inv)


def norm_backward(grad, normed, scale_inv, gain):
    scaled = grad * gain
    return scale_inv * (
        scaled
        - jnp.mean(scaled, axis=-1, keepdims=True)
        - normed * jnp.mean(scaled * normed, axis=-1, keepdims=True)
    )


def gelu_parts(pre):
    cdf = 0.5 * (1.0 + lax.erf(pre * 0.7071067811865476))
    dens = jnp.exp(-0.5 * pre * pre) * 0.3989422804014327
    return (pre * cdf, cdf + pre * dens)


def dot(left, right, left_dim, right_dim):
    return lax.dot_general(
        left, right, (((left_dim,), (right_dim,)), ((), ())), preferred_element_type=f32
    )


def head_masks(heads, width):
    head_of = lax.broadcasted_iota(jnp.int32, (1, width), 1) // (width // heads)
    return [(head_of == h).astype(f32) for h in range(heads)]


def spread(value, masks):
    return jnp.concatenate([value * mask.astype(bf16) for mask in masks], axis=0)


def fold(value, masks):
    rows = value.shape[0] // len(masks)
    total = value[:rows] * masks[0]
    for h in range(1, len(masks)):
        total = total + value[h * rows : (h + 1) * rows] * masks[h]
    return total


def each_window(windows, body):
    together = 4 if windows % 4 == 0 else 1

    def step(i, carry):
        for j in range(together):
            body(i * together + j)
        return carry

    lax.fori_loop(0, windows // together, step, 0)


def attend_kernel(heads, scale, xn_ref, w_ref, vec_ref, bias_ref, qkv_ref, p_ref, att_ref):
    _, windows, padded, width = qkv_ref.shape
    xn = xn_ref[...]

    def put(c, value):
        qkv_ref[c] = value.astype(bf16).reshape(windows, padded, width)

    put(0, (dot(xn, w_ref[0], 1, 0) + vec_ref[:, :width]) * scale)
    put(1, dot(xn, w_ref[1], 1, 0))
    put(2, dot(xn, w_ref[2], 1, 0) + vec_ref[:, width : 2 * width])
    masks = head_masks(heads, width)

    def window(w):
        scores = dot(qkv_ref[1, w], spread(qkv_ref[0, w], masks), 1, 1) + bias_ref[...]
        top = jnp.max(scores, axis=0, keepdims=True)
        powers = jnp.exp(scores - top)
        probs = powers * (1.0 / jnp.sum(powers, axis=0, keepdims=True))
        p_ref[w] = probs
        att = fold(dot(probs.astype(bf16), qkv_ref[2, w], 0, 0), masks)
        att_ref[w] = att.astype(bf16)

    each_window(windows, window)


def attend(xn, w, vec, bias, heads, scale, windows, padded):
    width = w.shape[2]
    lanes = heads * padded
    return pl.pallas_call(
        functools.partial(attend_kernel, heads, scale),
        out_shape=(
            jax.ShapeDtypeStruct((3, windows, padded, width), bf16),
            jax.ShapeDtypeStruct((windows, padded, lanes), f32),
            jax.ShapeDtypeStruct((windows, padded, width), bf16),
        ),
        name="attend",
        cost_estimate=pl.CostEstimate(
            flops=2 * xn.size * 3 * width, bytes_accessed=4 * xn.size, transcendentals=0
        ),
    )(xn, w, vec, bias)


def attend_back_kernel(
    heads,
    scale,
    dmid_ref,
    xn_ref,
    wp_ref,
    qkv_ref,
    p_ref,
    att_ref,
    dqkv_ref,
    g_ref,
    ds_ref,
    gb_ref,
    datt_ref,
):
    _, windows, padded, width = qkv_ref.shape
    dmid = dmid_ref[...]
    datt_ref[...] = dot(dmid, wp_ref[...], 1, 1).astype(bf16).reshape(windows, padded, width)
    ds_ref[...] = jnp.zeros_like(ds_ref)
    gb_ref[...] = jnp.zeros_like(gb_ref)
    masks = head_masks(heads, width)

    def window(w):
        probs = p_ref[w]
        spread_d = spread(datt_ref[w], masks)
        dv = dot(probs.astype(bf16), spread_d, 1, 0)
        dprobs = dot(qkv_ref[2, w], spread_d, 1, 1)
        dscores = probs * (dprobs - jnp.sum(probs * dprobs, axis=0, keepdims=True))
        ds_ref[...] += dscores
        ds_b = dscores.astype(bf16)
        dk = dot(ds_b, spread(qkv_ref[0, w], masks), 1, 0)
        dq = fold(dot(ds_b, qkv_ref[1, w], 0, 0), masks) * scale
        dqkv_ref[w] = jnp.concatenate([dq, dk, dv], axis=1).astype(bf16)
        gb_ref[0:1, :] += jnp.sum(dq, axis=0, keepdims=True)
        gb_ref[1:2, :] += jnp.sum(dv, axis=0, keepdims=True)

    each_window(windows, window)
    dqkv = dqkv_ref[...].reshape(windows * padded, 3 * width)
    g_ref[:, : 3 * width] = dot(xn_ref[...], dqkv, 0, 0).astype(bf16)
    g_ref[:, 3 * width :] = dot(dmid, att_ref[...], 0, 0).astype(bf16)


def attend_back(dmid, xn, wp, qkv, probs, att, heads, scale):
    _, windows, padded, width = qkv.shape
    return pl.pallas_call(
        functools.partial(attend_back_kernel, heads, scale),
        out_shape=(
            jax.ShapeDtypeStruct((windows, padded, 3 * width), bf16),
            jax.ShapeDtypeStruct((dmid.shape[1], 4 * width), bf16),
            jax.ShapeDtypeStruct(probs.shape[1:], f32),
            jax.ShapeDtypeStruct((2, width), f32),
        ),
        scratch_shapes=[pltpu.VMEM((windows, padded, width), bf16)],
        name="attend_back",
        cost_estimate=pl.CostEstimate(
            flops=2 * dmid.size * 8 * width, bytes_accessed=4 * dmid.size, transcendentals=0
        ),
    )(dmid, xn, wp, qkv, probs, att)


def mlp_kernel(
    offset, xn_ref, gout_ref, w1_ref, vec_ref, w2_ref, hidden_ref, dpre_ref, gb_ref, g_ref, sum_ref
):
    ff = w1_ref.shape[1]

    @pl.when(pl.program_id(0) == 0)
    def _():
        gb_ref[...] = jnp.zeros_like(gb_ref)
        sum_ref[...] = jnp.zeros_like(sum_ref)

    xn = xn_ref[...]
    gout = gout_ref[...]
    pre = dot(xn, w1_ref[...], 1, 0) + vec_ref[:, offset:]
    act, slope = gelu_parts(pre)
    hidden = act.astype(bf16)
    hidden_ref[...] = hidden
    dpre = dot(gout, w2_ref[...], 1, 1) * slope
    gb_ref[...] += jnp.sum(dpre, axis=0, keepdims=True)
    dpre_b = dpre.astype(bf16)
    dpre_ref[...] = dpre_b
    sum_ref[:ff] += dot(dpre_b, xn, 0, 0)
    sum_ref[ff:] += dot(hidden, gout, 0, 0)

    @pl.when(pl.program_id(0) == pl.num_programs(0) - 1)
    def _():
        g_ref[...] = sum_ref[...].astype(bf16)


def split_kernel(parts, digit_ref, *refs):
    pieces = refs[parts:]
    rows = pieces[0].shape[0]
    for j, piece in enumerate(pieces):
        start = pl.multiple_of((digit_ref[0] ^ j) * rows, rows)
        total = refs[0][pl.ds(start, rows), :].astype(f32)
        for ref in refs[1:parts]:
            total = total + ref[pl.ds(start, rows), :].astype(f32)
        piece[...] = total.astype(bf16)


def split(values, digit, ways):
    rows, width = values[0].shape
    return pl.pallas_call(
        functools.partial(split_kernel, len(values)),
        in_specs=[pl.BlockSpec(memory_space=pltpu.SMEM)]
        + [pl.BlockSpec(memory_space=pltpu.VMEM)] * len(values),
        out_shape=[shape_of((rows // ways, width), bf16)] * ways,
        name="split",
    )(digit, *values)


def merge_kernel(ways, digit_ref, *refs):
    out_ref = refs[ways]
    rows = refs[0].shape[0]
    for j in range(ways):
        start = pl.multiple_of((digit_ref[0] ^ j) * rows, rows)
        out_ref[pl.ds(start, rows), :] = refs[j][...].astype(out_ref.dtype)


def merge(pieces, digit, dtype):
    ways = len(pieces)
    rows, width = pieces[0].shape
    return pl.pallas_call(
        functools.partial(merge_kernel, ways),
        in_specs=[pl.BlockSpec(memory_space=pltpu.SMEM)]
        + [pl.BlockSpec(memory_space=pltpu.VMEM)] * ways,
        out_shape=shape_of((rows * ways, width), dtype),
        name="merge",
    )(digit, *pieces)


def by_rows(kernel, rows, cut, whole, cut_outs, whole_outs, flops, scratch=()):
    chunk = CHUNK if rows % CHUNK == 0 else rows

    def cut_spec(value):
        return pl.BlockSpec((chunk,) + value.shape[1:], lambda i: (i,) + (0,) * (value.ndim - 1))

    def whole_spec(value):
        return pl.BlockSpec(value.shape, lambda i: (0,) * value.ndim)

    return pl.pallas_call(
        kernel,
        grid=(rows // chunk,),
        in_specs=[cut_spec(v) for v in cut] + [whole_spec(v) for v in whole],
        out_specs=[cut_spec(v) for v in cut_outs] + [whole_spec(v) for v in whole_outs],
        out_shape=list(cut_outs) + list(whole_outs),
        scratch_shapes=list(scratch),
        cost_estimate=pl.CostEstimate(
            flops=flops,
            bytes_accessed=sum(v.size * v.dtype.itemsize for v in cut),
            transcendentals=0,
        ),
    )(*cut, *whole)


def shape_of(shape, dtype=f32):
    return jax.ShapeDtypeStruct(shape, dtype)


def enter_kernel(count, *refs):
    x_ref, atts = refs[0], refs[1 : 1 + count]
    b_ref, gain_ref, shift_ref = refs[1 + count : 4 + count]
    weights = refs[4 + count : 4 + 2 * count]
    mid_ref, xn_ref = refs[4 + 2 * count :]
    total = dot(atts[0][...], weights[0][...], 1, 0)
    for att, weight in zip(atts[1:], weights[1:]):
        total = total + dot(att[...], weight[...], 1, 0)
    mid = x_ref[...].astype(f32) + (total + b_ref[...])
    mid_ref[...] = mid
    xn_ref[...] = norm_forward(mid, gain_ref[...], shift_ref[...])[0].astype(bf16)


def leave_kernel(count, *refs):
    mid_ref, hiddens = refs[0], refs[1 : 1 + count]
    b_ref, weights = refs[1 + count], refs[2 + count : 2 + 2 * count]
    out_ref = refs[2 + 2 * count]
    total = dot(hiddens[0][...], weights[0][...], 1, 0)
    for hidden, weight in zip(hiddens[1:], weights[1:]):
        total = total + dot(hidden[...], weight[...], 1, 0)
    out_ref[...] = (mid_ref[...] + total + b_ref[...]).astype(bf16)


def mid_back_kernel(count, *refs):
    mid_ref, gout_ref = refs[:2]
    dpres = refs[2 : 2 + count]
    gain_ref, shift_ref = refs[2 + count : 4 + count]
    weights = refs[4 + count : 4 + 2 * count]
    dmid_ref, dmid_b_ref, sums_ref = refs[4 + 2 * count :]

    @pl.when(pl.program_id(0) == 0)
    def _():
        sums_ref[...] = jnp.zeros_like(sums_ref)

    dxn = dot(dpres[0][...], weights[0][...], 1, 1)
    for dpre, weight in zip(dpres[1:], weights[1:]):
        dxn = dxn + dot(dpre[...], weight[...], 1, 1)
    gain = gain_ref[...]
    _, normed, scale_inv = norm_forward(mid_ref[...], gain, shift_ref[...])
    gout = gout_ref[...].astype(f32)
    dmid = gout + norm_backward(dxn, normed, scale_inv, gain)
    dmid_ref[...] = dmid
    dmid_b_ref[...] = dmid.astype(bf16)
    for at, value in enumerate((dxn * normed, dxn, dmid, gout)):
        sums_ref[at : at + 1, :] += jnp.sum(value, axis=0, keepdims=True)


def in_back_kernel(count, *refs):
    x_ref, dmid_ref = refs[:2]
    grads = refs[2 : 2 + count]
    gain_ref, shift_ref = refs[2 + count : 4 + count]
    weights = refs[4 + count : 4 + 2 * count]
    out_ref, sums_ref = refs[4 + 2 * count :]

    @pl.when(pl.program_id(0) == 0)
    def _():
        sums_ref[...] = jnp.zeros_like(sums_ref)

    dxn = jnp.zeros(dmid_ref.shape, f32)
    for at in range(count):
        for c in range(3):
            cols = weights[at].shape[2]
            dxn = dxn + dot(grads[at][:, c * cols : (c + 1) * cols], weights[at][c], 1, 1)
    gain = gain_ref[...]
    _, normed, scale_inv = norm_forward(x_ref[...].astype(f32), gain, shift_ref[...])
    out_ref[...] = (dmid_ref[...] + norm_backward(dxn, normed, scale_inv, gain)).astype(bf16)
    for at, value in enumerate((dxn * normed, dxn)):
        sums_ref[at : at + 1, :] += jnp.sum(value, axis=0, keepdims=True)


def local(
    inputs,
    image_count,
    rel_index,
    rel_table,
    norm1_gain,
    norm1_shift,
    w_qkv,
    bias_qv,
    w_proj,
    b_proj,
    norm2_gain,
    norm2_shift,
    w_fc1,
    b_fc1,
    w_fc2,
    b_fc2,
    out_grad,
):
    rows, width = inputs.shape
    window = rel_index.shape[0]
    offsets, heads = rel_table.shape
    shards = lax.axis_size("tensor")
    me = lax.axis_index("tensor")
    head_dim = w_qkv.shape[2] // heads
    scale = head_dim ** (-0.5)
    windows = rows // window
    padded = -(-window // ROW_TILE) * ROW_TILE
    n = windows * padded
    row = lambda value: value.reshape(1, -1)

    def swap(value, bit):
        return lax.ppermute(value, "tensor", [(i, i ^ bit) for i in range(shards)])

    def gather(value):
        got = [value]
        for m in range(1, shards):
            low = m & -m
            got.append(swap(got[m ^ low], low))
        return got

    def pad_rows(value):
        value = value.reshape(windows, window, -1)
        return jnp.pad(value, ((0, 0), (0, padded - window), (0, 0))).reshape(n, -1)

    def cut_rows(value):
        return value.reshape(windows, padded, -1)[:, :window].reshape(rows, -1)

    index = jnp.pad(
        rel_index, ((0, padded - window), (0, padded - window)), constant_values=-1
    )
    onehot = (index[:, :, None] == jnp.arange(offsets, dtype=jnp.int32)).astype(f32)
    bias = jnp.einsum("qkt,th->khq", onehot, rel_table, precision=lax.Precision.HIGHEST)
    keys = jnp.arange(padded, dtype=jnp.int32)[:, None, None]
    bias = jnp.where(keys < window, bias, FAR_BELOW).reshape(padded, heads * padded)

    biases = gather(bias)
    vectors = gather(row(jnp.concatenate([bias_qv.reshape(-1), b_fc1])))
    wqs = gather(w_qkv)
    wps = gather(w_proj)
    w1s = gather(w_fc1)
    w2s = gather(w_fc2)

    row_ids = me * rows + jnp.arange(rows, dtype=jnp.int32)
    live = (row_ids // IMG_TOKENS < image_count[0])[:, None]
    xn1 = norm_forward(inputs.astype(f32), norm1_gain, norm1_shift)[0].astype(bf16)
    xn1 = pad_rows(xn1)
    x_pad = pad_rows(inputs)
    gout = pad_rows(jnp.where(live, out_grad, jnp.zeros_like(out_grad)))

    order = range(shards)
    qkvs, probs, atts = [], [], []
    for m in order:
        qkv, p, att = attend(xn1, wqs[m], vectors[m], biases[m], heads, scale, windows, padded)
        qkvs.append(qkv)
        probs.append(p)
        atts.append(att.reshape(n, -1))

    mid, xn2 = by_rows(
        functools.partial(enter_kernel, shards),
        n,
        [x_pad] + atts,
        [row(b_proj), row(norm2_gain), row(norm2_shift)] + wps,
        [shape_of((n, width)), shape_of((n, width), bf16)],
        [],
        2 * n * width * width,
    )

    ff = w_fc1.shape[1]
    hiddens, dpres, g_b1s, g_fcs = {}, {}, {}, {}
    back_order = list(reversed(order))
    for m in back_order:
        hiddens[m], dpres[m], g_b1s[m], g_fcs[m] = by_rows(
            functools.partial(mlp_kernel, bias_qv.size),
            n,
            [xn2, gout],
            [w1s[m], vectors[m], w2s[m]],
            [shape_of((n, ff), bf16), shape_of((n, ff), bf16)],
            [shape_of((1, ff)), shape_of((2 * ff, width), bf16)],
            8 * n * width * ff,
            [pltpu.VMEM((2 * ff, width), f32)],
        )

    def scatter(parts):
        held = {m: [parts[m]] for m in parts}
        for m in range(shards - 1, 0, -1):
            low = m & -m
            total = held[m][0]
            for term in held[m][1:]:
                total = total + term
            held[m ^ low].append(swap(total, low))
        return held[0]

    groups = lax.axis_size("dp")
    group = lax.axis_index("dp")

    def swap_dp(value, bits):
        return lax.ppermute(value, "dp", [(i, i ^ bits) for i in range(groups)])

    def swap_all(pieces, stride):
        got = []
        for j, piece in enumerate(pieces):
            got.append(swap_dp(piece, j * stride) if j else piece)
        return got

    def sum_dp(terms, ways):
        stages = []
        stride = 1
        for way in ways:
            stages.append((stride, way, (group // stride % way).reshape(1)))
            stride *= way
        for stride, way, digit in stages:
            terms = swap_all(split(terms, digit, way), stride)
        total = terms[0].astype(f32)
        for term in terms[1:]:
            total = total + term.astype(f32)
        total = total.astype(bf16)
        for at, (stride, way, digit) in reversed(list(enumerate(stages))):
            pieces = swap_all([total] * way, stride)
            total = merge(pieces, digit, f32 if at == 0 else bf16)
        return total

    def ways_of(most):
        left = groups
        ways = []
        while left > 1:
            ways.append(min(most[min(len(ways), len(most) - 1)], left))
            left //= ways[-1]
        return ways

    g_fc = sum_dp(scatter(g_fcs), ways_of((2, 4)))
    g_fc1, g_fc2 = g_fc[:ff].T, g_fc[ff:]

    listed = lambda parts: [parts[m] for m in order]
    dmid, dmid_b, sums2 = by_rows(
        functools.partial(mid_back_kernel, shards),
        n,
        [mid, gout] + listed(dpres),
        [row(norm2_gain), row(norm2_shift)] + w1s,
        [shape_of((n, width)), shape_of((n, width), bf16)],
        [shape_of((8, width))],
        2 * n * width * ff * shards,
    )

    dqkvs, dss, g_bqvs, g_atts = {}, {}, {}, {}
    for m in back_order:
        dqkv, g_atts[m], dss[m], g_bqvs[m] = attend_back(
            dmid_b, xn1, wps[m], qkvs[m], probs[m], atts[m], heads, scale
        )
        dqkvs[m] = dqkv.reshape(n, -1)
    g_att = sum_dp(scatter(g_atts), ways_of((8,)))
    cols = w_qkv.shape[2]
    g_qkv = jnp.stack([g_att[:, c * cols : (c + 1) * cols] for c in range(3)])
    g_proj = g_att[:, 3 * cols :].T

    in_grad, sums1 = by_rows(
        functools.partial(in_back_kernel, shards),
        n,
        [x_pad, dmid] + listed(dqkvs),
        [row(norm1_gain), row(norm1_shift)] + wqs,
        [shape_of((n, width), bf16)],
        [shape_of((8, width))],
        6 * n * width * width,
    )
    (outputs,) = by_rows(
        functools.partial(leave_kernel, shards),
        n,
        [mid] + listed(hiddens),
        [row(b_fc2)] + w2s,
        [shape_of((n, width), bf16)],
        [],
        2 * n * width * ff * shards,
    )
    outputs = cut_rows(outputs)
    outputs = jnp.where(live, outputs, jnp.zeros_like(outputs))
    in_grad = cut_rows(in_grad)

    ds_all = jnp.stack(listed(dss)).reshape(shards, padded, heads, padded)
    g_tabs = jnp.einsum(
        "qkt,mkhq->mth", onehot, ds_all, precision=lax.Precision.HIGHEST
    )
    per_shard = jnp.concatenate(
        [
            g_tabs.reshape(shards, -1),
            jnp.stack(listed(g_bqvs)).reshape(shards, -1),
            jnp.stack(listed(g_b1s)).reshape(shards, -1),
        ],
        axis=1,
    )
    shared = jnp.concatenate([sums2[:4].reshape(-1), sums1[:2].reshape(-1)])
    per_shard = jnp.concatenate(
        [per_shard, jnp.broadcast_to(shared, (shards, shared.size))], axis=1
    )
    small = sum(scatter({m: per_shard[m] for m in order}))
    bit = 1
    while bit < groups:
        small = small + swap_dp(small, bit)
        bit *= 2
    pieces = []
    at = 0
    for shape in (rel_table.shape, bias_qv.shape, b_fc1.shape) + ((width,),) * 6:
        size = 1
        for extent in shape:
            size *= extent
        pieces.append(small[at : at + size].reshape(shape))
        at += size
    g_tab, g_bqv, g_b_fc1, g_n2g, g_n2s, g_bp, g_b_fc2, g_n1g, g_n1s = pieces
    return (
        outputs,
        in_grad,
        g_tab,
        g_n1g,
        g_n1s,
        g_qkv,
        g_bqv,
        g_proj,
        g_bp,
        g_n2g,
        g_n2s,
        g_fc1,
        g_b_fc1,
        g_fc2,
        g_b_fc2,
    )


def solution(mesh):
    placed = (
        P(("dp", "tensor"), None),
        P("dp"),
        P(),
        P(None, "tensor"),
        P(),
        P(),
        P(None, None, "tensor"),
        P(None, "tensor"),
        P("tensor", None),
        P(),
        P(),
        P(),
        P(None, "tensor"),
        P("tensor"),
        P("tensor", None),
        P(),
        P(("dp", "tensor"), None),
    )
    return jax.shard_map(
        local,
        mesh=mesh,
        in_specs=placed,
        out_specs=(
            P(("dp", "tensor"), None),
            P(("dp", "tensor"), None),
            P(None, "tensor"),
            P(),
            P(),
            P(None, None, "tensor"),
            P(None, "tensor"),
            P("tensor", None),
            P(),
            P(),
            P(),
            P(None, "tensor"),
            P("tensor"),
            P("tensor", None),
            P(),
        ),
        check_vma=False,
    )
```

time: 644 us -> 293 us (0.45)
  waiting for transfers between devices: 339 us -> 71 us
  Pallas kernels: 0 us -> 130 us
  matrix products: 87.7 us -> 4.52 us
  local copies, waits for them, and re-layouts: 90.1 us -> 22.9 us
  blocking collectives: 61.6 us -> 0 us
  starting transfers between devices: 0.37 us -> 53.2 us
  other arithmetic: 44.5 us -> 7.63 us
  between operations: 15.3 us -> 2.16 us
    reduce_scatter x4 -> x0, waiting for transfers between devices: 184 us -> none  [the longest x1 59.8 us: local(): lax.psum_scatter(jnp.dot(rows, w_proj, preferred_element_type=jnp.float32...]
    pallas_call x0 -> x22, Pallas kernels: none -> 130 us  [the longest x8 55.8 us: by_rows(): pl.pallas_call(kernel, grid=(rows // chunk,), in_specs=[cut_spec(v) for v...]
    all_gather x4 -> x0, waiting for transfers between devices: 100 us -> none  [the longest x1 29.6 us: local(): xn1 = lax.all_gather(xn1_local, 'tensor', axis=0, tiled=True)]
    dot_general x22 -> x2, matrix products: 87.7 us -> 4.52 us  [the longest x1 2.82 us: local(): jnp.einsum('qkt,th->khq', onehot, rel_table, precision=lax.Precision.HIGH...]
    ppermute x0 -> x52, waiting for transfers between devices: none -> 71 us  [the longest x27 46.7 us: swap(): return lax.ppermute(value, 'tensor', [(i, i ^ bit) for i in range(shards)])]
    psum x2 -> x0, blocking collectives: 61.6 us -> none  [the longest x1 39.5 us: local(): lax.psum((g_n1g, g_n1s, g_bp, g_n2g, g_n2s, g_b_fc2), ('dp', 'tensor'))]
    psum x1 -> x0, waiting for transfers between devices: 54.7 us -> none  [local(): lax.psum(g_qkv.astype(jnp.bfloat16), 'dp').astype(jnp.float32)]
    ppermute x0 -> x52, starting transfers between devices: none -> 53.2 us  [the longest x25 39.2 us: swap_dp(): return lax.ppermute(value, 'dp', [(i, i ^ bits) for i in range(groups)])]
  transfers between devices with their start and end apart: 9 -> 52, of which waited for: 9 -> 16; matrix products, arithmetic and copies ran while one was open for 8% -> 9% of each run, Pallas kernels for 0% -> 44%
where the time goes in v1:
time: 293 us; the launch traced here: 291 us
  Pallas kernels  130 us (44%)
  waiting for transfers between devices  71 us (24%)
  starting transfers between devices  53.2 us (18%)
  local copies, waits for them, and re-layouts  22.9 us (8%)
  other arithmetic  7.63 us (3%)
  matrix products  4.52 us (2%)
    pallas_call x8, Pallas kernels, by_rows(): pl.pallas_call(kernel, grid=(rows // chunk,), in_specs=[cut_spec(v) for v...  55.8 us
    ppermute x27, waiting for transfers between devices, swap(): return lax.ppermute(value, 'tensor', [(i, i ^ bit) for i in range(shards)])  46.7 us
    ppermute x25, starting transfers between devices, swap_dp(): return lax.ppermute(value, 'dp', [(i, i ^ bits) for i in range(groups)])  39.2 us
    pallas_call x4, Pallas kernels, attend_back(): pl.pallas_call(functools.partial(attend_back_kernel, heads, scale), out_s...  35.4 us
    pallas_call x4, Pallas kernels, attend(): pl.pallas_call(functools.partial(attend_kernel, heads, scale), out_shape=...  24.5 us
    ppermute x25, waiting for transfers between devices, swap_dp(): return lax.ppermute(value, 'dp', [(i, i ^ bits) for i in range(groups)])  24.3 us
    ppermute x27, starting transfers between devices, swap(): return lax.ppermute(value, 'tensor', [(i, i ^ bit) for i in range(shards)])  13.9 us
    unnamed x117, local copies, waits for them, and re-layouts  9.26 us
  transfers between devices with their start and end apart: 52, of which 16 were waited for; matrix products, arithmetic and copies ran while one was open for 9% of the time, Pallas kernels for 44%

profile of v1, /device:TPU:0, one launch (start us, length us, event | category | flops | bytes accessed | tf_op | source)
XLA Modules:
  0.0 291.3 jit_solution(4435003043763693525)
XLA Ops:
  1.5 3.0 %collective-permute-start.4 = (f32[1,768]{1,0:T(1,128)S(1)}, f32[1,768]{1,0:T(1,128)S(1)}, u32[]{:S(2)}, u32[]{:S(2)}) collective-permute-start(f32[1,768]{1,0:T(1,128)S(1)} %reshape.198.vec_ref), channel_id=1, source_target_pairs={{0,2},{1,3},{2,0},{3,1},{4,6},{5,7},{6,4},{7,5},{8,10},{9,11},{10,... | collective-permute-start | bytes 9224 | tf_op jit(solution)/shard_map/ppermute | solution.py:380
  5.4 2.8 fusion.1
  9.3 1.7 collective-permute-start.3
  12.5 1.0 collective-permute-start.15
  15.8 31.3 %collective-permute-done.10.refs_10_.wp_ref = bf16[128,512]{1,0:T(8,128)(2,1)} collective-permute-done((bf16[128,512]{1,0:T(8,128)(2,1)S(1)}, bf16[128,512]{1,0:T(8,128)(2,1)}, u32[]{:S(2)}, u32[]{:S(2)}) %collective-permute-start.10) | collective-permute-done | bytes 131104 | tf_op jit(solution)/shard_map/ppermute | solution.py:380
  50.7 1.3 broadcast_select_fusion.1
  52.3 1.1 pad.15
  53.5 6.1 %attend.4 = (bf16[3,16,64,128]{3,2,1,0:T(8,128)(2,1)}, f32[16,64,256]{2,1,0:T(8,128)}, bf16[16,64,128]{2,1,0:T(8,128)(2,1)}) custom-call(bf16[1024,512]{1,0:T(8,128)(2,1)} %bitcast.69, bf16[3,512,128]{2,1,0:T(8,128)(2,1)} %refs_8_.5, f32[1,768]{1,0:T(1,128)} %copy-done.34, f32[64,256]{1,0:T(8,128)} %copy-done.14), custom_call_target="tpu_custom_call" | custom-call | flops 402653184 | bytes 2097152 | tf_op jit(solution)/shard_map/attend/pallas_call | solution.py:106
  60.1 1.1 pad.17
  61.2 1.1 pad.14
  62.3 6.1 %attend.6 = (bf16[3,16,64,128]{3,2,1,0:T(8,128)(2,1)}, f32[16,64,256]{2,1,0:T(8,128)}, bf16[16,64,128]{2,1,0:T(8,128)(2,1)}) custom-call(bf16[1024,512]{1,0:T(8,128)(2,1)} %bitcast.70, bf16[3,512,128]{2,1,0:T(8,128)(2,1)} %collective-permute-done.3.w_ref.refs_10_, f32[1,768]{1,0:T(1,128)} %copy-done.38, f32[64,256]{1,0:T(8,128)} %copy-done.20), custom_call_target="tpu_custom_call" | custom-call | flops 402653184 | bytes 2097152 | tf_op jit(solution)/shard_map/attend/pallas_call | solution.py:106
  68.3 6.1 %attend.5 = (bf16[3,16,64,128]{3,2,1,0:T(8,128)(2,1)}, f32[16,64,256]{2,1,0:T(8,128)}, bf16[16,64,128]{2,1,0:T(8,128)(2,1)}) custom-call(bf16[1024,512]{1,0:T(8,128)(2,1)} %bitcast.71, bf16[3,512,128]{2,1,0:T(8,128)(2,1)} %copy-done.4, f32[1,768]{1,0:T(1,128)} %copy-done.39, f32[64,256]{1,0:T(8,128)} %collective-permute-done.2.bias_ref), custom_call_target="tpu_custom_call" | custom-call | flops 402653184 | bytes 2097152 | tf_op jit(solution)/shard_map/attend/pallas_call | solution.py:106
  74.5 6.2 %attend.7 = (bf16[3,16,64,128]{3,2,1,0:T(8,128)(2,1)}, f32[16,64,256]{2,1,0:T(8,128)}, bf16[16,64,128]{2,1,0:T(8,128)(2,1)}) custom-call(bf16[1024,512]{1,0:T(8,128)(2,1)} %bitcast.72, bf16[3,512,128]{2,1,0:T(8,128)(2,1)} %collective-permute-done.6.w_ref.refs_11_, f32[1,768]{1,0:T(1,128)} %copy-done.40, f32[64,256]{1,0:T(8,128)} %copy-done.21), custom_call_target="tpu_custom_call" | custom-call | flops 402653184 | bytes 2097152 | tf_op jit(solution)/shard_map/attend/pallas_call | solution.py:106
  80.6 5.1 %shard_map.280 = (f32[1024,512]{1,0:T(8,128)}, bf16[1024,512]{1,0:T(8,128)(2,1)}) custom-call(bf16[1024,512]{1,0:T(8,128)(2,1)} %bitcast.77, bf16[1024,128]{1,0:T(8,128)(2,1)} %bitcast.85, bf16[1024,128]{1,0:T(8,128)(2,1)} %bitcast.87, bf16[1024,128]{1,0:T(8,128)(2,1)} %bitcast.89, bf16[1024,128]{1,0:T(8,128)(2,1)} %bitcast.91, f32[1,512]{1,0:T(1,128)} %bitcast.112, ...), custom_call_target="tpu_custom_call" | custom-call | flops 536870912 | bytes 2097152 | tf_op jit(solution)/shard_map/pallas_call | solution.py:259
  85.7 7.0 %shard_map.284 = (bf16[1024,512]{1,0:T(8,128)(2,1)}, bf16[1024,512]{1,0:T(8,128)(2,1)}, f32[1,512]{1,0:T(1,128)}, bf16[1024,512]{1,0:T(8,128)(2,1)}) custom-call(bf16[1024,512]{1,0:T(8,128)(2,1)} %get-tuple-element.85.xn_ref, bf16[1024,512]{1,0:T(8,128)(2,1)} %bitcast.79, bf16[512,512]{1,0:T(8,128)(2,1)} %collective-permute-done.16.w1_ref.refs_11_, ...), custom_call_target="tpu_custom_call" | custom-call | flops 2147483648 | bytes 2097152 | tf_op jit(solution)/shard_map/pallas_call | solution.py:259
  93.2 7.0 %shard_map.282 = (bf16[1024,512]{1,0:T(8,128)(2,1)}, bf16[1024,512]{1,0:T(8,128)(2,1)}, f32[1,512]{1,0:T(1,128)}, bf16[1024,512]{1,0:T(8,128)(2,1)}) custom-call(bf16[1024,512]{1,0:T(8,128)(2,1)} %get-tuple-element.85.xn_ref, bf16[1024,512]{1,0:T(8,128)(2,1)} %bitcast.80, bf16[512,512]{1,0:T(8,128)(2,1)} %collective-permute-done.12.w1_ref.refs_9_, ...), custom_call_target="tpu_custom_call" | custom-call | flops 2147483648 | bytes 2097152 | tf_op jit(solution)/shard_map/pallas_call | solution.py:259
  100.4 7.2 %shard_map.281 = (bf16[1024,512]{1,0:T(8,128)(2,1)}, bf16[1024,512]{1,0:T(8,128)(2,1)}, f32[1,512]{1,0:T(1,128)}, bf16[1024,512]{1,0:T(8,128)(2,1)}) custom-call(bf16[1024,512]{1,0:T(8,128)(2,1)} %get-tuple-element.85.xn_ref, bf16[1024,512]{1,0:T(8,128)(2,1)} %bitcast.81, bf16[512,512]{1,0:T(8,128)(2,1)} %refs_8_.4, f32[1,768]{1,0:T(1,128)} %copy-done.34, ...), custom_call_target="tpu_custom_call" | custom-call | flops 2147483648 | bytes 2097152 | tf_op jit(solution)/shard_map/pallas_call | solution.py:259
  107.6 7.0 %shard_map.283 = (bf16[1024,512]{1,0:T(8,128)(2,1)}, bf16[1024,512]{1,0:T(8,128)(2,1)}, f32[1,512]{1,0:T(1,128)}, bf16[1024,512]{1,0:T(8,128)(2,1)}) custom-call(bf16[1024,512]{1,0:T(8,128)(2,1)} %get-tuple-element.85.xn_ref, bf16[1024,512]{1,0:T(8,128)(2,1)} %bitcast.82, bf16[512,512]{1,0:T(8,128)(2,1)} %collective-permute-done.14.w1_ref.refs_10_, ...), custom_call_target="tpu_custom_call" | custom-call | flops 2147483648 | bytes 2097152 | tf_op jit(solution)/shard_map/pallas_call | solution.py:259
  114.6 8.0 %shard_map.286 = (f32[1024,512]{1,0:T(8,128)}, bf16[1024,512]{1,0:T(8,128)(2,1)}, f32[8,512]{1,0:T(8,128)}) custom-call(f32[1024,512]{1,0:T(8,128)} %get-tuple-element.84.refs_0_, bf16[1024,512]{1,0:T(8,128)(2,1)} %bitcast.83, bf16[1024,512]{1,0:T(8,128)(2,1)} %get-tuple-element.90.refs_2_, bf16[1024,512]{1,0:T(8,128)(2,1)} %get-tuple-element.91.refs_3_, ...), custom_call_target="tpu_custom_call" | custom-call | flops 2147483648 | bytes 7340032 | tf_op jit(solution)/shard_map/pallas_call | solution.py:259
  122.7 8.9 %attend_back.7 = (bf16[16,64,384]{2,1,0:T(8,128)(2,1)}, bf16[512,512]{1,0:T(8,128)(2,1)}, f32[64,256]{1,0:T(8,128)}, f32[2,128]{1,0:T(2,128)}) custom-call(bf16[1024,512]{1,0:T(8,128)(2,1)} %get-tuple-element.95.dmid_ref, bf16[1024,512]{1,0:T(8,128)(2,1)} %bitcast.73, bf16[128,512]{1,0:T(8,128)(2,1)} %collective-permute-done.11.refs_11_.wp_ref, ...), custom_call_target="tpu_custom_call" | custom-call | flops 1073741824 | bytes 2097152 | tf_op jit(solution)/shard_map/attend_back/pallas_call | solution.py:164
  131.8 8.8 %attend_back.4 = (bf16[16,64,384]{2,1,0:T(8,128)(2,1)}, bf16[512,512]{1,0:T(8,128)(2,1)}, f32[64,256]{1,0:T(8,128)}, f32[2,128]{1,0:T(2,128)}) custom-call(bf16[1024,512]{1,0:T(8,128)(2,1)} %get-tuple-element.95.dmid_ref, bf16[1024,512]{1,0:T(8,128)(2,1)} %bitcast.74, bf16[128,512]{1,0:T(8,128)(2,1)} %wp_ref.1, ...), custom_call_target="tpu_custom_call" | custom-call | flops 1073741824 | bytes 2097152 | tf_op jit(solution)/shard_map/attend_back/pallas_call | solution.py:164
  140.6 8.8 %attend_back.6 = (bf16[16,64,384]{2,1,0:T(8,128)(2,1)}, bf16[512,512]{1,0:T(8,128)(2,1)}, f32[64,256]{1,0:T(8,128)}, f32[2,128]{1,0:T(2,128)}) custom-call(bf16[1024,512]{1,0:T(8,128)(2,1)} %get-tuple-element.95.dmid_ref, bf16[1024,512]{1,0:T(8,128)(2,1)} %bitcast.75, bf16[128,512]{1,0:T(8,128)(2,1)} %collective-permute-done.10.refs_10_.wp_ref, ...), custom_call_target="tpu_custom_call" | custom-call | flops 1073741824 | bytes 2097152 | tf_op jit(solution)/shard_map/attend_back/pallas_call | solution.py:164
  149.5 8.9 %attend_back.5 = (bf16[16,64,384]{2,1,0:T(8,128)(2,1)}, bf16[512,512]{1,0:T(8,128)(2,1)}, f32[64,256]{1,0:T(8,128)}, f32[2,128]{1,0:T(2,128)}) custom-call(bf16[1024,512]{1,0:T(8,128)(2,1)} %get-tuple-element.95.dmid_ref, bf16[1024,512]{1,0:T(8,128)(2,1)} %bitcast.76, bf16[128,512]{1,0:T(8,128)(2,1)} %copy-done.10, ...), custom_call_target="tpu_custom_call" | custom-call | flops 1073741824 | bytes 2097152 | tf_op jit(solution)/shard_map/attend_back/pallas_call | solution.py:164
  159.5 7.9 %shard_map.287 = (bf16[1024,512]{1,0:T(8,128)(2,1)}, f32[8,512]{1,0:T(8,128)}) custom-call(bf16[1024,512]{1,0:T(8,128)(2,1)} %bitcast.78, f32[1024,512]{1,0:T(8,128)} %get-tuple-element.94.refs_1_, bf16[1024,384]{1,0:T(8,128)(2,1)} %bitcast.95, bf16[1024,384]{1,0:T(8,128)(2,1)} %bitcast.97, bf16[1024,384]{1,0:T(8,128)(2,1)} %bitcast.96, ...), custom_call_target="tpu_custom_call" | custom-call | flops 1610612736 | bytes 6291456 | tf_op jit(solution)/shard_map/pallas_call | solution.py:259
  168.7 1.7 fusion.12
  171.1 2.0 add.121
  173.1 1.4 collective-permute-start.25
  174.5 10.3 %collective-permute-done.42.refs_1_ = bf16[1024,512]{1,0:T(8,128)(2,1)S(1)} collective-permute-done((bf16[1024,512]{1,0:T(8,128)(2,1)S(1)}, bf16[1024,512]{1,0:T(8,128)(2,1)S(1)}, u32[]{:S(2)}, u32[]{:S(2)}) %collective-permute-start.42) | collective-permute-done | bytes 1048608 | tf_op jit(solution)/shard_map/ppermute | solution.py:380
  185.8 3.1 %split.4 = (bf16[512,512]{1,0:T(8,128)(2,1)}, bf16[512,512]{1,0:T(8,128)(2,1)}) custom-call(s32[1]{0:T(128)} %bitcast.41.digit_ref, bf16[1024,512]{1,0:T(8,128)(2,1)} %get-tuple-element.135.refs_0_, bf16[1024,512]{1,0:T(8,128)(2,1)} %copy-done.6, bf16[1024,512]{1,0:T(8,128)(2,1)} %collective-permute-done.43.refs_2_), custom_call_target="tpu_custom_call" | custom-call | tf_op jit(solution)/shard_map/split/pallas_call | solution.py:221
  188.9 1.5 collective-permute-start.44
  192.5 3.2 %collective-permute-done.19 = f32[4516]{0:T(1024)S(1)} collective-permute-done((f32[4516]{0:T(1024)S(1)}, f32[4516]{0:T(1024)S(1)}, u32[]{:S(2)}, u32[]{:S(2)}) %collective-permute-start.19) | collective-permute-done | bytes 18096 | tf_op jit(solution)/shard_map/ppermute | solution.py:380
  195.8 1.5 collective-permute-start.21
  197.3 4.8 %collective-permute-done.21 = f32[4516]{0:T(1024)S(1)} collective-permute-done((f32[4516]{0:T(1024)S(1)}, f32[4516]{0:T(1024)S(1)}, u32[]{:S(2)}, u32[]{:S(2)}) %collective-permute-start.21) | collective-permute-done | bytes 18096 | tf_op jit(solution)/shard_map/ppermute | solution.py:465
  202.0 1.6 collective-permute-start.22
  203.6 2.2 collective-permute-done.22
  205.8 2.6 collective-permute-start.23
  208.4 6.6 %shard_map.285 = bf16[1024,512]{1,0:T(8,128)(2,1)} custom-call(f32[1024,512]{1,0:T(8,128)} %get-tuple-element.84.refs_0_, bf16[1024,512]{1,0:T(8,128)(2,1)} %get-tuple-element.86.refs_1_, bf16[1024,512]{1,0:T(8,128)(2,1)} %get-tuple-element.87.refs_2_, bf16[1024,512]{1,0:T(8,128)(2,1)} %get-tuple-element.88.refs_3_, ...), custom_call_target="tpu_custom_call" | custom-call | flops 2147483648 | bytes 6291456 | tf_op jit(solution)/shard_map/pallas_call | solution.py:259
  215.0 1.2 slice.103
  216.5 2.3 split.3
  218.8 1.6 collective-permute-start.27
  220.4 1.5 collective-permute-start.28
  222.8 2.0 split.5
  225.6 3.6 %collective-permute-start.47 = (bf16[128,512]{1,0:T(8,128)(2,1)}, bf16[128,512]{1,0:T(8,128)(2,1)S(1)}, u32[]{:S(2)}, u32[]{:S(2)}) collective-permute-start(bf16[128,512]{1,0:T(8,128)(2,1)} %get-tuple-element.144), channel_id=1, source_target_pairs={{0,24},{4,28},{8,16},{12,20},{16,8},{20,12},{24,0},{28,4},{1,25},{... | collective-permute-start | bytes 393224 | tf_op jit(solution)/shard_map/ppermute | solution.py:465
  229.2 1.1 broadcast_select_fusion
  230.4 1.1 reshape.217
  232.4 2.6 collective-permute-start.31
  235.0 6.2 %collective-permute-done.46 = bf16[128,512]{1,0:T(8,128)(2,1)S(1)} collective-permute-done((bf16[128,512]{1,0:T(8,128)(2,1)}, bf16[128,512]{1,0:T(8,128)(2,1)S(1)}, u32[]{:S(2)}, u32[]{:S(2)}) %collective-permute-start.46) | collective-permute-done | bytes 131104 | tf_op jit(solution)/shard_map/ppermute | solution.py:465
  241.2 1.4 collective-permute-start.32
  242.6 2.4 collective-permute-start.33
  245.4 2.7 collective-permute-done.31
  248.1 2.1 collective-permute-done.33
  250.3 2.5 collective-permute-start.40
  252.8 1.7 collective-permute-start.39
  254.5 4.6 %collective-permute-start.38 = (bf16[64,512]{1,0:T(8,128)(2,1)S(1)}, bf16[64,512]{1,0:T(8,128)(2,1)S(1)}, u32[]{:S(2)}, u32[]{:S(2)}) collective-permute-start(bf16[64,512]{1,0:T(8,128)(2,1)S(1)} %add_convert_fusion.1.refs_0_), channel_id=1, source_target_pairs={{0,20},{4,16},{8,28},{12,24},{16,4},{20,0},{24,12},{28,8},{1,21},{... | collective-permute-start | bytes 196616 | tf_op jit(solution)/shard_map/ppermute | solution.py:465
  259.5 2.9 %collective-permute-start.48 = (bf16[128,512]{1,0:T(8,128)(2,1)S(1)}, bf16[128,512]{1,0:T(8,128)(2,1)S(1)}, u32[]{:S(2)}, u32[]{:S(2)}) collective-permute-start(bf16[128,512]{1,0:T(8,128)(2,1)S(1)} %add_convert_fusion.refs_0_), channel_id=1, source_target_pairs={{0,8},{4,12},{8,0},{12,4},{16,24},{20,28},{24,16},{28,20},{1,9},{5... | collective-permute-start | bytes 393224 | tf_op jit(solution)/shard_map/ppermute | solution.py:465
  263.1 5.3 %collective-permute-done.49.refs_2_ = bf16[128,512]{1,0:T(8,128)(2,1)S(1)} collective-permute-done((bf16[128,512]{1,0:T(8,128)(2,1)S(1)}, bf16[128,512]{1,0:T(8,128)(2,1)S(1)}, u32[]{:S(2)}, u32[]{:S(2)}) %collective-permute-start.49) | collective-permute-done | bytes 131104 | tf_op jit(solution)/shard_map/ppermute | solution.py:465
  268.4 2.8 collective-permute-start.36
  271.2 1.9 merge.4.refs_0_
  274.4 1.1 collective-permute-start.51
  278.7 2.1 merge.3
  280.8 1.3 slice_bitcast_fusion.1
  284.6 2.7 merge.5
  287.3 2.7 fusion.26
  290.0 1.3 copy.43
  (235 shorter events, 28.5 us)
Async XLA Ops:
  1.5 12.7 %copy-start.34 = (f32[1,768]{1,0:T(1,128)}, f32[1,768]{1,0:T(1,128)S(1)}, u32[]{:S(2)}) copy-start(f32[1,768]{1,0:T(1,128)S(1)} %reshape.198.vec_ref) | copy-start | bytes 9220
  1.5 9.7 %collective-permute-start.4 = (f32[1,768]{1,0:T(1,128)S(1)}, f32[1,768]{1,0:T(1,128)S(1)}, u32[]{:S(2)}, u32[]{:S(2)}) collective-permute-start(f32[1,768]{1,0:T(1,128)S(1)} %reshape.198.vec_ref), channel_id=1, source_target_pairs={{0,2},{1,3},{2,0},{3,1},{4,6},{5,7},{6,4},{7,5},{8,10},{9,11},{10,... | collective-permute-start | bytes 9224 | tf_op jit(solution)/shard_map/ppermute | solution.py:380
  4.5 6.8 %collective-permute-start.1 = (f32[1,768]{1,0:T(1,128)S(1)}, f32[1,768]{1,0:T(1,128)S(1)}, u32[]{:S(2)}, u32[]{:S(2)}) collective-permute-start(f32[1,768]{1,0:T(1,128)S(1)} %reshape.198.vec_ref), channel_id=1, source_target_pairs={{0,1},{1,0},{2,3},{3,2},{4,5},{5,4},{6,7},{7,6},{8,9},{9,8},{10,11... | collective-permute-start | bytes 9224 | tf_op jit(solution)/shard_map/ppermute | solution.py:380
  5.4 42.3 %copy-start.35 = (f32[512]{0:T(512)S(1)}, f32[512]{0:T(512)}, u32[]{:S(2)}) copy-start(f32[512]{0:T(512)} %param.22) | copy-start | bytes 6148
  5.4 42.2 %copy-start.36 = (f32[512]{0:T(512)S(1)}, f32[512]{0:T(512)}, u32[]{:S(2)}) copy-start(f32[512]{0:T(512)} %param.21) | copy-start | bytes 6148
  8.7 39.3 %copy-start.14 = (f32[64,256]{1,0:T(8,128)}, f32[64,256]{1,0:T(8,128)S(1)}, u32[]{:S(2)}) copy-start(f32[64,256]{1,0:T(8,128)S(1)} %reshape.199.bias_ref) | copy-start | bytes 196612
  8.7 5.0 %collective-permute-start.5 = (f32[64,256]{1,0:T(8,128)S(1)}, f32[64,256]{1,0:T(8,128)S(1)}, u32[]{:S(2)}, u32[]{:S(2)}) collective-permute-start(f32[64,256]{1,0:T(8,128)S(1)} %reshape.199.bias_ref), channel_id=1, source_target_pairs={{0,2},{1,3},{2,0},{3,1},{4,6},{5,7},{6,4},{7,5},{8,10},{9,11},{10,... | collective-permute-start | bytes 196616 | tf_op jit(solution)/shard_map/ppermute | solution.py:380
  8.9 5.3 %collective-permute-start.2 = (f32[64,256]{1,0:T(8,128)S(1)}, f32[64,256]{1,0:T(8,128)}, u32[]{:S(2)}, u32[]{:S(2)}) collective-permute-start(f32[64,256]{1,0:T(8,128)S(1)} %reshape.199.bias_ref), channel_id=1, source_target_pairs={{0,1},{1,0},{2,3},{3,2},{4,5},{5,4},{6,7},{7,6},{8,9},{9,8},{10,11... | collective-permute-start | bytes 196616 | tf_op jit(solution)/shard_map/ppermute | solution.py:380
  9.3 37.7 %collective-permute-start.3 = (bf16[3,512,128]{2,1,0:T(8,128)(2,1)S(1)}, bf16[3,512,128]{2,1,0:T(8,128)(2,1)}, u32[]{:S(2)}, u32[]{:S(2)}) collective-permute-start(bf16[3,512,128]{2,1,0:T(8,128)(2,1)S(1)} %copy-done.3), channel_id=1, source_target_pairs={{0,2},{1,3},{2,0},{3,1},{4,6},{5,7},{6,4},{7,5},{8,10},{9,11},{10,... | collective-permute-start | bytes 1179656 | tf_op jit(solution)/shard_map/ppermute | solution.py:380
  11.2 1.2 collective-permute-start.7
  11.4 37.3 %collective-permute-start.14 = (bf16[512,512]{1,0:T(8,128)(2,1)}, bf16[512,512]{1,0:T(8,128)(2,1)}, u32[]{:S(2)}, u32[]{:S(2)}) collective-permute-start(bf16[512,512]{1,0:T(8,128)(2,1)} %refs_8_.4), channel_id=1, source_target_pairs={{0,2},{1,3},{2,0},{3,1},{4,6},{5,7},{6,4},{7,5},{8,10},{9,11},{10,... | collective-permute-start | bytes 1572872 | tf_op jit(solution)/shard_map/ppermute | solution.py:380
  12.5 36.3 %collective-permute-start.15 = (bf16[512,512]{1,0:T(8,128)(2,1)}, bf16[512,512]{1,0:T(8,128)(2,1)}, u32[]{:S(2)}, u32[]{:S(2)}) collective-permute-start(bf16[512,512]{1,0:T(8,128)(2,1)} %refs_6_.1), channel_id=1, source_target_pairs={{0,2},{1,3},{2,0},{3,1},{4,6},{5,7},{6,4},{7,5},{8,10},{9,11},{10,... | collective-permute-start | bytes 1572872 | tf_op jit(solution)/shard_map/ppermute | solution.py:380
  13.7 33.4 %copy-start.20 = (f32[64,256]{1,0:T(8,128)}, f32[64,256]{1,0:T(8,128)S(1)}, u32[]{:S(2)}) copy-start(f32[64,256]{1,0:T(8,128)S(1)} %collective-permute-done.5.bias_ref) | copy-start | bytes 196612
  13.7 1.3 collective-permute-start.8
  14.2 35.3 %collective-permute-start = (bf16[3,512,128]{2,1,0:T(8,128)(2,1)S(1)}, bf16[3,512,128]{2,1,0:T(8,128)(2,1)S(1)}, u32[]{:S(2)}, u32[]{:S(2)}) collective-permute-start(bf16[3,512,128]{2,1,0:T(8,128)(2,1)S(1)} %copy-done.3), channel_id=1, source_target_pairs={{0,1},{1,0},{2,3},{3,2},{4,5},{5,4},{6,7},{7,6},{8,9},{9,8},{10,11... | collective-permute-start | bytes 1179656 | tf_op jit(solution)/shard_map/ppermute | solution.py:380
  15.0 32.1 %copy-start.21 = (f32[64,256]{1,0:T(8,128)}, f32[64,256]{1,0:T(8,128)S(1)}, u32[]{:S(2)}) copy-start(f32[64,256]{1,0:T(8,128)S(1)} %collective-permute-done.8.bias_ref) | copy-start | bytes 196612
  15.0 32.1 %collective-permute-start.10 = (bf16[128,512]{1,0:T(8,128)(2,1)S(1)}, bf16[128,512]{1,0:T(8,128)(2,1)}, u32[]{:S(2)}, u32[]{:S(2)}) collective-permute-start(bf16[128,512]{1,0:T(8,128)(2,1)S(1)} %copy-done.9), channel_id=1, source_target_pairs={{0,2},{1,3},{2,0},{3,1},{4,6},{5,7},{6,4},{7,5},{8,10},{9,11},{10,... | collective-permute-start | bytes 393224 | tf_op jit(solution)/shard_map/ppermute | solution.py:380
  47.1 2.2 collective-permute-start.9
  47.1 6.3 %collective-permute-start.6 = (bf16[3,512,128]{2,1,0:T(8,128)(2,1)}, bf16[3,512,128]{2,1,0:T(8,128)(2,1)}, u32[]{:S(2)}, u32[]{:S(2)}) collective-permute-start(bf16[3,512,128]{2,1,0:T(8,128)(2,1)} %collective-permute-done.3.w_ref.refs_10_), channel_id=1, source_target_pairs={{0,1},{1,0},{2,3},{3,2},{4,5},{5,4},{6,7},{7,6},{8,9},{9,8},{10,11... | collective-permute-start | bytes 1179656 | tf_op jit(solution)/shard_map/ppermute | solution.py:380
  48.7 37.0 %collective-permute-start.16 = (bf16[512,512]{1,0:T(8,128)(2,1)}, bf16[512,512]{1,0:T(8,128)(2,1)}, u32[]{:S(2)}, u32[]{:S(2)}) collective-permute-start(bf16[512,512]{1,0:T(8,128)(2,1)} %collective-permute-done.14.w1_ref.refs_10_), channel_id=1, source_target_pairs={{0,1},{1,0},{2,3},{3,2},{4,5},{5,4},{6,7},{7,6},{8,9},{9,8},{10,11... | collective-permute-start | bytes 1572872 | tf_op jit(solution)/shard_map/ppermute | solution.py:380
  48.8 36.9 %collective-permute-start.17 = (bf16[512,512]{1,0:T(8,128)(2,1)}, bf16[512,512]{1,0:T(8,128)(2,1)}, u32[]{:S(2)}, u32[]{:S(2)}) collective-permute-start(bf16[512,512]{1,0:T(8,128)(2,1)} %collective-permute-done.15.w2_ref.refs_8_), channel_id=1, source_target_pairs={{0,1},{1,0},{2,3},{3,2},{4,5},{5,4},{6,7},{7,6},{8,9},{9,8},{10,11... | collective-permute-start | bytes 1572872 | tf_op jit(solution)/shard_map/ppermute | solution.py:380
  49.3 43.9 %collective-permute-start.12 = (bf16[512,512]{1,0:T(8,128)(2,1)}, bf16[512,512]{1,0:T(8,128)(2,1)}, u32[]{:S(2)}, u32[]{:S(2)}) collective-permute-start(bf16[512,512]{1,0:T(8,128)(2,1)} %refs_8_.4), channel_id=1, source_target_pairs={{0,1},{1,0},{2,3},{3,2},{4,5},{5,4},{6,7},{7,6},{8,9},{9,8},{10,11... | collective-permute-start | bytes 1572872 | tf_op jit(solution)/shard_map/ppermute | solution.py:380
  50.0 43.3 %collective-permute-start.13 = (bf16[512,512]{1,0:T(8,128)(2,1)}, bf16[512,512]{1,0:T(8,128)(2,1)}, u32[]{:S(2)}, u32[]{:S(2)}) collective-permute-start(bf16[512,512]{1,0:T(8,128)(2,1)} %refs_6_.1), channel_id=1, source_target_pairs={{0,1},{1,0},{2,3},{3,2},{4,5},{5,4},{6,7},{7,6},{8,9},{9,8},{10,11... | collective-permute-start | bytes 1572872 | tf_op jit(solution)/shard_map/ppermute | solution.py:380
  53.4 27.3 %collective-permute-start.11 = (bf16[128,512]{1,0:T(8,128)(2,1)}, bf16[128,512]{1,0:T(8,128)(2,1)}, u32[]{:S(2)}, u32[]{:S(2)}) collective-permute-start(bf16[128,512]{1,0:T(8,128)(2,1)} %collective-permute-done.10.refs_10_.wp_ref), channel_id=1, source_target_pairs={{0,1},{1,0},{2,3},{3,2},{4,5},{5,4},{6,7},{7,6},{8,9},{9,8},{10,11... | collective-permute-start | bytes 393224 | tf_op jit(solution)/shard_map/ppermute | solution.py:380
  92.7 65.6 %collective-permute-start.41 = (bf16[1024,512]{1,0:T(8,128)(2,1)}, bf16[1024,512]{1,0:T(8,128)(2,1)S(1)}, u32[]{:S(2)}, u32[]{:S(2)}) collective-permute-start(bf16[1024,512]{1,0:T(8,128)(2,1)} %get-tuple-element.137), channel_id=1, source_target_pairs={{0,1},{1,0},{2,3},{3,2},{4,5},{5,4},{6,7},{7,6},{8,9},{9,8},{10,11... | collective-permute-start | bytes 3145736 | tf_op jit(solution)/shard_map/ppermute | solution.py:380
  100.2 74.3 %collective-permute-start.43 = (bf16[1024,512]{1,0:T(8,128)(2,1)}, bf16[1024,512]{1,0:T(8,128)(2,1)}, u32[]{:S(2)}, u32[]{:S(2)}) collective-permute-start(bf16[1024,512]{1,0:T(8,128)(2,1)} %get-tuple-element.138), channel_id=1, source_target_pairs={{0,1},{1,0},{2,3},{3,2},{4,5},{5,4},{6,7},{7,6},{8,9},{9,8},{10,11... | collective-permute-start | bytes 3145736 | tf_op jit(solution)/shard_map/ppermute | solution.py:380
  131.5 39.6 %collective-permute-start.24 = (bf16[512,512]{1,0:T(8,128)(2,1)}, bf16[512,512]{1,0:T(8,128)(2,1)}, u32[]{:S(2)}, u32[]{:S(2)}) collective-permute-start(bf16[512,512]{1,0:T(8,128)(2,1)} %get-tuple-element.125), channel_id=1, source_target_pairs={{0,1},{1,0},{2,3},{3,2},{4,5},{5,4},{6,7},{7,6},{8,9},{9,8},{10,11... | collective-permute-start | bytes 1572872 | tf_op jit(solution)/shard_map/ppermute | solution.py:380
  158.7 26.1 %collective-permute-start.42 = (bf16[1024,512]{1,0:T(8,128)(2,1)S(1)}, bf16[1024,512]{1,0:T(8,128)(2,1)S(1)}, u32[]{:S(2)}, u32[]{:S(2)}) collective-permute-start(bf16[1024,512]{1,0:T(8,128)(2,1)S(1)} %add.131), channel_id=1, source_target_pairs={{0,2},{1,3},{2,0},{3,1},{4,6},{5,7},{6,4},{7,5},{8,10},{9,11},{10,... | collective-permute-start | bytes 3145736 | tf_op jit(solution)/shard_map/ppermute | solution.py:380
  170.8 45.7 %collective-permute-start.26 = (bf16[512,512]{1,0:T(8,128)(2,1)}, bf16[512,512]{1,0:T(8,128)(2,1)}, u32[]{:S(2)}, u32[]{:S(2)}) collective-permute-start(bf16[512,512]{1,0:T(8,128)(2,1)} %get-tuple-element.126), channel_id=1, source_target_pairs={{0,1},{1,0},{2,3},{3,2},{4,5},{5,4},{6,7},{7,6},{8,9},{9,8},{10,11... | collective-permute-start | bytes 1572872 | tf_op jit(solution)/shard_map/ppermute | solution.py:380
  173.1 43.5 %collective-permute-start.25 = (bf16[512,512]{1,0:T(8,128)(2,1)}, bf16[512,512]{1,0:T(8,128)(2,1)}, u32[]{:S(2)}, u32[]{:S(2)}) collective-permute-start(bf16[512,512]{1,0:T(8,128)(2,1)} %add.121), channel_id=1, source_target_pairs={{0,2},{1,3},{2,0},{3,1},{4,6},{5,7},{6,4},{7,5},{8,10},{9,11},{10,... | collective-permute-start | bytes 1572872 | tf_op jit(solution)/shard_map/ppermute | solution.py:380
  188.9 33.1 %collective-permute-start.44 = (bf16[512,512]{1,0:T(8,128)(2,1)}, bf16[512,512]{1,0:T(8,128)(2,1)S(1)}, u32[]{:S(2)}, u32[]{:S(2)}) collective-permute-start(bf16[512,512]{1,0:T(8,128)(2,1)} %get-tuple-element.140), channel_id=1, source_target_pairs={{0,4},{4,0},{8,12},{12,8},{16,20},{20,16},{24,28},{28,24},{1,5},{5... | collective-permute-start | bytes 1572872 | tf_op jit(solution)/shard_map/ppermute | solution.py:465
  190.6 1.3 collective-permute-start.18
  190.7 1.8 collective-permute-start.20
  191.9 3.9 %collective-permute-start.19 = (f32[4516]{0:T(1024)S(1)}, f32[4516]{0:T(1024)S(1)}, u32[]{:S(2)}, u32[]{:S(2)}) collective-permute-start(f32[4516]{0:T(1024)S(1)} %add.114), channel_id=1, source_target_pairs={{0,2},{1,3},{2,0},{3,1},{4,6},{5,7},{6,4},{7,5},{8,10},{9,11},{10,... | collective-permute-start | bytes 54200 | tf_op jit(solution)/shard_map/ppermute | solution.py:380
  195.8 6.3 %collective-permute-start.21 = (f32[4516]{0:T(1024)S(1)}, f32[4516]{0:T(1024)S(1)}, u32[]{:S(2)}, u32[]{:S(2)}) collective-permute-start(f32[4516]{0:T(1024)S(1)} %add_add_fusion), channel_id=1, source_target_pairs={{0,4},{4,0},{8,12},{12,8},{16,20},{20,16},{24,28},{28,24},{1,5},{5... | collective-permute-start | bytes 54200 | tf_op jit(solution)/shard_map/ppermute | solution.py:465
  202.0 3.8 %collective-permute-start.22 = (f32[4516]{0:T(1024)S(1)}, f32[4516]{0:T(1024)S(1)}, u32[]{:S(2)}, u32[]{:S(2)}) collective-permute-start(f32[4516]{0:T(1024)S(1)} %add.117), channel_id=1, source_target_pairs={{0,8},{4,12},{8,0},{12,4},{16,24},{20,28},{24,16},{28,20},{1,9},{5... | collective-permute-start | bytes 54200 | tf_op jit(solution)/shard_map/ppermute | solution.py:465
  205.8 19.8 %collective-permute-start.23 = (f32[4516]{0:T(1024)S(1)}, f32[4516]{0:T(1024)S(1)}, u32[]{:S(2)}, u32[]{:S(2)}) collective-permute-start(f32[4516]{0:T(1024)S(1)} %add.118), channel_id=1, source_target_pairs={{0,16},{4,20},{8,24},{12,28},{16,0},{20,4},{24,8},{28,12},{1,17},{... | collective-permute-start | bytes 54200 | tf_op jit(solution)/shard_map/ppermute | solution.py:465
  218.8 12.7 %collective-permute-start.27 = (bf16[64,512]{1,0:T(8,128)(2,1)}, bf16[64,512]{1,0:T(8,128)(2,1)S(1)}, u32[]{:S(2)}, u32[]{:S(2)}) collective-permute-start(bf16[64,512]{1,0:T(8,128)(2,1)} %get-tuple-element.128), channel_id=1, source_target_pairs={{0,4},{4,0},{8,12},{12,8},{16,20},{20,16},{24,28},{28,24},{1,5},{5... | collective-permute-start | bytes 196616 | tf_op jit(solution)/shard_map/ppermute | solution.py:465
  220.4 11.2 %collective-permute-start.28 = (bf16[64,512]{1,0:T(8,128)(2,1)}, bf16[64,512]{1,0:T(8,128)(2,1)S(1)}, u32[]{:S(2)}, u32[]{:S(2)}) collective-permute-start(bf16[64,512]{1,0:T(8,128)(2,1)} %get-tuple-element.129), channel_id=1, source_target_pairs={{0,8},{4,12},{8,0},{12,4},{16,24},{20,28},{24,16},{28,20},{1,9},{5... | collective-permute-start | bytes 196616 | tf_op jit(solution)/shard_map/ppermute | solution.py:465
  224.8 7.6 %collective-permute-start.45 = (bf16[128,512]{1,0:T(8,128)(2,1)}, bf16[128,512]{1,0:T(8,128)(2,1)S(1)}, u32[]{:S(2)}, u32[]{:S(2)}) collective-permute-start(bf16[128,512]{1,0:T(8,128)(2,1)} %get-tuple-element.142), channel_id=1, source_target_pairs={{0,8},{4,12},{8,0},{12,4},{16,24},{20,28},{24,16},{28,20},{1,9},{5... | collective-permute-start | bytes 393224 | tf_op jit(solution)/shard_map/ppermute | solution.py:465
  225.3 15.9 %collective-permute-start.46 = (bf16[128,512]{1,0:T(8,128)(2,1)}, bf16[128,512]{1,0:T(8,128)(2,1)S(1)}, u32[]{:S(2)}, u32[]{:S(2)}) collective-permute-start(bf16[128,512]{1,0:T(8,128)(2,1)} %get-tuple-element.143), channel_id=1, source_target_pairs={{0,16},{4,20},{8,24},{12,28},{16,0},{20,4},{24,8},{28,12},{1,17},{... | collective-permute-start | bytes 393224 | tf_op jit(solution)/shard_map/ppermute | solution.py:465
  225.6 17.0 %collective-permute-start.47 = (bf16[128,512]{1,0:T(8,128)(2,1)}, bf16[128,512]{1,0:T(8,128)(2,1)S(1)}, u32[]{:S(2)}, u32[]{:S(2)}) collective-permute-start(bf16[128,512]{1,0:T(8,128)(2,1)} %get-tuple-element.144), channel_id=1, source_target_pairs={{0,24},{4,28},{8,16},{12,20},{16,8},{20,12},{24,0},{28,4},{1,25},{... | collective-permute-start | bytes 393224 | tf_op jit(solution)/shard_map/ppermute | solution.py:465
  230.2 12.3 %copy-start.49 = (bf16[64,512]{1,0:T(8,128)(2,1)S(1)}, bf16[64,512]{1,0:T(8,128)(2,1)}, u32[]{:S(2)}) copy-start(bf16[64,512]{1,0:T(8,128)(2,1)} %get-tuple-element.134) | copy-start | bytes 196612
  230.3 14.7 %copy-start.16 = (bf16[128,512]{1,0:T(8,128)(2,1)S(1)}, bf16[128,512]{1,0:T(8,128)(2,1)}, u32[]{:S(2)}) copy-start(bf16[128,512]{1,0:T(8,128)(2,1)} %get-tuple-element.141) | copy-start | bytes 393220
  230.4 19.9 %copy-start.22 = (bf16[64,512]{1,0:T(8,128)(2,1)S(1)}, bf16[64,512]{1,0:T(8,128)(2,1)}, u32[]{:S(2)}) copy-start(bf16[64,512]{1,0:T(8,128)(2,1)} %get-tuple-element.127) | copy-start | bytes 196612
  231.5 13.5 %collective-permute-start.29 = (bf16[64,512]{1,0:T(8,128)(2,1)S(1)}, bf16[64,512]{1,0:T(8,128)(2,1)S(1)}, u32[]{:S(2)}, u32[]{:S(2)}) collective-permute-start(bf16[64,512]{1,0:T(8,128)(2,1)S(1)} %copy-done.53), channel_id=1, source_target_pairs={{0,12},{4,8},{8,4},{12,0},{16,28},{20,24},{24,20},{28,16},{1,13},{... | collective-permute-start | bytes 196616 | tf_op jit(solution)/shard_map/ppermute | solution.py:465
  231.6 13.8 %collective-permute-start.30 = (bf16[64,512]{1,0:T(8,128)(2,1)S(1)}, bf16[64,512]{1,0:T(8,128)(2,1)S(1)}, u32[]{:S(2)}, u32[]{:S(2)}) collective-permute-start(bf16[64,512]{1,0:T(8,128)(2,1)S(1)} %copy-done.52), channel_id=1, source_target_pairs={{0,16},{4,20},{8,24},{12,28},{16,0},{20,4},{24,8},{28,12},{1,17},{... | collective-permute-start | bytes 196616 | tf_op jit(solution)/shard_map/ppermute | solution.py:465
  232.4 15.8 %collective-permute-start.31 = (bf16[64,512]{1,0:T(8,128)(2,1)S(1)}, bf16[64,512]{1,0:T(8,128)(2,1)S(1)}, u32[]{:S(2)}, u32[]{:S(2)}) collective-permute-start(bf16[64,512]{1,0:T(8,128)(2,1)S(1)} %copy-done.51), channel_id=1, source_target_pairs={{0,20},{4,16},{8,28},{12,24},{16,4},{20,0},{24,12},{28,8},{1,21},{... | collective-permute-start | bytes 196616 | tf_op jit(solution)/shard_map/ppermute | solution.py:465
  241.2 6.9 %collective-permute-start.32 = (bf16[64,512]{1,0:T(8,128)(2,1)S(1)}, bf16[64,512]{1,0:T(8,128)(2,1)S(1)}, u32[]{:S(2)}, u32[]{:S(2)}) collective-permute-start(bf16[64,512]{1,0:T(8,128)(2,1)S(1)} %copy-done.50), channel_id=1, source_target_pairs={{0,24},{4,28},{8,16},{12,20},{16,8},{20,12},{24,0},{28,4},{1,25},{... | collective-permute-start | bytes 196616 | tf_op jit(solution)/shard_map/ppermute | solution.py:465
  242.6 7.7 %collective-permute-start.33 = (bf16[64,512]{1,0:T(8,128)(2,1)S(1)}, bf16[64,512]{1,0:T(8,128)(2,1)S(1)}, u32[]{:S(2)}, u32[]{:S(2)}) collective-permute-start(bf16[64,512]{1,0:T(8,128)(2,1)S(1)} %copy-done.49), channel_id=1, source_target_pairs={{0,28},{4,24},{8,20},{12,16},{16,12},{20,8},{24,4},{28,0},{1,29},{... | collective-permute-start | bytes 196616 | tf_op jit(solution)/shard_map/ppermute | solution.py:465
  245.0 26.2 %copy-start.13 = (bf16[128,512]{1,0:T(8,128)(2,1)}, bf16[128,512]{1,0:T(8,128)(2,1)S(1)}, u32[]{:S(2)}) copy-start(bf16[128,512]{1,0:T(8,128)(2,1)S(1)} %add_convert_fusion.refs_0_) | copy-start | bytes 393220
  245.0 14.4 %collective-permute-start.50 = (bf16[128,512]{1,0:T(8,128)(2,1)S(1)}, bf16[128,512]{1,0:T(8,128)(2,1)S(1)}, u32[]{:S(2)}, u32[]{:S(2)}) collective-permute-start(bf16[128,512]{1,0:T(8,128)(2,1)S(1)} %add_convert_fusion.refs_0_), channel_id=1, source_target_pairs={{0,24},{4,28},{8,16},{12,20},{16,8},{20,12},{24,0},{28,4},{1,25},{... | collective-permute-start | bytes 393224 | tf_op jit(solution)/shard_map/ppermute | solution.py:465
  250.3 27.4 %copy-start.15 = (bf16[64,512]{1,0:T(8,128)(2,1)}, bf16[64,512]{1,0:T(8,128)(2,1)S(1)}, u32[]{:S(2)}) copy-start(bf16[64,512]{1,0:T(8,128)(2,1)S(1)} %add_convert_fusion.1.refs_0_) | copy-start | bytes 196612
  250.3 22.9 %collective-permute-start.40 = (bf16[64,512]{1,0:T(8,128)(2,1)S(1)}, bf16[64,512]{1,0:T(8,128)(2,1)S(1)}, u32[]{:S(2)}, u32[]{:S(2)}) collective-permute-start(bf16[64,512]{1,0:T(8,128)(2,1)S(1)} %add_convert_fusion.1.refs_0_), channel_id=1, source_target_pairs={{0,28},{4,24},{8,20},{12,16},{16,12},{20,8},{24,4},{28,0},{1,29},{... | collective-permute-start | bytes 196616 | tf_op jit(solution)/shard_map/ppermute | solution.py:465
  252.8 20.7 %collective-permute-start.39 = (bf16[64,512]{1,0:T(8,128)(2,1)S(1)}, bf16[64,512]{1,0:T(8,128)(2,1)S(1)}, u32[]{:S(2)}, u32[]{:S(2)}) collective-permute-start(bf16[64,512]{1,0:T(8,128)(2,1)S(1)} %add_convert_fusion.1.refs_0_), channel_id=1, source_target_pairs={{0,24},{4,28},{8,16},{12,20},{16,8},{20,12},{24,0},{28,4},{1,25},{... | collective-permute-start | bytes 196616 | tf_op jit(solution)/shard_map/ppermute | solution.py:465
  254.5 19.9 %collective-permute-start.38 = (bf16[64,512]{1,0:T(8,128)(2,1)S(1)}, bf16[64,512]{1,0:T(8,128)(2,1)S(1)}, u32[]{:S(2)}, u32[]{:S(2)}) collective-permute-start(bf16[64,512]{1,0:T(8,128)(2,1)S(1)} %add_convert_fusion.1.refs_0_), channel_id=1, source_target_pairs={{0,20},{4,16},{8,28},{12,24},{16,4},{20,0},{24,12},{28,8},{1,21},{... | collective-permute-start | bytes 196616 | tf_op jit(solution)/shard_map/ppermute | solution.py:465
  259.1 9.3 %collective-permute-start.49 = (bf16[128,512]{1,0:T(8,128)(2,1)S(1)}, bf16[128,512]{1,0:T(8,128)(2,1)S(1)}, u32[]{:S(2)}, u32[]{:S(2)}) collective-permute-start(bf16[128,512]{1,0:T(8,128)(2,1)S(1)} %add_convert_fusion.refs_0_), channel_id=1, source_target_pairs={{0,16},{4,20},{8,24},{12,28},{16,0},{20,4},{24,8},{28,12},{1,17},{... | collective-permute-start | bytes 393224 | tf_op jit(solution)/shard_map/ppermute | solution.py:465
  259.5 11.7 %copy-start.17 = (bf16[128,512]{1,0:T(8,128)(2,1)}, bf16[128,512]{1,0:T(8,128)(2,1)S(1)}, u32[]{:S(2)}) copy-start(bf16[128,512]{1,0:T(8,128)(2,1)S(1)} %collective-permute-done.50.refs_3_) | copy-start | bytes 393220
  259.5 8.9 %collective-permute-start.48 = (bf16[128,512]{1,0:T(8,128)(2,1)S(1)}, bf16[128,512]{1,0:T(8,128)(2,1)S(1)}, u32[]{:S(2)}, u32[]{:S(2)}) collective-permute-start(bf16[128,512]{1,0:T(8,128)(2,1)S(1)} %add_convert_fusion.refs_0_), channel_id=1, source_target_pairs={{0,8},{4,12},{8,0},{12,4},{16,24},{20,28},{24,16},{28,20},{1,9},{5... | collective-permute-start | bytes 393224 | tf_op jit(solution)/shard_map/ppermute | solution.py:465
  268.4 8.5 %collective-permute-start.37 = (bf16[64,512]{1,0:T(8,128)(2,1)S(1)}, bf16[64,512]{1,0:T(8,128)(2,1)S(1)}, u32[]{:S(2)}, u32[]{:S(2)}) collective-permute-start(bf16[64,512]{1,0:T(8,128)(2,1)S(1)} %add_convert_fusion.1.refs_0_), channel_id=1, source_target_pairs={{0,16},{4,20},{8,24},{12,28},{16,0},{20,4},{24,8},{28,12},{1,17},{... | collective-permute-start | bytes 196616 | tf_op jit(solution)/shard_map/ppermute | solution.py:465
  268.4 8.5 %collective-permute-start.36 = (bf16[64,512]{1,0:T(8,128)(2,1)S(1)}, bf16[64,512]{1,0:T(8,128)(2,1)S(1)}, u32[]{:S(2)}, u32[]{:S(2)}) collective-permute-start(bf16[64,512]{1,0:T(8,128)(2,1)S(1)} %add_convert_fusion.1.refs_0_), channel_id=1, source_target_pairs={{0,12},{4,8},{8,4},{12,0},{16,28},{20,24},{24,20},{28,16},{1,13},{... | collective-permute-start | bytes 196616 | tf_op jit(solution)/shard_map/ppermute | solution.py:465
  273.2 4.3 %collective-permute-start.35 = (bf16[64,512]{1,0:T(8,128)(2,1)S(1)}, bf16[64,512]{1,0:T(8,128)(2,1)S(1)}, u32[]{:S(2)}, u32[]{:S(2)}) collective-permute-start(bf16[64,512]{1,0:T(8,128)(2,1)S(1)} %add_convert_fusion.1.refs_0_), channel_id=1, source_target_pairs={{0,8},{4,12},{8,0},{12,4},{16,24},{20,28},{24,16},{28,20},{1,9},{5... | collective-permute-start | bytes 196616 | tf_op jit(solution)/shard_map/ppermute | solution.py:465
  273.4 4.3 %collective-permute-start.34 = (bf16[64,512]{1,0:T(8,128)(2,1)S(1)}, bf16[64,512]{1,0:T(8,128)(2,1)S(1)}, u32[]{:S(2)}, u32[]{:S(2)}) collective-permute-start(bf16[64,512]{1,0:T(8,128)(2,1)S(1)} %add_convert_fusion.1.refs_0_), channel_id=1, source_target_pairs={{0,4},{4,0},{8,12},{12,8},{16,20},{20,16},{24,28},{28,24},{1,5},{5... | collective-permute-start | bytes 196616 | tf_op jit(solution)/shard_map/ppermute | solution.py:465
  274.4 9.5 %collective-permute-start.51 = (bf16[512,512]{1,0:T(8,128)(2,1)}, bf16[512,512]{1,0:T(8,128)(2,1)S(1)}, u32[]{:S(2)}, u32[]{:S(2)}) collective-permute-start(bf16[512,512]{1,0:T(8,128)(2,1)} %merge.4.refs_0_), channel_id=1, source_target_pairs={{0,4},{4,0},{8,12},{12,8},{16,20},{20,16},{24,28},{28,24},{1,5},{5... | collective-permute-start | bytes 1572872 | tf_op jit(solution)/shard_map/ppermute | solution.py:465
  (42 other events, 195.8 us)

commit v2 on v1

--- a/solution.py
+++ b/solution.py
@@ -11,6 +11,7 @@
 IMG_TOKENS = 196
 ROW_TILE = 16
 CHUNK = 256
+TOGETHER = 4
 FAR_BELOW = -1e30
 
 eps = 1e-05
@@ -66,11 +67,10 @@
 
 
 def each_window(windows, body):
-    together = 4 if windows % 4 == 0 else 1
+    together = TOGETHER if windows % TOGETHER == 0 else 1
 
     def step(i, carry):
-        for j in range(together):
-            body(i * together + j)
+        body([i * together + j for j in range(together)])
         return carry
 
     lax.fori_loop(0, windows // together, step, 0)
@@ -88,16 +88,19 @@
     put(2, dot(xn, w_ref[2], 1, 0) + vec_ref[:, width : 2 * width])
     masks = head_masks(heads, width)
 
-    def window(w):
-        scores = dot(qkv_ref[1, w], spread(qkv_ref[0, w], masks), 1, 1) + bias_ref[...]
-        top = jnp.max(scores, axis=0, keepdims=True)
-        powers = jnp.exp(scores - top)
-        probs = powers * (1.0 / jnp.sum(powers, axis=0, keepdims=True))
-        p_ref[w] = probs
-        att = fold(dot(probs.astype(bf16), qkv_ref[2, w], 0, 0), masks)
-        att_ref[w] = att.astype(bf16)
-
-    each_window(windows, window)
+    def some(ws):
+        queries = [spread(qkv_ref[0, w], masks) for w in ws]
+        scores = [dot(qkv_ref[1, w], q, 1, 1) + bias_ref[...] for w, q in zip(ws, queries)]
+        tops = [jnp.max(x, axis=0, keepdims=True) for x in scores]
+        powers = [jnp.exp(x - top) for x, top in zip(scores, tops)]
+        sums = [jnp.sum(x, axis=0, keepdims=True) for x in powers]
+        probs = [x * (1.0 / total) for x, total in zip(powers, sums)]
+        outs = [dot(x.astype(bf16), qkv_ref[2, w], 0, 0) for w, x in zip(ws, probs)]
+        for w, x, out in zip(ws, probs, outs):
+            p_ref[w] = x
+            att_ref[w] = fold(out, masks).astype(bf16)
+
+    each_window(windows, some)
 
 
 def attend(xn, w, vec, bias, heads, scale, windows, padded):
@@ -139,21 +142,24 @@
     gb_ref[...] = jnp.zeros_like(gb_ref)
     masks = head_masks(heads, width)
 
-    def window(w):
-        probs = p_ref[w]
-        spread_d = spread(datt_ref[w], masks)
-        dv = dot(probs.astype(bf16), spread_d, 1, 0)
-        dprobs = dot(qkv_ref[2, w], spread_d, 1, 1)
-        dscores = probs * (dprobs - jnp.sum(probs * dprobs, axis=0, keepdims=True))
-        ds_ref[...] += dscores
-        ds_b = dscores.astype(bf16)
-        dk = dot(ds_b, spread(qkv_ref[0, w], masks), 1, 0)
-        dq = fold(dot(ds_b, qkv_ref[1, w], 0, 0), masks) * scale
-        dqkv_ref[w] = jnp.concatenate([dq, dk, dv], axis=1).astype(bf16)
-        gb_ref[0:1, :] += jnp.sum(dq, axis=0, keepdims=True)
-        gb_ref[1:2, :] += jnp.sum(dv, axis=0, keepdims=True)
-
-    each_window(windows, window)
+    def some(ws):
+        probs = [p_ref[w] for w in ws]
+        grads = [spread(datt_ref[w], masks) for w in ws]
+        dprobs = [dot(qkv_ref[2, w], d, 1, 1) for w, d in zip(ws, grads)]
+        dvs = [dot(x.astype(bf16), d, 1, 0) for x, d in zip(probs, grads)]
+        inner = [jnp.sum(x * dx, axis=0, keepdims=True) for x, dx in zip(probs, dprobs)]
+        dscores = [x * (dx - total) for x, dx, total in zip(probs, dprobs, inner)]
+        ds_b = [x.astype(bf16) for x in dscores]
+        queries = [spread(qkv_ref[0, w], masks) for w in ws]
+        dks = [dot(x, q, 1, 0) for x, q in zip(ds_b, queries)]
+        dqs = [fold(dot(x, qkv_ref[1, w], 0, 0), masks) * scale for w, x in zip(ws, ds_b)]
+        for w, dq, dk, dv in zip(ws, dqs, dks, dvs):
+            dqkv_ref[w] = jnp.concatenate([dq, dk, dv], axis=1).astype(bf16)
+        ds_ref[...] += sum(dscores)
+        gb_ref[0:1, :] += jnp.sum(sum(dqs), axis=0, keepdims=True)
+        gb_ref[1:2, :] += jnp.sum(sum(dvs), axis=0, keepdims=True)
+
+    each_window(windows, some)
     dqkv = dqkv_ref[...].reshape(windows * padded, 3 * width)
     g_ref[:, : 3 * width] = dot(xn_ref[...], dqkv, 0, 0).astype(bf16)
     g_ref[:, 3 * width :] = dot(dmid, att_ref[...], 0, 0).astype(bf16)
@@ -228,21 +234,35 @@
 
 
 def merge_kernel(ways, digit_ref, *refs):
-    out_ref = refs[ways]
+    out_ref = refs[-1]
     rows = refs[0].shape[0]
     for j in range(ways):
         start = pl.multiple_of((digit_ref[0] ^ j) * rows, rows)
         out_ref[pl.ds(start, rows), :] = refs[j][...].astype(out_ref.dtype)
-
-
-def merge(pieces, digit, dtype):
+    if len(refs) == ways + 1:
+        return
+    first, second = refs[ways : ways + 2]
+    if len(first.shape) == 3:
+        cols = first.shape[2]
+        for c in range(3):
+            first[c] = out_ref[:, c * cols : (c + 1) * cols]
+        second[...] = out_ref[:, 3 * cols :].T
+    else:
+        ff = second.shape[0]
+        first[...] = out_ref[:ff, :].T
+        second[...] = out_ref[ff:, :]
+
+
+def merge(pieces, digit, results):
     ways = len(pieces)
     rows, width = pieces[0].shape
+    whole = (rows * ways, width)
     return pl.pallas_call(
         functools.partial(merge_kernel, ways),
         in_specs=[pl.BlockSpec(memory_space=pltpu.SMEM)]
         + [pl.BlockSpec(memory_space=pltpu.VMEM)] * ways,
-        out_shape=shape_of((rows * ways, width), dtype),
+        out_shape=[shape_of(r) for r in results] if results else shape_of(whole, bf16),
+        scratch_shapes=[pltpu.VMEM(whole, f32)] if results else [],
         name="merge",
     )(digit, *pieces)
 
@@ -470,22 +490,25 @@
             got.append(swap_dp(piece, j * stride) if j else piece)
         return got
 
-    def sum_dp(terms, ways):
+    def sum_dp(terms, ways, results):
         stages = []
         stride = 1
         for way in ways:
             stages.append((stride, way, (group // stride % way).reshape(1)))
             stride *= way
+        first = None
         for stride, way, digit in stages:
-            terms = swap_all(split(terms, digit, way), stride)
+            pieces = split(terms, digit, way)
+            first = pieces[0] if first is None else first
+            terms = swap_all(pieces, stride)
         total = terms[0].astype(f32)
         for term in terms[1:]:
             total = total + term.astype(f32)
         total = total.astype(bf16)
         for at, (stride, way, digit) in reversed(list(enumerate(stages))):
             pieces = swap_all([total] * way, stride)
-            total = merge(pieces, digit, f32 if at == 0 else bf16)
-        return total
+            total = merge(pieces, digit, None if at else results)
+        return total, first
 
     def ways_of(most):
         left = groups
@@ -495,8 +518,8 @@
             left //= ways[-1]
         return ways
 
-    g_fc = sum_dp(scatter(g_fcs), ways_of((2, 4)))
-    g_fc1, g_fc2 = g_fc[:ff].T, g_fc[ff:]
+    g_fc, _ = sum_dp(scatter(g_fcs), ways_of((4, 2)), [(width, ff), (ff, width)])
+    g_fc1, g_fc2 = g_fc
 
     listed = lambda parts: [parts[m] for m in order]
     dmid, dmid_b, sums2 = by_rows(
@@ -515,10 +538,8 @@
             dmid_b, xn1, wps[m], qkvs[m], probs[m], atts[m], heads, scale
         )
         dqkvs[m] = dqkv.reshape(n, -1)
-    g_att = sum_dp(scatter(g_atts), ways_of((8,)))
-    cols = w_qkv.shape[2]
-    g_qkv = jnp.stack([g_att[:, c * cols : (c + 1) * cols] for c in range(3)])
-    g_proj = g_att[:, 3 * cols :].T
+    g_att, after_split = sum_dp(scatter(g_atts), ways_of((4, 2)), [w_qkv.shape, w_proj.shape])
+    g_qkv, g_proj = g_att
 
     in_grad, sums1 = by_rows(
         functools.partial(in_back_kernel, shards),
@@ -542,7 +563,8 @@
     outputs = jnp.where(live, outputs, jnp.zeros_like(outputs))
     in_grad = cut_rows(in_grad)
 
-    ds_all = jnp.stack(listed(dss)).reshape(shards, padded, heads, padded)
+    *late_ds, _ = lax.optimization_barrier((*listed(dss), after_split))
+    ds_all = jnp.stack(late_ds).reshape(shards, padded, heads, padded)
     g_tabs = jnp.einsum(
         "qkt,mkhq->mth", onehot, ds_all, precision=lax.Precision.HIGHEST
     )

time: 293 us -> 243 us (0.83)
  waiting for transfers between devices: 71 us -> 40 us
  starting transfers between devices: 53.2 us -> 41.9 us
  Pallas kernels: 130 us -> 120 us
    ppermute x27, waiting for transfers between devices: 46.7 us -> 27.8 us  [swap(): return lax.ppermute(value, 'tensor', [(i, i ^ bit) for i in range(shards)])]
    ppermute x25 -> x19, starting transfers between devices: 39.2 us -> 26.8 us  [swap_dp(): return lax.ppermute(value, 'dp', [(i, i ^ bits) for i in range(groups)])]
    ppermute x25 -> x19, waiting for transfers between devices: 24.3 us -> 12.2 us  [swap_dp(): return lax.ppermute(value, 'dp', [(i, i ^ bits) for i in range(groups)])]
    pallas_call x4, Pallas kernels: 35.4 us -> 25.6 us  [attend_back(): pl.pallas_call(functools.partial(attend_back_kernel, heads, scale), out_s...]
    pallas_call x4, Pallas kernels: 24.5 us -> 20.9 us  [attend(): pl.pallas_call(functools.partial(attend_kernel, heads, scale), out_shape=...]
    unnamed x117 -> x121, local copies, waits for them, and re-layouts: 9.26 us -> 12.3 us
    pallas_call x3 -> x4, Pallas kernels: 7.43 us -> 9.21 us  [split(): pl.pallas_call(functools.partial(split_kernel, len(values)), in_specs=[pl...]
    pallas_call x3 -> x4, Pallas kernels: 6.68 us -> 8.42 us  [merge(): pl.pallas_call(functools.partial(merge_kernel, ways), in_specs=[pl.BlockS...]
  transfers between devices with their start and end apart: 52 -> 46, of which waited for: 16 -> 9; matrix products, arithmetic and copies ran while one was open for 9% -> 11% of each run, Pallas kernels for 44% -> 48%
where the time goes in v2:
time: 243 us; the launch traced here: 242 us
  Pallas kernels  120 us (49%)
  starting transfers between devices  41.9 us (17%)
  waiting for transfers between devices  40 us (16%)
  local copies, waits for them, and re-layouts  25.8 us (11%)
  matrix products  6.03 us (2%)
  other arithmetic  5.91 us (2%)
    pallas_call x8, Pallas kernels, by_rows(): pl.pallas_call(kernel, grid=(rows // chunk,), in_specs=[cut_spec(v) for v...  55.8 us
    ppermute x27, waiting for transfers between devices, swap(): return lax.ppermute(value, 'tensor', [(i, i ^ bit) for i in range(shards)])  27.8 us
    ppermute x19, starting transfers between devices, swap_dp(): return lax.ppermute(value, 'dp', [(i, i ^ bits) for i in range(groups)])  26.8 us
    pallas_call x4, Pallas kernels, attend_back(): pl.pallas_call(functools.partial(attend_back_kernel, heads, scale), out_s...  25.6 us
    pallas_call x4, Pallas kernels, attend(): pl.pallas_call(functools.partial(attend_kernel, heads, scale), out_shape=...  20.9 us
    ppermute x27, starting transfers between devices, swap(): return lax.ppermute(value, 'tensor', [(i, i ^ bit) for i in range(shards)])  15.1 us
    unnamed x121, local copies, waits for them, and re-layouts  12.3 us
    ppermute x19, waiting for transfers between devices, swap_dp(): return lax.ppermute(value, 'dp', [(i, i ^ bits) for i in range(groups)])  12.2 us
  transfers between devices with their start and end apart: 46, of which 9 were waited for; matrix products, arithmetic and copies ran while one was open for 11% of the time, Pallas kernels for 48%

profile of v2, /device:TPU:0, one launch (start us, length us, event | category | flops | bytes accessed | tf_op | source)
XLA Modules:
  0.0 241.6 jit_solution(10583035811153530509)
XLA Ops:
  0.7 0.8 pad_maximum_fusion.2
  1.5 3.0 %collective-permute-start.4 = (f32[1,768]{1,0:T(1,128)S(1)}, f32[1,768]{1,0:T(1,128)S(1)}, u32[]{:S(2)}, u32[]{:S(2)}) collective-permute-start(f32[1,768]{1,0:T(1,128)S(1)} %reshape.197.vec_ref), channel_id=1, source_target_pairs={{0,2},{1,3},{2,0},{3,1},{4,6},{5,7},{6,4},{7,5},{8,10},{9,11},{10,... | collective-permute-start | bytes 9224 | tf_op jit(solution)/shard_map/ppermute | solution.py:400
  4.5 0.8 copy.44
  6.0 2.8 %fusion.1 = f32[64,64,4]{0,2,1:T(4,128)S(1)} fusion(s32[64,64]{0,1:T(8,128)S(1)} %pad.16.clone, f32[169,4]{0,1:T(4,128)S(1)} %copy-done), kind=kOutput, calls=%fused_computation.2 | convolution fusion | flops 33918976 | bytes 84624 | tf_op jit(solution)/shard_map/qkt,th->khq/dot_general | solution.py:420
  9.9 1.7 collective-permute-start.3
  12.9 1.2 collective-permute-done.7.vec_ref
  15.0 7.9 %collective-permute-done.3.w_ref.refs_10_ = bf16[3,512,128]{2,1,0:T(8,128)(2,1)} collective-permute-done((bf16[3,512,128]{2,1,0:T(8,128)(2,1)S(1)}, bf16[3,512,128]{2,1,0:T(8,128)(2,1)}, u32[]{:S(2)}, u32[]{:S(2)}) %collective-permute-start.3) | collective-permute-done | bytes 393248 | tf_op jit(solution)/shard_map/ppermute | solution.py:400
  25.8 1.5 collective-permute-start.15
  27.7 1.1 pad.15
  29.5 5.2 %attend.4 = (bf16[3,16,64,128]{3,2,1,0:T(8,128)(2,1)}, f32[16,64,256]{2,1,0:T(8,128)}, bf16[16,64,128]{2,1,0:T(8,128)(2,1)}) custom-call(bf16[1024,512]{1,0:T(8,128)(2,1)} %bitcast.58, bf16[3,512,128]{2,1,0:T(8,128)(2,1)} %refs_8_.5, f32[1,768]{1,0:T(1,128)} %copy-done.40, f32[64,256]{1,0:T(8,128)} %copy-done.17), custom_call_target="tpu_custom_call" | custom-call | flops 402653184 | bytes 2097152 | tf_op jit(solution)/shard_map/attend/pallas_call | solution.py:109
  35.2 1.1 pad.17
  36.3 1.1 pad.14
  37.4 5.2 %attend.6 = (bf16[3,16,64,128]{3,2,1,0:T(8,128)(2,1)}, f32[16,64,256]{2,1,0:T(8,128)}, bf16[16,64,128]{2,1,0:T(8,128)(2,1)}) custom-call(bf16[1024,512]{1,0:T(8,128)(2,1)} %bitcast.59, bf16[3,512,128]{2,1,0:T(8,128)(2,1)} %collective-permute-done.3.w_ref.refs_10_, f32[1,768]{1,0:T(1,128)} %copy-done.46, f32[64,256]{1,0:T(8,128)} %copy-done.33), custom_call_target="tpu_custom_call" | custom-call | flops 402653184 | bytes 2097152 | tf_op jit(solution)/shard_map/attend/pallas_call | solution.py:109
  42.6 5.2 %attend.5 = (bf16[3,16,64,128]{3,2,1,0:T(8,128)(2,1)}, f32[16,64,256]{2,1,0:T(8,128)}, bf16[16,64,128]{2,1,0:T(8,128)(2,1)}) custom-call(bf16[1024,512]{1,0:T(8,128)(2,1)} %bitcast.60, bf16[3,512,128]{2,1,0:T(8,128)(2,1)} %copy-done.4, f32[1,768]{1,0:T(1,128)} %copy-done.47, f32[64,256]{1,0:T(8,128)} %copy-done.32), custom_call_target="tpu_custom_call" | custom-call | flops 402653184 | bytes 2097152 | tf_op jit(solution)/shard_map/attend/pallas_call | solution.py:109
  47.8 5.3 %attend.7 = (bf16[3,16,64,128]{3,2,1,0:T(8,128)(2,1)}, f32[16,64,256]{2,1,0:T(8,128)}, bf16[16,64,128]{2,1,0:T(8,128)(2,1)}) custom-call(bf16[1024,512]{1,0:T(8,128)(2,1)} %bitcast.61, bf16[3,512,128]{2,1,0:T(8,128)(2,1)} %collective-permute-done.6.w_ref.refs_11_, f32[1,768]{1,0:T(1,128)} %copy-done.48, f32[64,256]{1,0:T(8,128)} %copy-done.34), custom_call_target="tpu_custom_call" | custom-call | flops 402653184 | bytes 2097152 | tf_op jit(solution)/shard_map/attend/pallas_call | solution.py:109
  53.6 5.1 %shard_map.280 = (f32[1024,512]{1,0:T(8,128)}, bf16[1024,512]{1,0:T(8,128)(2,1)}) custom-call(bf16[1024,512]{1,0:T(8,128)(2,1)} %bitcast.66, bf16[1024,128]{1,0:T(8,128)(2,1)} %bitcast.74, bf16[1024,128]{1,0:T(8,128)(2,1)} %bitcast.78, bf16[1024,128]{1,0:T(8,128)(2,1)} %bitcast.76, bf16[1024,128]{1,0:T(8,128)(2,1)} %bitcast.80, f32[1,512]{1,0:T(1,128)} %bitcast.101, ...), custom_call_target="tpu_custom_call" | custom-call | flops 536870912 | bytes 2097152 | tf_op jit(solution)/shard_map/pallas_call | solution.py:279
  58.7 7.0 %shard_map.282 = (bf16[1024,512]{1,0:T(8,128)(2,1)}, bf16[1024,512]{1,0:T(8,128)(2,1)}, f32[1,512]{1,0:T(1,128)}, bf16[1024,512]{1,0:T(8,128)(2,1)}) custom-call(bf16[1024,512]{1,0:T(8,128)(2,1)} %get-tuple-element.91.xn_ref, bf16[1024,512]{1,0:T(8,128)(2,1)} %bitcast.68, bf16[512,512]{1,0:T(8,128)(2,1)} %collective-permute-done.12.w1_ref.refs_9_, ...), custom_call_target="tpu_custom_call" | custom-call | flops 2147483648 | bytes 2097152 | tf_op jit(solution)/shard_map/pallas_call | solution.py:279
  66.2 7.0 %shard_map.281 = (bf16[1024,512]{1,0:T(8,128)(2,1)}, bf16[1024,512]{1,0:T(8,128)(2,1)}, f32[1,512]{1,0:T(1,128)}, bf16[1024,512]{1,0:T(8,128)(2,1)}) custom-call(bf16[1024,512]{1,0:T(8,128)(2,1)} %get-tuple-element.91.xn_ref, bf16[1024,512]{1,0:T(8,128)(2,1)} %bitcast.69, bf16[512,512]{1,0:T(8,128)(2,1)} %refs_8_.4, f32[1,768]{1,0:T(1,128)} %copy-done.40, ...), custom_call_target="tpu_custom_call" | custom-call | flops 2147483648 | bytes 2097152 | tf_op jit(solution)/shard_map/pallas_call | solution.py:279
  73.2 7.2 %shard_map.283 = (bf16[1024,512]{1,0:T(8,128)(2,1)}, bf16[1024,512]{1,0:T(8,128)(2,1)}, f32[1,512]{1,0:T(1,128)}, bf16[1024,512]{1,0:T(8,128)(2,1)}) custom-call(bf16[1024,512]{1,0:T(8,128)(2,1)} %get-tuple-element.91.xn_ref, bf16[1024,512]{1,0:T(8,128)(2,1)} %bitcast.70, bf16[512,512]{1,0:T(8,128)(2,1)} %collective-permute-done.14.w1_ref.refs_10_, ...), custom_call_target="tpu_custom_call" | custom-call | flops 2147483648 | bytes 2097152 | tf_op jit(solution)/shard_map/pallas_call | solution.py:279
  81.2 0.8 copy-done.10
  82.0 7.0 %shard_map.284 = (bf16[1024,512]{1,0:T(8,128)(2,1)}, bf16[1024,512]{1,0:T(8,128)(2,1)}, f32[1,512]{1,0:T(1,128)}, bf16[1024,512]{1,0:T(8,128)(2,1)}) custom-call(bf16[1024,512]{1,0:T(8,128)(2,1)} %get-tuple-element.91.xn_ref, bf16[1024,512]{1,0:T(8,128)(2,1)} %bitcast.71, bf16[512,512]{1,0:T(8,128)(2,1)} %copy-done.11, f32[1,768]{1,0:T(1,128)} %copy-done.48, ...), custom_call_target="tpu_custom_call" | custom-call | flops 2147483648 | bytes 2097152 | tf_op jit(solution)/shard_map/pallas_call | solution.py:279
  89.2 8.0 %shard_map.286 = (f32[1024,512]{1,0:T(8,128)}, bf16[1024,512]{1,0:T(8,128)(2,1)}, f32[8,512]{1,0:T(8,128)}) custom-call(f32[1024,512]{1,0:T(8,128)} %get-tuple-element.90.refs_0_, bf16[1024,512]{1,0:T(8,128)(2,1)} %bitcast.72, bf16[1024,512]{1,0:T(8,128)(2,1)} %get-tuple-element.96.refs_2_, bf16[1024,512]{1,0:T(8,128)(2,1)} %get-tuple-element.97.refs_3_, ...), custom_call_target="tpu_custom_call" | custom-call | flops 2147483648 | bytes 7340032 | tf_op jit(solution)/shard_map/pallas_call | solution.py:279
  97.2 6.4 %attend_back.7 = (bf16[16,64,384]{2,1,0:T(8,128)(2,1)}, bf16[512,512]{1,0:T(8,128)(2,1)}, f32[64,256]{1,0:T(8,128)}, f32[2,128]{1,0:T(2,128)}) custom-call(bf16[1024,512]{1,0:T(8,128)(2,1)} %get-tuple-element.101.dmid_ref, bf16[1024,512]{1,0:T(8,128)(2,1)} %bitcast.62, bf16[128,512]{1,0:T(8,128)(2,1)} %collective-permute-done.11.refs_11_.wp_ref, ...), custom_call_target="tpu_custom_call" | custom-call | flops 1073741824 | bytes 2097152 | tf_op jit(solution)/shard_map/attend_back/pallas_call | solution.py:170
  104.0 6.4 %attend_back.5 = (bf16[16,64,384]{2,1,0:T(8,128)(2,1)}, bf16[512,512]{1,0:T(8,128)(2,1)}, f32[64,256]{1,0:T(8,128)}, f32[2,128]{1,0:T(2,128)}) custom-call(bf16[1024,512]{1,0:T(8,128)(2,1)} %get-tuple-element.101.dmid_ref, bf16[1024,512]{1,0:T(8,128)(2,1)} %bitcast.63, bf16[128,512]{1,0:T(8,128)(2,1)} %copy-done.14, ...), custom_call_target="tpu_custom_call" | custom-call | flops 1073741824 | bytes 2097152 | tf_op jit(solution)/shard_map/attend_back/pallas_call | solution.py:170
  110.5 6.4 %attend_back.4 = (bf16[16,64,384]{2,1,0:T(8,128)(2,1)}, bf16[512,512]{1,0:T(8,128)(2,1)}, f32[64,256]{1,0:T(8,128)}, f32[2,128]{1,0:T(2,128)}) custom-call(bf16[1024,512]{1,0:T(8,128)(2,1)} %get-tuple-element.101.dmid_ref, bf16[1024,512]{1,0:T(8,128)(2,1)} %bitcast.64, bf16[128,512]{1,0:T(8,128)(2,1)} %wp_ref.1, ...), custom_call_target="tpu_custom_call" | custom-call | flops 1073741824 | bytes 2097152 | tf_op jit(solution)/shard_map/attend_back/pallas_call | solution.py:170
  116.9 6.4 %attend_back.6 = (bf16[16,64,384]{2,1,0:T(8,128)(2,1)}, bf16[512,512]{1,0:T(8,128)(2,1)}, f32[64,256]{1,0:T(8,128)}, f32[2,128]{1,0:T(2,128)}) custom-call(bf16[1024,512]{1,0:T(8,128)(2,1)} %get-tuple-element.101.dmid_ref, bf16[1024,512]{1,0:T(8,128)(2,1)} %bitcast.65, bf16[128,512]{1,0:T(8,128)(2,1)} %collective-permute-done.10.refs_10_.wp_ref, ...), custom_call_target="tpu_custom_call" | custom-call | flops 1073741824 | bytes 2097152 | tf_op jit(solution)/shard_map/attend_back/pallas_call | solution.py:170
  123.3 7.8 %shard_map.287 = (bf16[1024,512]{1,0:T(8,128)(2,1)}, f32[8,512]{1,0:T(8,128)}) custom-call(bf16[1024,512]{1,0:T(8,128)(2,1)} %bitcast.67, f32[1024,512]{1,0:T(8,128)} %get-tuple-element.100.refs_1_, bf16[1024,384]{1,0:T(8,128)(2,1)} %bitcast.85, bf16[1024,384]{1,0:T(8,128)(2,1)} %bitcast.84, bf16[1024,384]{1,0:T(8,128)(2,1)} %bitcast.86, ...), custom_call_target="tpu_custom_call" | custom-call | flops 1610612736 | bytes 6291456 | tf_op jit(solution)/shard_map/pallas_call | solution.py:279
  131.1 0.8 slice_bitcast_fusion.1
  132.1 1.1 collective-permute-start.19
  134.2 1.0 collective-permute-start.36
  135.4 11.6 %collective-permute-done.19.refs_1_ = bf16[512,512]{1,0:T(8,128)(2,1)S(1)} collective-permute-done((bf16[512,512]{1,0:T(8,128)(2,1)S(1)}, bf16[512,512]{1,0:T(8,128)(2,1)S(1)}, u32[]{:S(2)}, u32[]{:S(2)}) %collective-permute-start.19) | collective-permute-done | bytes 524320 | tf_op jit(solution)/shard_map/ppermute | solution.py:400
  147.8 2.3 split.4
  150.3 1.0 stack.47
  151.2 1.6 stack.48
  152.8 3.2 %fusion.12 = f32[4,169,4]{1,2,0:T(4,128)} fusion(s32[64,64]{0,1:T(8,128)} %copy-done.39, f32[1,64,4,64]{3,2,1,0:T(4,128)} %stack.48, f32[1,64,4,64]{3,2,1,0:T(4,128)S(1)} %stack.47, f32[1,64,4,64]{3,2,1,0:T(4,128)S(1)} %stack.46, f32[1,64,4,64]{3,2,1,0:T(4,128)S(1)} %stack.45), kind=kOutput, calls=%fused_computation.14 | convolution fusion | flops 133795840 | bytes 289344 | tf_op jit(solution)/shard_map/qkt,mkhq->mth/dot_general | solution.py:568
  156.0 0.9 copy.38
  157.2 0.8 concatenate.13
  159.5 1.0 collective-permute-start.22
  160.5 1.5 collective-permute-start.27
  162.0 1.6 collective-permute-start.28
  163.6 5.7 %collective-permute-done.22 = f32[4516]{0:T(1024)S(1)} collective-permute-done((f32[4516]{0:T(1024)S(1)}, f32[4516]{0:T(1024)S(1)}, u32[]{:S(2)}, u32[]{:S(2)}) %collective-permute-start.22) | collective-permute-done | bytes 18096 | tf_op jit(solution)/shard_map/ppermute | solution.py:400
  169.3 2.5 %collective-permute-start.29 = (bf16[128,512]{1,0:T(8,128)(2,1)}, bf16[128,512]{1,0:T(8,128)(2,1)S(1)}, u32[]{:S(2)}, u32[]{:S(2)}) collective-permute-start(bf16[128,512]{1,0:T(8,128)(2,1)} %get-tuple-element.140), channel_id=1, source_target_pairs={{0,12},{4,8},{8,4},{12,0},{16,28},{20,24},{24,20},{28,16},{1,13},{... | collective-permute-start | bytes 393224 | tf_op jit(solution)/shard_map/ppermute | solution.py:485
  173.9 3.1 %split.6 = (bf16[256,512]{1,0:T(8,128)(2,1)}, bf16[256,512]{1,0:T(8,128)(2,1)}, bf16[256,512]{1,0:T(8,128)(2,1)}, bf16[256,512]{1,0:T(8,128)(2,1)}) custom-call(s32[1]{0:T(128)} %bitcast.23.digit_ref, bf16[1024,512]{1,0:T(8,128)(2,1)} %get-tuple-element.145.refs_0_, bf16[1024,512]{1,0:T(8,128)(2,1)} %copy-done.7, bf16[1024,512]{1,0:T(8,128)(2,1)} %copy-done.6), custom_call_target="tpu_custom_call" | custom-call | tf_op jit(solution)/shard_map/split/pallas_call | solution.py:227
  177.0 1.5 collective-permute-start.38
  179.0 1.5 collective-permute-start.40
  182.5 1.8 split.5
  184.3 2.6 %collective-permute-start.30 = (bf16[64,512]{1,0:T(8,128)(2,1)}, bf16[64,512]{1,0:T(8,128)(2,1)S(1)}, u32[]{:S(2)}, u32[]{:S(2)}) collective-permute-start(bf16[64,512]{1,0:T(8,128)(2,1)} %get-tuple-element.142), channel_id=1, source_target_pairs={{0,16},{4,20},{8,24},{12,28},{16,0},{20,4},{24,8},{28,12},{1,17},{... | collective-permute-start | bytes 196616 | tf_op jit(solution)/shard_map/ppermute | solution.py:485
  186.8 6.6 %shard_map.285 = bf16[1024,512]{1,0:T(8,128)(2,1)} custom-call(f32[1024,512]{1,0:T(8,128)} %get-tuple-element.90.refs_0_, bf16[1024,512]{1,0:T(8,128)(2,1)} %get-tuple-element.92.refs_1_, bf16[1024,512]{1,0:T(8,128)(2,1)} %get-tuple-element.93.refs_2_, bf16[1024,512]{1,0:T(8,128)(2,1)} %get-tuple-element.94.refs_3_, ...), custom_call_target="tpu_custom_call" | custom-call | flops 2147483648 | bytes 6291456 | tf_op jit(solution)/shard_map/pallas_call | solution.py:279
  193.5 1.2 slice.79
  196.3 2.1 split.7
  198.3 2.6 %collective-permute-start.41 = (bf16[128,512]{1,0:T(8,128)(2,1)}, bf16[128,512]{1,0:T(8,128)(2,1)S(1)}, u32[]{:S(2)}, u32[]{:S(2)}) collective-permute-start(bf16[128,512]{1,0:T(8,128)(2,1)} %get-tuple-element.154), channel_id=1, source_target_pairs={{0,16},{4,20},{8,24},{12,28},{16,0},{20,4},{24,8},{28,12},{1,17},{... | collective-permute-start | bytes 393224 | tf_op jit(solution)/shard_map/ppermute | solution.py:485
  201.4 6.5 %collective-permute-done.41 = bf16[128,512]{1,0:T(8,128)(2,1)S(1)} collective-permute-done((bf16[128,512]{1,0:T(8,128)(2,1)}, bf16[128,512]{1,0:T(8,128)(2,1)S(1)}, u32[]{:S(2)}, u32[]{:S(2)}) %collective-permute-start.41) | collective-permute-done | bytes 131104 | tf_op jit(solution)/shard_map/ppermute | solution.py:485
  207.9 0.9 add_convert_fusion.refs_0_
  208.9 1.1 broadcast_select_fusion
  210.1 1.1 reshape.216
  211.9 1.5 merge.4.refs_0_
  213.4 6.6 %collective-permute-start.34 = (bf16[128,512]{1,0:T(8,128)(2,1)}, bf16[128,512]{1,0:T(8,128)(2,1)S(1)}, u32[]{:S(2)}, u32[]{:S(2)}) collective-permute-start(bf16[128,512]{1,0:T(8,128)(2,1)} %merge.4.refs_0_), channel_id=1, source_target_pairs={{0,12},{4,8},{8,4},{12,0},{16,28},{20,24},{24,20},{28,16},{1,13},{... | collective-permute-start | bytes 393224 | tf_op jit(solution)/shard_map/ppermute | solution.py:485
  220.6 1.7 merge.6.refs_0_
  222.3 2.0 collective-permute-start.44
  224.3 1.5 collective-permute-start.43
  228.5 4.8 %collective-permute-done.33.refs_2_ = bf16[128,512]{1,0:T(8,128)(2,1)S(1)} collective-permute-done((bf16[128,512]{1,0:T(8,128)(2,1)}, bf16[128,512]{1,0:T(8,128)(2,1)S(1)}, u32[]{:S(2)}, u32[]{:S(2)}) %collective-permute-start.33) | collective-permute-done | bytes 131104 | tf_op jit(solution)/shard_map/ppermute | solution.py:485
  233.3 0.9 collective-permute-done.32.refs_1_
  234.9 2.2 merge.5
  238.6 3.0 %merge.7 = (f32[512,512]{1,0:T(8,128)}, f32[512,512]{1,0:T(8,128)}) custom-call(s32[1]{0:T(128)} %bitcast.23.digit_ref, bf16[256,512]{1,0:T(8,128)(2,1)} %merge.6.refs_0_, bf16[256,512]{1,0:T(8,128)(2,1)} %copy-done.24, bf16[256,512]{1,0:T(8,128)(2,1)} %copy-done.23, bf16[256,512]{1,0:T(8,128)(2,1)} %copy-done.22), custom_call_target="tpu_custom_call" | custom-call | tf_op jit(solution)/shard_map/merge/pallas_call | solution.py:260
  (226 shorter events, 26.6 us)
Async XLA Ops:
  0.7 10.9 %copy-start.2 = (bf16[784,512]{1,0:T(8,128)(2,1)S(1)}, bf16[784,512]{1,0:T(8,128)(2,1)}, u32[]{:S(2)}) copy-start(bf16[784,512]{1,0:T(8,128)(2,1)} %param.17) | copy-start | bytes 2408452
  1.5 10.8 %copy-start.40 = (f32[1,768]{1,0:T(1,128)}, f32[1,768]{1,0:T(1,128)S(1)}, u32[]{:S(2)}) copy-start(f32[1,768]{1,0:T(1,128)S(1)} %reshape.197.vec_ref) | copy-start | bytes 9220
  1.5 10.8 %collective-permute-start.4 = (f32[1,768]{1,0:T(1,128)S(1)}, f32[1,768]{1,0:T(1,128)S(1)}, u32[]{:S(2)}, u32[]{:S(2)}) collective-permute-start(f32[1,768]{1,0:T(1,128)S(1)} %reshape.197.vec_ref), channel_id=1, source_target_pairs={{0,2},{1,3},{2,0},{3,1},{4,6},{5,7},{6,4},{7,5},{8,10},{9,11},{10,... | collective-permute-start | bytes 9224 | tf_op jit(solution)/shard_map/ppermute | solution.py:400
  4.5 7.8 %collective-permute-start.1 = (f32[1,768]{1,0:T(1,128)S(1)}, f32[1,768]{1,0:T(1,128)S(1)}, u32[]{:S(2)}, u32[]{:S(2)}) collective-permute-start(f32[1,768]{1,0:T(1,128)S(1)} %reshape.197.vec_ref), channel_id=1, source_target_pairs={{0,1},{1,0},{2,3},{3,2},{4,5},{5,4},{6,7},{7,6},{8,9},{9,8},{10,11... | collective-permute-start | bytes 9224 | tf_op jit(solution)/shard_map/ppermute | solution.py:400
  6.0 16.8 %copy-start.43 = (f32[512]{0:T(512)S(1)}, f32[512]{0:T(512)}, u32[]{:S(2)}) copy-start(f32[512]{0:T(512)} %param.22) | copy-start | bytes 6148
  6.0 16.8 %copy-start.44 = (f32[512]{0:T(512)S(1)}, f32[512]{0:T(512)}, u32[]{:S(2)}) copy-start(f32[512]{0:T(512)} %param.21) | copy-start | bytes 6148
  9.3 13.9 %copy-start.17 = (f32[64,256]{1,0:T(8,128)}, f32[64,256]{1,0:T(8,128)S(1)}, u32[]{:S(2)}) copy-start(f32[64,256]{1,0:T(8,128)S(1)} %reshape.198.bias_ref) | copy-start | bytes 196612
  9.3 5.2 %collective-permute-start.5 = (f32[64,256]{1,0:T(8,128)S(1)}, f32[64,256]{1,0:T(8,128)S(1)}, u32[]{:S(2)}, u32[]{:S(2)}) collective-permute-start(f32[64,256]{1,0:T(8,128)S(1)} %reshape.198.bias_ref), channel_id=1, source_target_pairs={{0,2},{1,3},{2,0},{3,1},{4,6},{5,7},{6,4},{7,5},{8,10},{9,11},{10,... | collective-permute-start | bytes 196616 | tf_op jit(solution)/shard_map/ppermute | solution.py:400
  9.4 5.0 %collective-permute-start.2 = (f32[64,256]{1,0:T(8,128)S(1)}, f32[64,256]{1,0:T(8,128)S(1)}, u32[]{:S(2)}, u32[]{:S(2)}) collective-permute-start(f32[64,256]{1,0:T(8,128)S(1)} %reshape.198.bias_ref), channel_id=1, source_target_pairs={{0,1},{1,0},{2,3},{3,2},{4,5},{5,4},{6,7},{7,6},{8,9},{9,8},{10,11... | collective-permute-start | bytes 196616 | tf_op jit(solution)/shard_map/ppermute | solution.py:400
  9.9 12.9 %collective-permute-start.3 = (bf16[3,512,128]{2,1,0:T(8,128)(2,1)S(1)}, bf16[3,512,128]{2,1,0:T(8,128)(2,1)}, u32[]{:S(2)}, u32[]{:S(2)}) collective-permute-start(bf16[3,512,128]{2,1,0:T(8,128)(2,1)S(1)} %copy-done.3), channel_id=1, source_target_pairs={{0,2},{1,3},{2,0},{3,1},{4,6},{5,7},{6,4},{7,5},{8,10},{9,11},{10,... | collective-permute-start | bytes 1179656 | tf_op jit(solution)/shard_map/ppermute | solution.py:400
  12.3 15.3 %copy-start.46 = (f32[1,768]{1,0:T(1,128)}, f32[1,768]{1,0:T(1,128)S(1)}, u32[]{:S(2)}) copy-start(f32[1,768]{1,0:T(1,128)S(1)} %collective-permute-done.4.vec_ref) | copy-start | bytes 9220
  12.3 13.5 %collective-permute-start = (bf16[3,512,128]{2,1,0:T(8,128)(2,1)S(1)}, bf16[3,512,128]{2,1,0:T(8,128)(2,1)S(1)}, u32[]{:S(2)}, u32[]{:S(2)}) collective-permute-start(bf16[3,512,128]{2,1,0:T(8,128)(2,1)S(1)} %copy-done.3), channel_id=1, source_target_pairs={{0,1},{1,0},{2,3},{3,2},{4,5},{5,4},{6,7},{7,6},{8,9},{9,8},{10,11... | collective-permute-start | bytes 1179656 | tf_op jit(solution)/shard_map/ppermute | solution.py:400
  12.4 15.2 %copy-start.47 = (f32[1,768]{1,0:T(1,128)}, f32[1,768]{1,0:T(1,128)S(1)}, u32[]{:S(2)}) copy-start(f32[1,768]{1,0:T(1,128)S(1)} %collective-permute-done.1.vec_ref) | copy-start | bytes 9220
  12.4 1.7 collective-permute-start.7
  14.1 13.5 %copy-start.48 = (f32[1,768]{1,0:T(1,128)}, f32[1,768]{1,0:T(1,128)S(1)}, u32[]{:S(2)}) copy-start(f32[1,768]{1,0:T(1,128)S(1)} %collective-permute-done.7.vec_ref) | copy-start | bytes 9220
  14.1 11.1 %collective-permute-start.10 = (bf16[128,512]{1,0:T(8,128)(2,1)S(1)}, bf16[128,512]{1,0:T(8,128)(2,1)}, u32[]{:S(2)}, u32[]{:S(2)}) collective-permute-start(bf16[128,512]{1,0:T(8,128)(2,1)S(1)} %copy-done.13), channel_id=1, source_target_pairs={{0,2},{1,3},{2,0},{3,1},{4,6},{5,7},{6,4},{7,5},{8,10},{9,11},{10,... | collective-permute-start | bytes 393224 | tf_op jit(solution)/shard_map/ppermute | solution.py:400
  14.4 13.2 %copy-start.33 = (f32[64,256]{1,0:T(8,128)}, f32[64,256]{1,0:T(8,128)S(1)}, u32[]{:S(2)}) copy-start(f32[64,256]{1,0:T(8,128)S(1)} %collective-permute-done.5.bias_ref) | copy-start | bytes 196612
  14.4 11.4 %collective-permute-start.9 = (bf16[128,512]{1,0:T(8,128)(2,1)S(1)}, bf16[128,512]{1,0:T(8,128)(2,1)S(1)}, u32[]{:S(2)}, u32[]{:S(2)}) collective-permute-start(bf16[128,512]{1,0:T(8,128)(2,1)S(1)} %copy-done.13), channel_id=1, source_target_pairs={{0,1},{1,0},{2,3},{3,2},{4,5},{5,4},{6,7},{7,6},{8,9},{9,8},{10,11... | collective-permute-start | bytes 393224 | tf_op jit(solution)/shard_map/ppermute | solution.py:400
  14.5 13.2 %copy-start.32 = (f32[64,256]{1,0:T(8,128)}, f32[64,256]{1,0:T(8,128)S(1)}, u32[]{:S(2)}) copy-start(f32[64,256]{1,0:T(8,128)S(1)} %collective-permute-done.2.bias_ref) | copy-start | bytes 196612
  14.5 9.4 %collective-permute-start.8 = (f32[64,256]{1,0:T(8,128)S(1)}, f32[64,256]{1,0:T(8,128)S(1)}, u32[]{:S(2)}, u32[]{:S(2)}) collective-permute-start(f32[64,256]{1,0:T(8,128)S(1)} %collective-permute-done.5.bias_ref), channel_id=1, source_target_pairs={{0,1},{1,0},{2,3},{3,2},{4,5},{5,4},{6,7},{7,6},{8,9},{9,8},{10,11... | collective-permute-start | bytes 196616 | tf_op jit(solution)/shard_map/ppermute | solution.py:400
  22.8 6.4 %collective-permute-start.6 = (bf16[3,512,128]{2,1,0:T(8,128)(2,1)}, bf16[3,512,128]{2,1,0:T(8,128)(2,1)}, u32[]{:S(2)}, u32[]{:S(2)}) collective-permute-start(bf16[3,512,128]{2,1,0:T(8,128)(2,1)} %collective-permute-done.3.w_ref.refs_10_), channel_id=1, source_target_pairs={{0,1},{1,0},{2,3},{3,2},{4,5},{5,4},{6,7},{7,6},{8,9},{9,8},{10,11... | collective-permute-start | bytes 1179656 | tf_op jit(solution)/shard_map/ppermute | solution.py:400
  23.9 11.0 %copy-start.34 = (f32[64,256]{1,0:T(8,128)}, f32[64,256]{1,0:T(8,128)S(1)}, u32[]{:S(2)}) copy-start(f32[64,256]{1,0:T(8,128)S(1)} %collective-permute-done.8.bias_ref) | copy-start | bytes 196612
  23.9 34.8 %collective-permute-start.12 = (bf16[512,512]{1,0:T(8,128)(2,1)}, bf16[512,512]{1,0:T(8,128)(2,1)}, u32[]{:S(2)}, u32[]{:S(2)}) collective-permute-start(bf16[512,512]{1,0:T(8,128)(2,1)} %refs_8_.4), channel_id=1, source_target_pairs={{0,1},{1,0},{2,3},{3,2},{4,5},{5,4},{6,7},{7,6},{8,9},{9,8},{10,11... | collective-permute-start | bytes 1572872 | tf_op jit(solution)/shard_map/ppermute | solution.py:400
  25.2 27.9 %collective-permute-start.14 = (bf16[512,512]{1,0:T(8,128)(2,1)}, bf16[512,512]{1,0:T(8,128)(2,1)}, u32[]{:S(2)}, u32[]{:S(2)}) collective-permute-start(bf16[512,512]{1,0:T(8,128)(2,1)} %refs_8_.4), channel_id=1, source_target_pairs={{0,2},{1,3},{2,0},{3,1},{4,6},{5,7},{6,4},{7,5},{8,10},{9,11},{10,... | collective-permute-start | bytes 1572872 | tf_op jit(solution)/shard_map/ppermute | solution.py:400
  25.8 32.9 %collective-permute-start.13 = (bf16[512,512]{1,0:T(8,128)(2,1)}, bf16[512,512]{1,0:T(8,128)(2,1)}, u32[]{:S(2)}, u32[]{:S(2)}) collective-permute-start(bf16[512,512]{1,0:T(8,128)(2,1)} %refs_6_.1), channel_id=1, source_target_pairs={{0,1},{1,0},{2,3},{3,2},{4,5},{5,4},{6,7},{7,6},{8,9},{9,8},{10,11... | collective-permute-start | bytes 1572872 | tf_op jit(solution)/shard_map/ppermute | solution.py:400
  25.8 27.6 %collective-permute-start.15 = (bf16[512,512]{1,0:T(8,128)(2,1)}, bf16[512,512]{1,0:T(8,128)(2,1)}, u32[]{:S(2)}, u32[]{:S(2)}) collective-permute-start(bf16[512,512]{1,0:T(8,128)(2,1)} %refs_6_.1), channel_id=1, source_target_pairs={{0,2},{1,3},{2,0},{3,1},{4,6},{5,7},{6,4},{7,5},{8,10},{9,11},{10,... | collective-permute-start | bytes 1572872 | tf_op jit(solution)/shard_map/ppermute | solution.py:400
  29.2 24.3 %collective-permute-start.11 = (bf16[128,512]{1,0:T(8,128)(2,1)}, bf16[128,512]{1,0:T(8,128)(2,1)}, u32[]{:S(2)}, u32[]{:S(2)}) collective-permute-start(bf16[128,512]{1,0:T(8,128)(2,1)} %collective-permute-done.10.refs_10_.wp_ref), channel_id=1, source_target_pairs={{0,1},{1,0},{2,3},{3,2},{4,5},{5,4},{6,7},{7,6},{8,9},{9,8},{10,11... | collective-permute-start | bytes 393224 | tf_op jit(solution)/shard_map/ppermute | solution.py:400
  53.1 27.3 %collective-permute-start.16 = (bf16[512,512]{1,0:T(8,128)(2,1)}, bf16[512,512]{1,0:T(8,128)(2,1)S(1)}, u32[]{:S(2)}, u32[]{:S(2)}) collective-permute-start(bf16[512,512]{1,0:T(8,128)(2,1)} %collective-permute-done.14.w1_ref.refs_10_), channel_id=1, source_target_pairs={{0,1},{1,0},{2,3},{3,2},{4,5},{5,4},{6,7},{7,6},{8,9},{9,8},{10,11... | collective-permute-start | bytes 1572872 | tf_op jit(solution)/shard_map/ppermute | solution.py:400
  53.4 27.0 %collective-permute-start.17 = (bf16[512,512]{1,0:T(8,128)(2,1)}, bf16[512,512]{1,0:T(8,128)(2,1)S(1)}, u32[]{:S(2)}, u32[]{:S(2)}) collective-permute-start(bf16[512,512]{1,0:T(8,128)(2,1)} %collective-permute-done.15.w2_ref.refs_8_), channel_id=1, source_target_pairs={{0,1},{1,0},{2,3},{3,2},{4,5},{5,4},{6,7},{7,6},{8,9},{9,8},{10,11... | collective-permute-start | bytes 1572872 | tf_op jit(solution)/shard_map/ppermute | solution.py:400
  65.7 106.7 %collective-permute-start.37 = (bf16[1024,512]{1,0:T(8,128)(2,1)}, bf16[1024,512]{1,0:T(8,128)(2,1)S(1)}, u32[]{:S(2)}, u32[]{:S(2)}) collective-permute-start(bf16[1024,512]{1,0:T(8,128)(2,1)} %get-tuple-element.148), channel_id=1, source_target_pairs={{0,1},{1,0},{2,3},{3,2},{4,5},{5,4},{6,7},{7,6},{8,9},{9,8},{10,11... | collective-permute-start | bytes 3145736 | tf_op jit(solution)/shard_map/ppermute | solution.py:400
  89.0 44.9 %collective-permute-start.35 = (bf16[1024,512]{1,0:T(8,128)(2,1)}, bf16[1024,512]{1,0:T(8,128)(2,1)S(1)}, u32[]{:S(2)}, u32[]{:S(2)}) collective-permute-start(bf16[1024,512]{1,0:T(8,128)(2,1)} %get-tuple-element.147), channel_id=1, source_target_pairs={{0,1},{1,0},{2,3},{3,2},{4,5},{5,4},{6,7},{7,6},{8,9},{9,8},{10,11... | collective-permute-start | bytes 3145736 | tf_op jit(solution)/shard_map/ppermute | solution.py:400
  103.6 28.3 %collective-permute-start.18 = (bf16[512,512]{1,0:T(8,128)(2,1)}, bf16[512,512]{1,0:T(8,128)(2,1)S(1)}, u32[]{:S(2)}, u32[]{:S(2)}) collective-permute-start(bf16[512,512]{1,0:T(8,128)(2,1)} %get-tuple-element.121), channel_id=1, source_target_pairs={{0,1},{1,0},{2,3},{3,2},{4,5},{5,4},{6,7},{7,6},{8,9},{9,8},{10,11... | collective-permute-start | bytes 1572872 | tf_op jit(solution)/shard_map/ppermute | solution.py:400
  110.4 25.0 %collective-permute-start.20 = (bf16[512,512]{1,0:T(8,128)(2,1)}, bf16[512,512]{1,0:T(8,128)(2,1)}, u32[]{:S(2)}, u32[]{:S(2)}) collective-permute-start(bf16[512,512]{1,0:T(8,128)(2,1)} %get-tuple-element.122), channel_id=1, source_target_pairs={{0,1},{1,0},{2,3},{3,2},{4,5},{5,4},{6,7},{7,6},{8,9},{9,8},{10,11... | collective-permute-start | bytes 1572872 | tf_op jit(solution)/shard_map/ppermute | solution.py:400
  123.3 9.9 %copy-start.49 = (f32[1,512]{1,0:T(1,128)S(1)}, f32[1,512]{1,0:T(1,128)}, u32[]{:S(2)}) copy-start(f32[1,512]{1,0:T(1,128)} %get-tuple-element.133) | copy-start | bytes 6148
  123.3 9.9 %copy-start.50 = (f32[1,512]{1,0:T(1,128)S(1)}, f32[1,512]{1,0:T(1,128)}, u32[]{:S(2)}) copy-start(f32[1,512]{1,0:T(1,128)} %get-tuple-element.132) | copy-start | bytes 6148
  132.1 14.9 %collective-permute-start.19 = (bf16[512,512]{1,0:T(8,128)(2,1)S(1)}, bf16[512,512]{1,0:T(8,128)(2,1)S(1)}, u32[]{:S(2)}, u32[]{:S(2)}) collective-permute-start(bf16[512,512]{1,0:T(8,128)(2,1)S(1)} %add.90), channel_id=1, source_target_pairs={{0,2},{1,3},{2,0},{3,1},{4,6},{5,7},{6,4},{7,5},{8,10},{9,11},{10,... | collective-permute-start | bytes 1572872 | tf_op jit(solution)/shard_map/ppermute | solution.py:400
  134.2 15.8 %copy-start.36 = (f32[64,256]{1,0:T(8,128)S(1)}, f32[64,256]{1,0:T(8,128)}, u32[]{:S(2)}) copy-start(f32[64,256]{1,0:T(8,128)} %get-tuple-element.124) | copy-start | bytes 196612
  134.2 15.9 %copy-start.35 = (f32[64,256]{1,0:T(8,128)S(1)}, f32[64,256]{1,0:T(8,128)}, u32[]{:S(2)}) copy-start(f32[64,256]{1,0:T(8,128)} %get-tuple-element.125) | copy-start | bytes 196612
  134.2 38.7 %collective-permute-start.36 = (bf16[1024,512]{1,0:T(8,128)(2,1)S(1)}, bf16[1024,512]{1,0:T(8,128)(2,1)S(1)}, u32[]{:S(2)}, u32[]{:S(2)}) collective-permute-start(bf16[1024,512]{1,0:T(8,128)(2,1)S(1)} %add.99), channel_id=1, source_target_pairs={{0,2},{1,3},{2,0},{3,1},{4,6},{5,7},{6,4},{7,5},{8,10},{9,11},{10,... | collective-permute-start | bytes 3145736 | tf_op jit(solution)/shard_map/ppermute | solution.py:400
  158.2 1.3 collective-permute-start.21
  158.3 3.7 %collective-permute-start.23 = (f32[4516]{0:T(1024)S(1)}, f32[4516]{0:T(1024)S(1)}, u32[]{:S(2)}, u32[]{:S(2)}) collective-permute-start(f32[4516]{0:T(1024)S(1)} %get-tuple-element.173), channel_id=1, source_target_pairs={{0,1},{1,0},{2,3},{3,2},{4,5},{5,4},{6,7},{7,6},{8,9},{9,8},{10,11... | collective-permute-start | bytes 54200 | tf_op jit(solution)/shard_map/ppermute | solution.py:400
  159.5 9.8 %collective-permute-start.22 = (f32[4516]{0:T(1024)S(1)}, f32[4516]{0:T(1024)S(1)}, u32[]{:S(2)}, u32[]{:S(2)}) collective-permute-start(f32[4516]{0:T(1024)S(1)} %add.91), channel_id=1, source_target_pairs={{0,2},{1,3},{2,0},{3,1},{4,6},{5,7},{6,4},{7,5},{8,10},{9,11},{10,... | collective-permute-start | bytes 54200 | tf_op jit(solution)/shard_map/ppermute | solution.py:400
  160.5 18.5 %collective-permute-start.27 = (bf16[128,512]{1,0:T(8,128)(2,1)}, bf16[128,512]{1,0:T(8,128)(2,1)S(1)}, u32[]{:S(2)}, u32[]{:S(2)}) collective-permute-start(bf16[128,512]{1,0:T(8,128)(2,1)} %get-tuple-element.138), channel_id=1, source_target_pairs={{0,4},{4,0},{8,12},{12,8},{16,20},{20,16},{24,28},{28,24},{1,5},{5... | collective-permute-start | bytes 393224 | tf_op jit(solution)/shard_map/ppermute | solution.py:485
  162.0 19.3 %collective-permute-start.28 = (bf16[128,512]{1,0:T(8,128)(2,1)}, bf16[128,512]{1,0:T(8,128)(2,1)S(1)}, u32[]{:S(2)}, u32[]{:S(2)}) collective-permute-start(bf16[128,512]{1,0:T(8,128)(2,1)} %get-tuple-element.139), channel_id=1, source_target_pairs={{0,8},{4,12},{8,0},{12,4},{16,24},{20,28},{24,16},{28,20},{1,9},{5... | collective-permute-start | bytes 393224 | tf_op jit(solution)/shard_map/ppermute | solution.py:485
  169.3 12.5 %collective-permute-start.29 = (bf16[128,512]{1,0:T(8,128)(2,1)}, bf16[128,512]{1,0:T(8,128)(2,1)S(1)}, u32[]{:S(2)}, u32[]{:S(2)}) collective-permute-start(bf16[128,512]{1,0:T(8,128)(2,1)} %get-tuple-element.140), channel_id=1, source_target_pairs={{0,12},{4,8},{8,4},{12,0},{16,28},{20,24},{24,20},{28,16},{1,13},{... | collective-permute-start | bytes 393224 | tf_op jit(solution)/shard_map/ppermute | solution.py:485
  172.4 6.1 %collective-permute-start.24 = (f32[4516]{0:T(1024)}, f32[4516]{0:T(1024)}, u32[]{:S(2)}, u32[]{:S(2)}) collective-permute-start(f32[4516]{0:T(1024)} %add_add_fusion), channel_id=1, source_target_pairs={{0,4},{4,0},{8,12},{12,8},{16,20},{20,16},{24,28},{28,24},{1,5},{5... | collective-permute-start | bytes 54200 | tf_op jit(solution)/shard_map/ppermute | solution.py:485
  177.0 18.4 %collective-permute-start.38 = (bf16[256,512]{1,0:T(8,128)(2,1)}, bf16[256,512]{1,0:T(8,128)(2,1)S(1)}, u32[]{:S(2)}, u32[]{:S(2)}) collective-permute-start(bf16[256,512]{1,0:T(8,128)(2,1)} %get-tuple-element.150), channel_id=1, source_target_pairs={{0,4},{4,0},{8,12},{12,8},{16,20},{20,16},{24,28},{28,24},{1,5},{5... | collective-permute-start | bytes 786440 | tf_op jit(solution)/shard_map/ppermute | solution.py:485
  178.6 16.9 %collective-permute-start.39 = (bf16[256,512]{1,0:T(8,128)(2,1)}, bf16[256,512]{1,0:T(8,128)(2,1)S(1)}, u32[]{:S(2)}, u32[]{:S(2)}) collective-permute-start(bf16[256,512]{1,0:T(8,128)(2,1)} %get-tuple-element.151), channel_id=1, source_target_pairs={{0,8},{4,12},{8,0},{12,4},{16,24},{20,28},{24,16},{28,20},{1,9},{5... | collective-permute-start | bytes 786440 | tf_op jit(solution)/shard_map/ppermute | solution.py:485
  179.0 16.4 %collective-permute-start.40 = (bf16[256,512]{1,0:T(8,128)(2,1)}, bf16[256,512]{1,0:T(8,128)(2,1)S(1)}, u32[]{:S(2)}, u32[]{:S(2)}) collective-permute-start(bf16[256,512]{1,0:T(8,128)(2,1)} %get-tuple-element.152), channel_id=1, source_target_pairs={{0,12},{4,8},{8,4},{12,0},{16,28},{20,24},{24,20},{28,16},{1,13},{... | collective-permute-start | bytes 786440 | tf_op jit(solution)/shard_map/ppermute | solution.py:485
  181.3 13.7 %collective-permute-start.25 = (f32[4516]{0:T(1024)S(1)}, f32[4516]{0:T(1024)S(1)}, u32[]{:S(2)}, u32[]{:S(2)}) collective-permute-start(f32[4516]{0:T(1024)S(1)} %add.94), channel_id=1, source_target_pairs={{0,8},{4,12},{8,0},{12,4},{16,24},{20,28},{24,16},{28,20},{1,9},{5... | collective-permute-start | bytes 54200 | tf_op jit(solution)/shard_map/ppermute | solution.py:485
  184.3 16.7 %collective-permute-start.30 = (bf16[64,512]{1,0:T(8,128)(2,1)}, bf16[64,512]{1,0:T(8,128)(2,1)S(1)}, u32[]{:S(2)}, u32[]{:S(2)}) collective-permute-start(bf16[64,512]{1,0:T(8,128)(2,1)} %get-tuple-element.142), channel_id=1, source_target_pairs={{0,16},{4,20},{8,24},{12,28},{16,0},{20,4},{24,8},{28,12},{1,17},{... | collective-permute-start | bytes 196616 | tf_op jit(solution)/shard_map/ppermute | solution.py:485
  194.7 14.2 %copy-start.42 = (pred[784]{0:T(1024)(128)(4,1)S(1)}, pred[784]{0:T(1024)(128)(4,1)}, u32[]{:S(2)}) copy-start(pred[784]{0:T(1024)(128)(4,1)} %copy-done.41) | copy-start | bytes 2356
  195.0 16.2 %collective-permute-start.26 = (f32[4516]{0:T(1024)S(1)}, f32[4516]{0:T(1024)S(1)}, u32[]{:S(2)}, u32[]{:S(2)}) collective-permute-start(f32[4516]{0:T(1024)S(1)} %add.95), channel_id=1, source_target_pairs={{0,16},{4,20},{8,24},{12,28},{16,0},{20,4},{24,8},{28,12},{1,17},{... | collective-permute-start | bytes 54200 | tf_op jit(solution)/shard_map/ppermute | solution.py:485
  196.3 13.7 %copy-start.8 = (bf16[1024,512]{1,0:T(8,128)(2,1)S(1)}, bf16[1024,512]{1,0:T(8,128)(2,1)}, u32[]{:S(2)}) copy-start(bf16[1024,512]{1,0:T(8,128)(2,1)} %get-tuple-element.114) | copy-start | bytes 3145732
  198.3 9.5 %collective-permute-start.41 = (bf16[128,512]{1,0:T(8,128)(2,1)}, bf16[128,512]{1,0:T(8,128)(2,1)S(1)}, u32[]{:S(2)}, u32[]{:S(2)}) collective-permute-start(bf16[128,512]{1,0:T(8,128)(2,1)} %get-tuple-element.154), channel_id=1, source_target_pairs={{0,16},{4,20},{8,24},{12,28},{16,0},{20,4},{24,8},{28,12},{1,17},{... | collective-permute-start | bytes 393224 | tf_op jit(solution)/shard_map/ppermute | solution.py:485
  201.0 10.3 %collective-permute-start.31 = (bf16[64,512]{1,0:T(8,128)(2,1)S(1)}, bf16[64,512]{1,0:T(8,128)(2,1)S(1)}, u32[]{:S(2)}, u32[]{:S(2)}) collective-permute-start(bf16[64,512]{1,0:T(8,128)(2,1)S(1)} %add_convert_fusion.1.refs_0_), channel_id=1, source_target_pairs={{0,16},{4,20},{8,24},{12,28},{16,0},{20,4},{24,8},{28,12},{1,17},{... | collective-permute-start | bytes 196616 | tf_op jit(solution)/shard_map/ppermute | solution.py:485
  208.8 11.2 %collective-permute-start.42 = (bf16[128,512]{1,0:T(8,128)(2,1)S(1)}, bf16[128,512]{1,0:T(8,128)(2,1)S(1)}, u32[]{:S(2)}, u32[]{:S(2)}) collective-permute-start(bf16[128,512]{1,0:T(8,128)(2,1)S(1)} %add_convert_fusion.refs_0_), channel_id=1, source_target_pairs={{0,16},{4,20},{8,24},{12,28},{16,0},{20,4},{24,8},{28,12},{1,17},{... | collective-permute-start | bytes 393224 | tf_op jit(solution)/shard_map/ppermute | solution.py:485
  210.1 31.5 %copy-start.1 = (f32[169,4]{0,1:T(4,128)S(1)}, f32[169,4]{0,1:T(4,128)}, u32[]{:S(2)}) copy-start(f32[169,4]{0,1:T(4,128)} %param.20) | copy-start | bytes 8116
  213.4 13.9 %collective-permute-start.34 = (bf16[128,512]{1,0:T(8,128)(2,1)}, bf16[128,512]{1,0:T(8,128)(2,1)S(1)}, u32[]{:S(2)}, u32[]{:S(2)}) collective-permute-start(bf16[128,512]{1,0:T(8,128)(2,1)} %merge.4.refs_0_), channel_id=1, source_target_pairs={{0,12},{4,8},{8,4},{12,0},{16,28},{20,24},{24,20},{28,16},{1,13},{... | collective-permute-start | bytes 393224 | tf_op jit(solution)/shard_map/ppermute | solution.py:485
  222.3 14.7 %collective-permute-start.45 = (bf16[256,512]{1,0:T(8,128)(2,1)}, bf16[256,512]{1,0:T(8,128)(2,1)S(1)}, u32[]{:S(2)}, u32[]{:S(2)}) collective-permute-start(bf16[256,512]{1,0:T(8,128)(2,1)} %merge.6.refs_0_), channel_id=1, source_target_pairs={{0,12},{4,8},{8,4},{12,0},{16,28},{20,24},{24,20},{28,16},{1,13},{... | collective-permute-start | bytes 786440 | tf_op jit(solution)/shard_map/ppermute | solution.py:485
  222.3 14.7 %collective-permute-start.44 = (bf16[256,512]{1,0:T(8,128)(2,1)}, bf16[256,512]{1,0:T(8,128)(2,1)S(1)}, u32[]{:S(2)}, u32[]{:S(2)}) collective-permute-start(bf16[256,512]{1,0:T(8,128)(2,1)} %merge.6.refs_0_), channel_id=1, source_target_pairs={{0,8},{4,12},{8,0},{12,4},{16,24},{20,28},{24,16},{28,20},{1,9},{5... | collective-permute-start | bytes 786440 | tf_op jit(solution)/shard_map/ppermute | solution.py:485
  224.3 12.8 %collective-permute-start.43 = (bf16[256,512]{1,0:T(8,128)(2,1)}, bf16[256,512]{1,0:T(8,128)(2,1)S(1)}, u32[]{:S(2)}, u32[]{:S(2)}) collective-permute-start(bf16[256,512]{1,0:T(8,128)(2,1)} %merge.6.refs_0_), channel_id=1, source_target_pairs={{0,4},{4,0},{8,12},{12,8},{16,20},{20,16},{24,28},{28,24},{1,5},{5... | collective-permute-start | bytes 786440 | tf_op jit(solution)/shard_map/ppermute | solution.py:485
  227.3 6.0 %collective-permute-start.33 = (bf16[128,512]{1,0:T(8,128)(2,1)}, bf16[128,512]{1,0:T(8,128)(2,1)S(1)}, u32[]{:S(2)}, u32[]{:S(2)}) collective-permute-start(bf16[128,512]{1,0:T(8,128)(2,1)} %merge.4.refs_0_), channel_id=1, source_target_pairs={{0,8},{4,12},{8,0},{12,4},{16,24},{20,28},{24,16},{28,20},{1,9},{5... | collective-permute-start | bytes 393224 | tf_op jit(solution)/shard_map/ppermute | solution.py:485
  227.3 6.9 %collective-permute-start.32 = (bf16[128,512]{1,0:T(8,128)(2,1)}, bf16[128,512]{1,0:T(8,128)(2,1)S(1)}, u32[]{:S(2)}, u32[]{:S(2)}) collective-permute-start(bf16[128,512]{1,0:T(8,128)(2,1)} %merge.4.refs_0_), channel_id=1, source_target_pairs={{0,4},{4,0},{8,12},{12,8},{16,20},{20,16},{24,28},{28,24},{1,5},{5... | collective-permute-start | bytes 393224 | tf_op jit(solution)/shard_map/ppermute | solution.py:485
  (39 other events, 108.7 us)

commit v3 on v2

--- a/solution.py
+++ b/solution.py
@@ -10,7 +10,10 @@
 
 IMG_TOKENS = 196
 ROW_TILE = 16
-CHUNK = 256
+CHUNK = 512
+VMEM_ATTEND = 24 << 20
+VMEM_ROWS = 24 << 20
+VMEM_MOVE = 16 << 20
 TOGETHER = 4
 FAR_BELOW = -1e30
 
@@ -66,14 +69,15 @@
     return total
 
 
-def each_window(windows, body):
-    together = TOGETHER if windows % TOGETHER == 0 else 1
-
-    def step(i, carry):
-        body([i * together + j for j in range(together)])
-        return carry
-
-    lax.fori_loop(0, windows // together, step, 0)
+def together(windows):
+    return TOGETHER if windows % TOGETHER == 0 else 1
+
+
+def blocks(shape, axis=None, size=None):
+    if axis is None:
+        return pl.BlockSpec(shape, lambda i: (0,) * len(shape))
+    block = shape[:axis] + (size,) + shape[axis + 1 :]
+    return pl.BlockSpec(block, lambda i: tuple(i if a == axis else 0 for a in range(len(shape))))
 
 
 def attend_kernel(heads, scale, xn_ref, w_ref, vec_ref, bias_ref, qkv_ref, p_ref, att_ref):
@@ -100,20 +104,35 @@
             p_ref[w] = x
             att_ref[w] = fold(out, masks).astype(bf16)
 
-    each_window(windows, some)
+    some(range(windows))
 
 
 def attend(xn, w, vec, bias, heads, scale, windows, padded):
     width = w.shape[2]
     lanes = heads * padded
+    step = together(windows)
+    outs = [
+        kept((3, windows, padded, width), bf16),
+        kept((windows, padded, lanes)),
+        kept((windows, padded, width), bf16),
+    ]
     return pl.pallas_call(
         functools.partial(attend_kernel, heads, scale),
-        out_shape=(
-            jax.ShapeDtypeStruct((3, windows, padded, width), bf16),
-            jax.ShapeDtypeStruct((windows, padded, lanes), f32),
-            jax.ShapeDtypeStruct((windows, padded, width), bf16),
-        ),
+        grid=(windows // step,),
+        in_specs=[
+            blocks(xn.shape, 0, step * padded),
+            blocks(w.shape),
+            blocks(vec.shape),
+            blocks(bias.shape),
+        ],
+        out_specs=[
+            blocks(outs[0].shape, 1, step),
+            blocks(outs[1].shape, 0, step),
+            blocks(outs[2].shape, 0, step),
+        ],
+        out_shape=outs,
         name="attend",
+        compiler_params=pltpu.CompilerParams(vmem_limit_bytes=VMEM_ATTEND),
         cost_estimate=pl.CostEstimate(
             flops=2 * xn.size * 3 * width, bytes_accessed=4 * xn.size, transcendentals=0
         ),
@@ -134,12 +153,19 @@
     ds_ref,
     gb_ref,
     datt_ref,
+    all_ref,
 ):
     _, windows, padded, width = qkv_ref.shape
-    dmid = dmid_ref[...]
-    datt_ref[...] = dot(dmid, wp_ref[...], 1, 1).astype(bf16).reshape(windows, padded, width)
-    ds_ref[...] = jnp.zeros_like(ds_ref)
-    gb_ref[...] = jnp.zeros_like(gb_ref)
+    at = pl.program_id(0)
+    rows = pl.ds(pl.multiple_of(at * windows * padded, windows * padded), windows * padded)
+    datt = dot(dmid_ref[rows, :], wp_ref[...], 1, 1)
+    datt_ref[...] = datt.astype(bf16).reshape(windows, padded, width)
+
+    @pl.when(at == 0)
+    def _():
+        ds_ref[...] = jnp.zeros_like(ds_ref)
+        gb_ref[...] = jnp.zeros_like(gb_ref)
+
     masks = head_masks(heads, width)
 
     def some(ws):
@@ -159,28 +185,47 @@
         gb_ref[0:1, :] += jnp.sum(sum(dqs), axis=0, keepdims=True)
         gb_ref[1:2, :] += jnp.sum(sum(dvs), axis=0, keepdims=True)
 
-    each_window(windows, some)
-    dqkv = dqkv_ref[...].reshape(windows * padded, 3 * width)
-    g_ref[:, : 3 * width] = dot(xn_ref[...], dqkv, 0, 0).astype(bf16)
-    g_ref[:, 3 * width :] = dot(dmid, att_ref[...], 0, 0).astype(bf16)
+    some(range(windows))
+    all_ref[rows, :] = dqkv_ref[...].reshape(windows * padded, 3 * width)
+
+    @pl.when(at == pl.num_programs(0) - 1)
+    def _():
+        g_ref[:, : 3 * width] = dot(xn_ref[...], all_ref[...], 0, 0).astype(bf16)
+        g_ref[:, 3 * width :] = dot(dmid_ref[...], att_ref[...], 0, 0).astype(bf16)
 
 
 def attend_back(dmid, xn, wp, qkv, probs, att, heads, scale):
     _, windows, padded, width = qkv.shape
+    step = together(windows)
+    outs = [
+        kept((windows, padded, 3 * width), bf16),
+        shape_of((dmid.shape[1], 4 * width), bf16),
+        shape_of(probs.shape[1:]),
+        shape_of((2, width)),
+    ]
     return pl.pallas_call(
         functools.partial(attend_back_kernel, heads, scale),
-        out_shape=(
-            jax.ShapeDtypeStruct((windows, padded, 3 * width), bf16),
-            jax.ShapeDtypeStruct((dmid.shape[1], 4 * width), bf16),
-            jax.ShapeDtypeStruct(probs.shape[1:], f32),
-            jax.ShapeDtypeStruct((2, width), f32),
-        ),
-        scratch_shapes=[pltpu.VMEM((windows, padded, width), bf16)],
+        grid=(windows // step,),
+        in_specs=[
+            blocks(dmid.shape),
+            blocks(xn.shape),
+            blocks(wp.shape),
+            blocks(qkv.shape, 1, step),
+            blocks(probs.shape, 0, step),
+            blocks(att.shape),
+        ],
+        out_specs=[blocks(outs[0].shape, 0, step)] + [blocks(o.shape) for o in outs[1:]],
+        out_shape=outs,
+        scratch_shapes=[
+            pltpu.VMEM((step, padded, width), bf16),
+            pltpu.VMEM((windows * padded, 3 * width), bf16),
+        ],
         name="attend_back",
+        compiler_params=pltpu.CompilerParams(vmem_limit_bytes=VMEM_ATTEND),
         cost_estimate=pl.CostEstimate(
             flops=2 * dmid.size * 8 * width, bytes_accessed=4 * dmid.size, transcendentals=0
         ),
-    )(dmid, xn, wp, qkv, probs, att)
+    )(dmid, xn, wp, from_hbm(qkv), from_hbm(probs), att)
 
 
 def mlp_kernel(
@@ -230,6 +275,7 @@
         + [pl.BlockSpec(memory_space=pltpu.VMEM)] * len(values),
         out_shape=[shape_of((rows // ways, width), bf16)] * ways,
         name="split",
+        compiler_params=pltpu.CompilerParams(vmem_limit_bytes=VMEM_MOVE),
     )(digit, *values)
 
 
@@ -264,17 +310,18 @@
         out_shape=[shape_of(r) for r in results] if results else shape_of(whole, bf16),
         scratch_shapes=[pltpu.VMEM(whole, f32)] if results else [],
         name="merge",
+        compiler_params=pltpu.CompilerParams(vmem_limit_bytes=VMEM_MOVE),
     )(digit, *pieces)
 
 
-def by_rows(kernel, rows, cut, whole, cut_outs, whole_outs, flops, scratch=()):
-    chunk = CHUNK if rows % CHUNK == 0 else rows
+def by_rows(kernel, rows, cut, whole, cut_outs, whole_outs, flops, scratch=(), chunk=CHUNK):
+    chunk = chunk if rows % chunk == 0 else rows
 
     def cut_spec(value):
-        return pl.BlockSpec((chunk,) + value.shape[1:], lambda i: (i,) + (0,) * (value.ndim - 1))
+        return pl.BlockSpec((chunk,) + value.shape[1:], lambda i: (i,) + (0,) * (len(value.shape) - 1))
 
     def whole_spec(value):
-        return pl.BlockSpec(value.shape, lambda i: (0,) * value.ndim)
+        return pl.BlockSpec(value.shape, lambda i: (0,) * len(value.shape))
 
     return pl.pallas_call(
         kernel,
@@ -283,6 +330,7 @@
         out_specs=[cut_spec(v) for v in cut_outs] + [whole_spec(v) for v in whole_outs],
         out_shape=list(cut_outs) + list(whole_outs),
         scratch_shapes=list(scratch),
+        compiler_params=pltpu.CompilerParams(vmem_limit_bytes=VMEM_ROWS),
         cost_estimate=pl.CostEstimate(
             flops=flops,
             bytes_accessed=sum(v.size * v.dtype.itemsize for v in cut),
@@ -293,6 +341,51 @@
 
 def shape_of(shape, dtype=f32):
     return jax.ShapeDtypeStruct(shape, dtype)
+
+
+def kept(shape, dtype=f32):
+    return pltpu.HBM(shape, dtype)
+
+
+def from_hbm(value):
+    return pltpu.with_memory_space_constraint(value, pltpu.HBM)
+
+
+def prepare_kernel(
+    window, live_ref, x_ref, grad_ref, gain_ref, shift_ref, pad_ref, xn_ref, gout_ref, xs_ref, gs_ref
+):
+    rows = x_ref.shape[0]
+    windows, padded, _ = pad_ref.shape
+    live = lax.broadcasted_iota(jnp.int32, (rows, 1), 0) < live_ref[0]
+    xs_ref[:rows, :] = x_ref[...].astype(f32)
+    gs_ref[:rows, :] = jnp.where(live, grad_ref[...].astype(f32), 0.0)
+    xs_ref[rows:, :] = jnp.zeros_like(xs_ref[rows:, :])
+    gs_ref[rows:, :] = jnp.zeros_like(gs_ref[rows:, :])
+    real = lax.broadcasted_iota(jnp.int32, (padded, 1), 0) < window
+    gain = gain_ref[...]
+    shift = shift_ref[...]
+    for w in range(windows):
+        taken = slice(w * window, w * window + padded)
+        values = xs_ref[taken, :]
+        pad_ref[w] = jnp.where(real, values, 0.0).astype(bf16)
+        xn_ref[w] = jnp.where(real, norm_forward(values, gain, shift)[0], 0.0).astype(bf16)
+        gout_ref[w] = jnp.where(real, gs_ref[taken, :], 0.0).astype(bf16)
+
+
+def prepare(live, x, grad, gain, shift, window, padded):
+    rows, width = x.shape
+    shape = (rows // window, padded, width)
+    held = -(-(rows - window + padded) // ROW_TILE) * ROW_TILE
+    outs = pl.pallas_call(
+        functools.partial(prepare_kernel, window),
+        in_specs=[pl.BlockSpec(memory_space=pltpu.SMEM)]
+        + [pl.BlockSpec(memory_space=pltpu.VMEM)] * 4,
+        out_shape=[shape_of(shape, bf16)] * 3,
+        scratch_shapes=[pltpu.VMEM((held, width), f32)] * 2,
+        name="prepare",
+        compiler_params=pltpu.CompilerParams(vmem_limit_bytes=VMEM_ROWS),
+    )(live.reshape(1), x, grad, gain, shift)
+    return [out.reshape(-1, width) for out in outs]
 
 
 def enter_kernel(count, *refs):
@@ -406,10 +499,6 @@
             got.append(swap(got[m ^ low], low))
         return got
 
-    def pad_rows(value):
-        value = value.reshape(windows, window, -1)
-        return jnp.pad(value, ((0, 0), (0, padded - window), (0, 0))).reshape(n, -1)
-
     def cut_rows(value):
         return value.reshape(windows, padded, -1)[:, :window].reshape(rows, -1)
 
@@ -428,12 +517,11 @@
     w1s = gather(w_fc1)
     w2s = gather(w_fc2)
 
-    row_ids = me * rows + jnp.arange(rows, dtype=jnp.int32)
-    live = (row_ids // IMG_TOKENS < image_count[0])[:, None]
-    xn1 = norm_forward(inputs.astype(f32), norm1_gain, norm1_shift)[0].astype(bf16)
-    xn1 = pad_rows(xn1)
-    x_pad = pad_rows(inputs)
-    gout = pad_rows(jnp.where(live, out_grad, jnp.zeros_like(out_grad)))
+    live_rows = image_count[0] * IMG_TOKENS - me * rows
+    live = (jnp.arange(rows, dtype=jnp.int32) < live_rows)[:, None]
+    x_pad, xn1, gout = prepare(
+        live_rows, inputs, out_grad, row(norm1_gain), row(norm1_shift), window, padded
+    )
 
     order = range(shards)
     qkvs, probs, atts = [], [], []
@@ -446,9 +534,9 @@
     mid, xn2 = by_rows(
         functools.partial(enter_kernel, shards),
         n,
-        [x_pad] + atts,
+        [from_hbm(v) for v in [x_pad] + atts],
         [row(b_proj), row(norm2_gain), row(norm2_shift)] + wps,
-        [shape_of((n, width)), shape_of((n, width), bf16)],
+        [kept((n, width)), shape_of((n, width), bf16)],
         [],
         2 * n * width * width,
     )
@@ -456,16 +544,17 @@
     ff = w_fc1.shape[1]
     hiddens, dpres, g_b1s, g_fcs = {}, {}, {}, {}
     back_order = list(reversed(order))
-    for m in back_order:
+    for m in mlp_order(shards):
         hiddens[m], dpres[m], g_b1s[m], g_fcs[m] = by_rows(
             functools.partial(mlp_kernel, bias_qv.size),
             n,
             [xn2, gout],
             [w1s[m], vectors[m], w2s[m]],
-            [shape_of((n, ff), bf16), shape_of((n, ff), bf16)],
+            [kept((n, ff), bf16), kept((n, ff), bf16)],
             [shape_of((1, ff)), shape_of((2 * ff, width), bf16)],
             8 * n * width * ff,
             [pltpu.VMEM((2 * ff, width), f32)],
+            n,
         )
 
     def scatter(parts):
@@ -525,9 +614,9 @@
     dmid, dmid_b, sums2 = by_rows(
         functools.partial(mid_back_kernel, shards),
         n,
-        [mid, gout] + listed(dpres),
+        [from_hbm(v) for v in [mid, gout] + listed(dpres)],
         [row(norm2_gain), row(norm2_shift)] + w1s,
-        [shape_of((n, width)), shape_of((n, width), bf16)],
+        [kept((n, width)), shape_of((n, width), bf16)],
         [shape_of((8, width))],
         2 * n * width * ff * shards,
     )
@@ -544,7 +633,7 @@
     in_grad, sums1 = by_rows(
         functools.partial(in_back_kernel, shards),
         n,
-        [x_pad, dmid] + listed(dqkvs),
+        [from_hbm(v) for v in [x_pad, dmid] + listed(dqkvs)],
         [row(norm1_gain), row(norm1_shift)] + wqs,
         [shape_of((n, width), bf16)],
         [shape_of((8, width))],
@@ -553,7 +642,7 @@
     (outputs,) = by_rows(
         functools.partial(leave_kernel, shards),
         n,
-        [mid] + listed(hiddens),
+        [from_hbm(v) for v in [mid] + listed(hiddens)],
         [row(b_fc2)] + w2s,
         [shape_of((n, width), bf16)],
         [],
@@ -613,6 +702,10 @@
     )
 
 
+def mlp_order(shards):
+    return [1] * (shards > 1) + [m for m in range(shards - 1, -1, -1) if m != 1]
+
+
 def solution(mesh):
     placed = (
         P(("dp", "tensor"), None),

time: 243 us -> 216 us (0.89)
  Pallas kernels: 120 us -> 90.8 us
  waiting for transfers between devices: 40 us -> 50.9 us
  local copies, waits for them, and re-layouts: 25.8 us -> 22.1 us
    pallas_call x8, Pallas kernels: 55.8 us -> 40.6 us  [by_rows(): pl.pallas_call(kernel, grid=(rows // chunk,), in_specs=[cut_spec(v) for v...]
    ppermute x19, waiting for transfers between devices: 12.2 us -> 20.1 us  [swap_dp(): return lax.ppermute(value, 'dp', [(i, i ^ bits) for i in range(groups)])]
    pallas_call x4, Pallas kernels: 8.42 us -> 2.95 us  [merge(): pl.pallas_call(functools.partial(merge_kernel, ways), in_specs=[pl.BlockS...]
    pallas_call x4, Pallas kernels: 9.21 us -> 4.26 us  [split(): pl.pallas_call(functools.partial(split_kernel, len(values)), in_specs=[pl...]
    unnamed x121 -> x111, local copies, waits for them, and re-layouts: 12.3 us -> 16.7 us
    pallas_call x8 -> x9, Pallas kernels: 46.4 us -> 43.1 us  [the longest x4 26.1 us: attend_back(): pl.pallas_call(functools.partial(attend_back_kernel, heads, scale), grid=...]
    pad x3 -> x0, local copies, waits for them, and re-layouts: 3.27 us -> none  [pad_rows(): return jnp.pad(value, ((0, 0), (0, padded - window), (0, 0))).reshape(n, -1)]
    ppermute x27, waiting for transfers between devices: 27.8 us -> 30.8 us  [swap(): return lax.ppermute(value, 'tensor', [(i, i ^ bit) for i in range(shards)])]
  transfers between devices with their start and end apart: 46 -> 46, of which waited for: 9 -> 10; matrix products, arithmetic and copies ran while one was open for 11% -> 7% of each run, Pallas kernels for 48% -> 41%
where the time goes in v3:
time: 216 us; the launch traced here: 215 us
  Pallas kernels  90.8 us (42%)
  waiting for transfers between devices  50.9 us (24%)
  starting transfers between devices  41.3 us (19%)
  local copies, waits for them, and re-layouts  22.1 us (10%)
  matrix products  4.5 us (2%)
  other arithmetic  3.97 us (2%)
    pallas_call x8, Pallas kernels, by_rows(): pl.pallas_call(kernel, grid=(rows // chunk,), in_specs=[cut_spec(v) for v...  40.6 us
    ppermute x27, waiting for transfers between devices, swap(): return lax.ppermute(value, 'tensor', [(i, i ^ bit) for i in range(shards)])  30.8 us
    ppermute x19, starting transfers between devices, swap_dp(): return lax.ppermute(value, 'dp', [(i, i ^ bits) for i in range(groups)])  26.2 us
    pallas_call x4, Pallas kernels, attend_back(): pl.pallas_call(functools.partial(attend_back_kernel, heads, scale), grid=...  26.1 us
    ppermute x19, waiting for transfers between devices, swap_dp(): return lax.ppermute(value, 'dp', [(i, i ^ bits) for i in range(groups)])  20.1 us
    unnamed x111, local copies, waits for them, and re-layouts  16.7 us
    pallas_call x4, Pallas kernels, attend(): pl.pallas_call(functools.partial(attend_kernel, heads, scale), grid=(wind...  15.5 us
    ppermute x27, starting transfers between devices, swap(): return lax.ppermute(value, 'tensor', [(i, i ^ bit) for i in range(shards)])  15.1 us
  transfers between devices with their start and end apart: 46, of which 10 were waited for; matrix products, arithmetic and copies ran while one was open for 7% of the time, Pallas kernels for 41%

profile of v3, /device:TPU:0, one launch (start us, length us, event | category | flops | bytes accessed | tf_op | source)
XLA Modules:
  0.0 215.5 jit_solution(16599298061808675373)
XLA Ops:
  1.3 2.6 %collective-permute-start.3 = (bf16[3,512,128]{2,1,0:T(8,128)(2,1)}, bf16[3,512,128]{2,1,0:T(8,128)(2,1)S(1)}, u32[]{:S(2)}, u32[]{:S(2)}) collective-permute-start(bf16[3,512,128]{2,1,0:T(8,128)(2,1)} %refs_8_.5), channel_id=1, source_target_pairs={{0,2},{1,3},{2,0},{3,1},{4,6},{5,7},{6,4},{7,5},{8,10},{9,11},{10,... | collective-permute-start | bytes 1179656 | tf_op jit(solution)/shard_map/ppermute | solution.py:493
  3.8 0.8 copy.44
  5.3 2.8 %fusion.1 = f32[64,64,4]{0,2,1:T(4,128)S(1)} fusion(s32[64,64]{0,1:T(8,128)S(1)} %pad.4.clone, f32[169,4]{0,1:T(4,128)S(1)} %copy-done), kind=kOutput, calls=%fused_computation.2 | convolution fusion | flops 33918976 | bytes 84624 | tf_op jit(solution)/shard_map/qkt,th->khq/dot_general | solution.py:509
  8.8 1.9 collective-permute-start.4
  11.3 3.9 %collective-permute-done.4.vec_ref = f32[1,768]{1,0:T(1,128)S(1)} collective-permute-done((f32[1,768]{1,0:T(1,128)S(1)}, f32[1,768]{1,0:T(1,128)S(1)}, u32[]{:S(2)}, u32[]{:S(2)}) %collective-permute-start.4) | collective-permute-done | bytes 3104 | tf_op jit(solution)/shard_map/ppermute | solution.py:493
  18.1 1.7 collective-permute-start.10
  22.8 0.8 collective-permute-done.10.refs_10_.wp_ref
  23.6 1.7 collective-permute-start.15
  27.2 1.1 copy-done.15
  29.7 1.4 prepare.1
  31.2 1.0 copy-done.2
  32.1 1.0 copy-done.4
  33.2 0.8 copy-done.20
  34.0 0.7 copy-done.30
  34.7 3.8 %attend.4 = (bf16[3,16,64,128]{3,2,1,0:T(8,128)(2,1)}, f32[16,64,256]{2,1,0:T(8,128)}, bf16[16,64,128]{2,1,0:T(8,128)(2,1)}) custom-call(bf16[1024,512]{1,0:T(8,128)(2,1)S(1)} %bitcast.58, bf16[3,512,128]{2,1,0:T(8,128)(2,1)S(1)} %copy-done.3, f32[1,768]{1,0:T(1,128)S(1)} %copy-done.30, f32[64,256]{1,0:T(8,128)S(1)} %copy-done.20), custom_call_target="tpu_custom_call" | custom-call | flops 402653184 | bytes 2097152 | tf_op jit(solution)/shard_map/attend/pallas_call | solution.py:119
  38.5 0.8 copy-done.22
  40.1 3.9 %attend.6 = (bf16[3,16,64,128]{3,2,1,0:T(8,128)(2,1)}, f32[16,64,256]{2,1,0:T(8,128)}, bf16[16,64,128]{2,1,0:T(8,128)(2,1)}) custom-call(bf16[1024,512]{1,0:T(8,128)(2,1)S(1)} %bitcast.59, bf16[3,512,128]{2,1,0:T(8,128)(2,1)S(1)} %collective-permute-done.3.w_ref.refs_10_, f32[1,768]{1,0:T(1,128)S(1)} %copy-done.40, f32[64,256]{1,0:T(8,128)S(1)} %copy-done.22), custom_call_target="tpu_custom_call" | custom-call | flops 402653184 | bytes 2097152 | tf_op jit(solution)/shard_map/attend/pallas_call | solution.py:119
  43.9 0.8 copy-done.26
  44.8 3.8 %attend.5 = (bf16[3,16,64,128]{3,2,1,0:T(8,128)(2,1)}, f32[16,64,256]{2,1,0:T(8,128)}, bf16[16,64,128]{2,1,0:T(8,128)(2,1)}) custom-call(bf16[1024,512]{1,0:T(8,128)(2,1)S(1)} %bitcast.60, bf16[3,512,128]{2,1,0:T(8,128)(2,1)S(1)} %collective-permute-done.w_ref.refs_9_, f32[1,768]{1,0:T(1,128)S(1)} %copy-done.43, f32[64,256]{1,0:T(8,128)S(1)} %copy-done.26), custom_call_target="tpu_custom_call" | custom-call | flops 402653184 | bytes 2097152 | tf_op jit(solution)/shard_map/attend/pallas_call | solution.py:119
  48.6 3.9 %attend.7 = (bf16[3,16,64,128]{3,2,1,0:T(8,128)(2,1)}, f32[16,64,256]{2,1,0:T(8,128)}, bf16[16,64,128]{2,1,0:T(8,128)(2,1)}) custom-call(bf16[1024,512]{1,0:T(8,128)(2,1)S(1)} %bitcast.61, bf16[3,512,128]{2,1,0:T(8,128)(2,1)S(1)} %collective-permute-done.6.w_ref.refs_11_, f32[1,768]{1,0:T(1,128)S(1)} %copy-done.38, f32[64,256]{1,0:T(8,128)S(1)} %copy-done.28), custom_call_target="tpu_custom_call" | custom-call | flops 402653184 | bytes 2097152 | tf_op jit(solution)/shard_map/attend/pallas_call | solution.py:119
  53.2 4.2 %shard_map.280 = (f32[1024,512]{1,0:T(8,128)}, bf16[1024,512]{1,0:T(8,128)(2,1)S(1)}) custom-call(bf16[1024,512]{1,0:T(8,128)(2,1)} %bitcast.66, bf16[1024,128]{1,0:T(8,128)(2,1)} %bitcast.74, bf16[1024,128]{1,0:T(8,128)(2,1)} %bitcast.78, bf16[1024,128]{1,0:T(8,128)(2,1)} %bitcast.76, bf16[1024,128]{1,0:T(8,128)(2,1)} %bitcast.80, f32[1,512]{1,0:T(1,128)S(1)} %bitcast.96, ...), custom_call_target="tpu_custom_call" | custom-call | flops 536870912 | bytes 2097152 | tf_op jit(solution)/shard_map/pallas_call | solution.py:326
  57.4 4.9 %shard_map.282 = (bf16[1024,512]{1,0:T(8,128)(2,1)}, bf16[1024,512]{1,0:T(8,128)(2,1)}, f32[1,512]{1,0:T(1,128)S(1)}, bf16[1024,512]{1,0:T(8,128)(2,1)}) custom-call(bf16[1024,512]{1,0:T(8,128)(2,1)S(1)} %get-tuple-element.96.xn_ref, bf16[1024,512]{1,0:T(8,128)(2,1)S(1)} %bitcast.70, bf16[512,512]{1,0:T(8,128)(2,1)} %collective-permute-done.12.w1_ref.refs_9_, ...), custom_call_target="tpu_custom_call" | custom-call | flops 2147483648 | bytes 2097152 | tf_op jit(solution)/shard_map/pallas_call | solution.py:326
  62.7 4.4 %shard_map.281 = (bf16[1024,512]{1,0:T(8,128)(2,1)}, bf16[1024,512]{1,0:T(8,128)(2,1)}, f32[1,512]{1,0:T(1,128)S(1)}, bf16[1024,512]{1,0:T(8,128)(2,1)S(1)}) custom-call(bf16[1024,512]{1,0:T(8,128)(2,1)S(1)} %get-tuple-element.96.xn_ref, bf16[1024,512]{1,0:T(8,128)(2,1)S(1)} %bitcast.71, bf16[512,512]{1,0:T(8,128)(2,1)} %refs_8_.4, f32[1,768]{1,0:T(1,128)S(1)} %copy-done.30, ...), custom_call_target="tpu_custom_call" | custom-call | flops 2147483648 | bytes 2097152 | tf_op jit(solution)/shard_map/pallas_call | solution.py:326
  67.2 4.9 %shard_map.283 = (bf16[1024,512]{1,0:T(8,128)(2,1)}, bf16[1024,512]{1,0:T(8,128)(2,1)}, f32[1,512]{1,0:T(1,128)S(1)}, bf16[1024,512]{1,0:T(8,128)(2,1)S(1)}) custom-call(bf16[1024,512]{1,0:T(8,128)(2,1)S(1)} %get-tuple-element.96.xn_ref, bf16[1024,512]{1,0:T(8,128)(2,1)S(1)} %bitcast.72, bf16[512,512]{1,0:T(8,128)(2,1)} %collective-permute-done.14.w1_ref.refs_10_, ...), custom_call_target="tpu_custom_call" | custom-call | flops 2147483648 | bytes 2097152 | tf_op jit(solution)/shard_map/pallas_call | solution.py:326
  72.1 3.0 %shard_map.284 = (bf16[1024,512]{1,0:T(8,128)(2,1)}, bf16[1024,512]{1,0:T(8,128)(2,1)}, f32[1,512]{1,0:T(1,128)S(1)}, bf16[1024,512]{1,0:T(8,128)(2,1)S(1)}) custom-call(bf16[1024,512]{1,0:T(8,128)(2,1)S(1)} %get-tuple-element.96.xn_ref, bf16[1024,512]{1,0:T(8,128)(2,1)S(1)} %bitcast.73, bf16[512,512]{1,0:T(8,128)(2,1)S(1)} %collective-permute-done.16.w1_ref.refs_11_, ...), custom_call_target="tpu_custom_call" | custom-call | flops 2147483648 | bytes 2097152 | tf_op jit(solution)/shard_map/pallas_call | solution.py:326
  75.2 7.4 %shard_map.286 = (f32[1024,512]{1,0:T(8,128)}, bf16[1024,512]{1,0:T(8,128)(2,1)S(1)}, f32[8,512]{1,0:T(8,128)S(1)}) custom-call(f32[1024,512]{1,0:T(8,128)} %get-tuple-element.95.refs_0_, bf16[1024,512]{1,0:T(8,128)(2,1)} %bitcast.69, bf16[1024,512]{1,0:T(8,128)(2,1)} %get-tuple-element.102.refs_2_, bf16[1024,512]{1,0:T(8,128)(2,1)} %get-tuple-element.103.refs_3_, ...), custom_call_target="tpu_custom_call" | custom-call | flops 2147483648 | bytes 7340032 | tf_op jit(solution)/shard_map/pallas_call | solution.py:326
  82.6 6.5 %attend_back.7 = (bf16[16,64,384]{2,1,0:T(8,128)(2,1)}, bf16[512,512]{1,0:T(8,128)(2,1)S(1)}, f32[64,256]{1,0:T(8,128)S(1)}, f32[2,128]{1,0:T(2,128)S(1)}) custom-call(bf16[1024,512]{1,0:T(8,128)(2,1)S(1)} %get-tuple-element.107.dmid_ref, bf16[1024,512]{1,0:T(8,128)(2,1)S(1)} %bitcast.62, bf16[128,512]{1,0:T(8,128)(2,1)S(1)} %collective-permute-done.11.refs_11_.wp_ref, ...), custom_call_target="tpu_custom_call" | custom-call | flops 1073741824 | bytes 2097152 | tf_op jit(solution)/shard_map/attend_back/pallas_call | solution.py:206
  90.2 6.5 %attend_back.5 = (bf16[16,64,384]{2,1,0:T(8,128)(2,1)}, bf16[512,512]{1,0:T(8,128)(2,1)S(1)}, f32[64,256]{1,0:T(8,128)S(1)}, f32[2,128]{1,0:T(2,128)S(1)}) custom-call(bf16[1024,512]{1,0:T(8,128)(2,1)S(1)} %get-tuple-element.107.dmid_ref, bf16[1024,512]{1,0:T(8,128)(2,1)S(1)} %bitcast.63, bf16[128,512]{1,0:T(8,128)(2,1)S(1)} %copy-done.18, ...), custom_call_target="tpu_custom_call" | custom-call | flops 1073741824 | bytes 2097152 | tf_op jit(solution)/shard_map/attend_back/pallas_call | solution.py:206
  96.8 6.5 %attend_back.4 = (bf16[16,64,384]{2,1,0:T(8,128)(2,1)}, bf16[512,512]{1,0:T(8,128)(2,1)S(1)}, f32[64,256]{1,0:T(8,128)S(1)}, f32[2,128]{1,0:T(2,128)S(1)}) custom-call(bf16[1024,512]{1,0:T(8,128)(2,1)S(1)} %get-tuple-element.107.dmid_ref, bf16[1024,512]{1,0:T(8,128)(2,1)S(1)} %bitcast.64, bf16[128,512]{1,0:T(8,128)(2,1)S(1)} %copy-done.16, ...), custom_call_target="tpu_custom_call" | custom-call | flops 1073741824 | bytes 2097152 | tf_op jit(solution)/shard_map/attend_back/pallas_call | solution.py:206
  103.4 6.5 %attend_back.6 = (bf16[16,64,384]{2,1,0:T(8,128)(2,1)}, bf16[512,512]{1,0:T(8,128)(2,1)S(1)}, f32[64,256]{1,0:T(8,128)S(1)}, f32[2,128]{1,0:T(2,128)S(1)}) custom-call(bf16[1024,512]{1,0:T(8,128)(2,1)S(1)} %get-tuple-element.107.dmid_ref, bf16[1024,512]{1,0:T(8,128)(2,1)S(1)} %bitcast.65, bf16[128,512]{1,0:T(8,128)(2,1)} %collective-permute-done.10.refs_10_.wp_ref, ...), custom_call_target="tpu_custom_call" | custom-call | flops 1073741824 | bytes 2097152 | tf_op jit(solution)/shard_map/attend_back/pallas_call | solution.py:206
  109.9 6.3 %shard_map.287 = (bf16[1024,512]{1,0:T(8,128)(2,1)S(1)}, f32[8,512]{1,0:T(8,128)S(1)}) custom-call(bf16[1024,512]{1,0:T(8,128)(2,1)} %bitcast.67, f32[1024,512]{1,0:T(8,128)} %get-tuple-element.106.refs_1_, bf16[1024,384]{1,0:T(8,128)(2,1)} %bitcast.103, bf16[1024,384]{1,0:T(8,128)(2,1)} %bitcast.102, bf16[1024,384]{1,0:T(8,128)(2,1)} %bitcast.104, ...), custom_call_target="tpu_custom_call" | custom-call | flops 1610612736 | bytes 6291456 | tf_op jit(solution)/shard_map/pallas_call | solution.py:326
  116.8 1.3 add.53
  118.0 1.7 collective-permute-start.36
  119.8 11.4 %collective-permute-done.19.refs_1_ = bf16[512,512]{1,0:T(8,128)(2,1)S(1)} collective-permute-done((bf16[512,512]{1,0:T(8,128)(2,1)S(1)}, bf16[512,512]{1,0:T(8,128)(2,1)S(1)}, u32[]{:S(2)}, u32[]{:S(2)}) %collective-permute-start.19) | collective-permute-done | bytes 524320 | tf_op jit(solution)/shard_map/ppermute | solution.py:493
  131.2 0.8 split.4
  132.5 1.7 fusion.6
  136.5 1.8 collective-permute-start.27
  138.3 1.6 collective-permute-start.28
  139.9 13.7 %collective-permute-done.22 = f32[4516]{0:T(1024)S(1)} collective-permute-done((f32[4516]{0:T(1024)S(1)}, f32[4516]{0:T(1024)S(1)}, u32[]{:S(2)}, u32[]{:S(2)}) %collective-permute-start.22) | collective-permute-done | bytes 18096 | tf_op jit(solution)/shard_map/ppermute | solution.py:493
  153.6 2.5 %collective-permute-start.29 = (bf16[128,512]{1,0:T(8,128)(2,1)}, bf16[128,512]{1,0:T(8,128)(2,1)}, u32[]{:S(2)}, u32[]{:S(2)}) collective-permute-start(bf16[128,512]{1,0:T(8,128)(2,1)} %get-tuple-element.146), channel_id=1, source_target_pairs={{0,12},{4,8},{8,4},{12,0},{16,28},{20,24},{24,20},{28,16},{1,13},{... | collective-permute-start | bytes 393224 | tf_op jit(solution)/shard_map/ppermute | solution.py:574
  157.3 2.3 %split.6 = (bf16[256,512]{1,0:T(8,128)(2,1)S(1)}, bf16[256,512]{1,0:T(8,128)(2,1)}, bf16[256,512]{1,0:T(8,128)(2,1)}, bf16[256,512]{1,0:T(8,128)(2,1)}) custom-call(s32[1]{0:T(128)} %bitcast.24.digit_ref, bf16[1024,512]{1,0:T(8,128)(2,1)S(1)} %copy-done.11, bf16[1024,512]{1,0:T(8,128)(2,1)S(1)} %collective-permute-done.36.refs_1_, ...), custom_call_target="tpu_custom_call" | custom-call | tf_op jit(solution)/shard_map/split/pallas_call | solution.py:272
  159.6 1.5 collective-permute-start.38
  161.1 0.7 collective-permute-start.39
  161.8 1.4 collective-permute-start.40
  163.2 0.7 add.48
  164.0 1.5 collective-permute-start.25
  165.4 1.0 split.5
  166.4 2.7 %collective-permute-start.30 = (bf16[64,512]{1,0:T(8,128)(2,1)S(1)}, bf16[64,512]{1,0:T(8,128)(2,1)S(1)}, u32[]{:S(2)}, u32[]{:S(2)}) collective-permute-start(bf16[64,512]{1,0:T(8,128)(2,1)S(1)} %get-tuple-element.148), channel_id=1, source_target_pairs={{0,16},{4,20},{8,24},{12,28},{16,0},{20,4},{24,8},{28,12},{1,17},{... | collective-permute-start | bytes 196616 | tf_op jit(solution)/shard_map/ppermute | solution.py:574
  169.1 5.5 %shard_map.285 = bf16[1024,512]{1,0:T(8,128)(2,1)S(1)} custom-call(f32[1024,512]{1,0:T(8,128)} %get-tuple-element.95.refs_0_, bf16[1024,512]{1,0:T(8,128)(2,1)} %get-tuple-element.98.refs_1_, bf16[1024,512]{1,0:T(8,128)(2,1)} %get-tuple-element.99.refs_2_, bf16[1024,512]{1,0:T(8,128)(2,1)} %get-tuple-element.100.refs_3_, ...), custom_call_target="tpu_custom_call" | custom-call | flops 2147483648 | bytes 6291456 | tf_op jit(solution)/shard_map/pallas_call | solution.py:326
  174.6 1.1 reshape.189
  176.0 1.9 collective-permute-start.26
  178.0 1.1 collective-permute-start.41
  179.1 2.0 collective-permute-start.31
  181.1 8.4 %collective-permute-done.41 = bf16[128,512]{1,0:T(8,128)(2,1)S(1)} collective-permute-done((bf16[128,512]{1,0:T(8,128)(2,1)S(1)}, bf16[128,512]{1,0:T(8,128)(2,1)S(1)}, u32[]{:S(2)}, u32[]{:S(2)}) %collective-permute-start.41) | collective-permute-done | bytes 131104 | tf_op jit(solution)/shard_map/ppermute | solution.py:574
  189.6 1.1 broadcast_select_fusion
  190.7 1.1 reshape.195
  191.9 2.4 %collective-permute-start.34 = (bf16[128,512]{1,0:T(8,128)(2,1)S(1)}, bf16[128,512]{1,0:T(8,128)(2,1)S(1)}, u32[]{:S(2)}, u32[]{:S(2)}) collective-permute-start(bf16[128,512]{1,0:T(8,128)(2,1)S(1)} %merge.4.refs_0_), channel_id=1, source_target_pairs={{0,12},{4,8},{8,4},{12,0},{16,28},{20,24},{24,20},{28,16},{1,13},{... | collective-permute-start | bytes 393224 | tf_op jit(solution)/shard_map/ppermute | solution.py:574
  194.3 1.7 collective-permute-done.42.refs_1_
  196.1 2.6 %collective-permute-start.44 = (bf16[256,512]{1,0:T(8,128)(2,1)S(1)}, bf16[256,512]{1,0:T(8,128)(2,1)S(1)}, u32[]{:S(2)}, u32[]{:S(2)}) collective-permute-start(bf16[256,512]{1,0:T(8,128)(2,1)S(1)} %merge.6.refs_0_), channel_id=1, source_target_pairs={{0,8},{4,12},{8,0},{12,4},{16,24},{20,28},{24,16},{28,20},{1,9},{5... | collective-permute-start | bytes 786440 | tf_op jit(solution)/shard_map/ppermute | solution.py:574
  198.6 0.9 collective-permute-start.43
  201.0 1.1 collective-permute-start.32
  202.8 9.8 %collective-permute-done.33.refs_2_ = bf16[128,512]{1,0:T(8,128)(2,1)S(1)} collective-permute-done((bf16[128,512]{1,0:T(8,128)(2,1)S(1)}, bf16[128,512]{1,0:T(8,128)(2,1)S(1)}, u32[]{:S(2)}, u32[]{:S(2)}) %collective-permute-start.33) | collective-permute-done | bytes 131104 | tf_op jit(solution)/shard_map/ppermute | solution.py:574
  212.6 1.1 merge.5
  213.7 1.8 merge.7
  (205 shorter events, 21.1 us)
Async XLA Ops:
  0.7 32.5 %copy-start.3 = (bf16[3,512,128]{2,1,0:T(8,128)(2,1)S(1)}, bf16[3,512,128]{2,1,0:T(8,128)(2,1)}, u32[]{:S(2)}) copy-start(bf16[3,512,128]{2,1,0:T(8,128)(2,1)} %refs_8_.5) | copy-start | bytes 1179652
  0.7 17.4 %copy-start.16 = (bf16[128,512]{1,0:T(8,128)(2,1)S(1)}, bf16[128,512]{1,0:T(8,128)(2,1)}, u32[]{:S(2)}) copy-start(bf16[128,512]{1,0:T(8,128)(2,1)} %wp_ref.1) | copy-start | bytes 393220
  0.7 26.5 %copy-start.14 = (bf16[784,512]{1,0:T(8,128)(2,1)S(1)}, bf16[784,512]{1,0:T(8,128)(2,1)}, u32[]{:S(2)}) copy-start(bf16[784,512]{1,0:T(8,128)(2,1)} %x_ref.1) | copy-start | bytes 2408452
  0.7 25.3 %collective-permute-start = (bf16[3,512,128]{2,1,0:T(8,128)(2,1)}, bf16[3,512,128]{2,1,0:T(8,128)(2,1)S(1)}, u32[]{:S(2)}, u32[]{:S(2)}) collective-permute-start(bf16[3,512,128]{2,1,0:T(8,128)(2,1)} %refs_8_.5), channel_id=1, source_target_pairs={{0,1},{1,0},{2,3},{3,2},{4,5},{5,4},{6,7},{7,6},{8,9},{9,8},{10,11... | collective-permute-start | bytes 1179656 | tf_op jit(solution)/shard_map/ppermute | solution.py:493
  1.3 20.4 %collective-permute-start.3 = (bf16[3,512,128]{2,1,0:T(8,128)(2,1)}, bf16[3,512,128]{2,1,0:T(8,128)(2,1)S(1)}, u32[]{:S(2)}, u32[]{:S(2)}) collective-permute-start(bf16[3,512,128]{2,1,0:T(8,128)(2,1)} %refs_8_.5), channel_id=1, source_target_pairs={{0,2},{1,3},{2,0},{3,1},{4,6},{5,7},{6,4},{7,5},{8,10},{9,11},{10,... | collective-permute-start | bytes 1179656 | tf_op jit(solution)/shard_map/ppermute | solution.py:493
  8.5 11.3 %collective-permute-start.5 = (f32[64,256]{1,0:T(8,128)S(1)}, f32[64,256]{1,0:T(8,128)S(1)}, u32[]{:S(2)}, u32[]{:S(2)}) collective-permute-start(f32[64,256]{1,0:T(8,128)S(1)} %reshape.178.bias_ref), channel_id=1, source_target_pairs={{0,2},{1,3},{2,0},{3,1},{4,6},{5,7},{6,4},{7,5},{8,10},{9,11},{10,... | collective-permute-start | bytes 196616 | tf_op jit(solution)/shard_map/ppermute | solution.py:493
  8.8 6.4 %collective-permute-start.4 = (f32[1,768]{1,0:T(1,128)S(1)}, f32[1,768]{1,0:T(1,128)S(1)}, u32[]{:S(2)}, u32[]{:S(2)}) collective-permute-start(f32[1,768]{1,0:T(1,128)S(1)} %reshape.177.vec_ref), channel_id=1, source_target_pairs={{0,2},{1,3},{2,0},{3,1},{4,6},{5,7},{6,4},{7,5},{8,10},{9,11},{10,... | collective-permute-start | bytes 9224 | tf_op jit(solution)/shard_map/ppermute | solution.py:493
  10.7 5.1 %collective-permute-start.1 = (f32[1,768]{1,0:T(1,128)S(1)}, f32[1,768]{1,0:T(1,128)S(1)}, u32[]{:S(2)}, u32[]{:S(2)}) collective-permute-start(f32[1,768]{1,0:T(1,128)S(1)} %reshape.177.vec_ref), channel_id=1, source_target_pairs={{0,1},{1,0},{2,3},{3,2},{4,5},{5,4},{6,7},{7,6},{8,9},{9,8},{10,11... | collective-permute-start | bytes 9224 | tf_op jit(solution)/shard_map/ppermute | solution.py:493
  15.2 2.3 %collective-permute-start.7 = (f32[1,768]{1,0:T(1,128)S(1)}, f32[1,768]{1,0:T(1,128)S(1)}, u32[]{:S(2)}, u32[]{:S(2)}) collective-permute-start(f32[1,768]{1,0:T(1,128)S(1)} %collective-permute-done.4.vec_ref), channel_id=1, source_target_pairs={{0,1},{1,0},{2,3},{3,2},{4,5},{5,4},{6,7},{7,6},{8,9},{9,8},{10,11... | collective-permute-start | bytes 9224 | tf_op jit(solution)/shard_map/ppermute | solution.py:493
  16.4 3.5 %collective-permute-start.2 = (f32[64,256]{1,0:T(8,128)S(1)}, f32[64,256]{1,0:T(8,128)S(1)}, u32[]{:S(2)}, u32[]{:S(2)}) collective-permute-start(f32[64,256]{1,0:T(8,128)S(1)} %reshape.178.bias_ref), channel_id=1, source_target_pairs={{0,1},{1,0},{2,3},{3,2},{4,5},{5,4},{6,7},{7,6},{8,9},{9,8},{10,11... | collective-permute-start | bytes 196616 | tf_op jit(solution)/shard_map/ppermute | solution.py:493
  18.1 5.5 %collective-permute-start.10 = (bf16[128,512]{1,0:T(8,128)(2,1)S(1)}, bf16[128,512]{1,0:T(8,128)(2,1)}, u32[]{:S(2)}, u32[]{:S(2)}) collective-permute-start(bf16[128,512]{1,0:T(8,128)(2,1)S(1)} %copy-done.16), channel_id=1, source_target_pairs={{0,2},{1,3},{2,0},{3,1},{4,6},{5,7},{6,4},{7,5},{8,10},{9,11},{10,... | collective-permute-start | bytes 393224 | tf_op jit(solution)/shard_map/ppermute | solution.py:493
  19.9 5.5 %collective-permute-start.9 = (bf16[128,512]{1,0:T(8,128)(2,1)S(1)}, bf16[128,512]{1,0:T(8,128)(2,1)S(1)}, u32[]{:S(2)}, u32[]{:S(2)}) collective-permute-start(bf16[128,512]{1,0:T(8,128)(2,1)S(1)} %copy-done.16), channel_id=1, source_target_pairs={{0,1},{1,0},{2,3},{3,2},{4,5},{5,4},{6,7},{7,6},{8,9},{9,8},{10,11... | collective-permute-start | bytes 393224 | tf_op jit(solution)/shard_map/ppermute | solution.py:493
  20.5 1.4 collective-permute-start.8
  21.6 11.5 %collective-permute-start.6 = (bf16[3,512,128]{2,1,0:T(8,128)(2,1)S(1)}, bf16[3,512,128]{2,1,0:T(8,128)(2,1)S(1)}, u32[]{:S(2)}, u32[]{:S(2)}) collective-permute-start(bf16[3,512,128]{2,1,0:T(8,128)(2,1)S(1)} %collective-permute-done.3.w_ref.refs_10_), channel_id=1, source_target_pairs={{0,1},{1,0},{2,3},{3,2},{4,5},{5,4},{6,7},{7,6},{8,9},{9,8},{10,11... | collective-permute-start | bytes 1179656 | tf_op jit(solution)/shard_map/ppermute | solution.py:493
  22.5 30.0 %collective-permute-start.14 = (bf16[512,512]{1,0:T(8,128)(2,1)}, bf16[512,512]{1,0:T(8,128)(2,1)}, u32[]{:S(2)}, u32[]{:S(2)}) collective-permute-start(bf16[512,512]{1,0:T(8,128)(2,1)} %refs_8_.4), channel_id=1, source_target_pairs={{0,2},{1,3},{2,0},{3,1},{4,6},{5,7},{6,4},{7,5},{8,10},{9,11},{10,... | collective-permute-start | bytes 1572872 | tf_op jit(solution)/shard_map/ppermute | solution.py:493
  23.6 29.5 %collective-permute-start.15 = (bf16[512,512]{1,0:T(8,128)(2,1)}, bf16[512,512]{1,0:T(8,128)(2,1)}, u32[]{:S(2)}, u32[]{:S(2)}) collective-permute-start(bf16[512,512]{1,0:T(8,128)(2,1)} %refs_6_.1), channel_id=1, source_target_pairs={{0,2},{1,3},{2,0},{3,1},{4,6},{5,7},{6,4},{7,5},{8,10},{9,11},{10,... | collective-permute-start | bytes 1572872 | tf_op jit(solution)/shard_map/ppermute | solution.py:493
  26.0 31.4 %collective-permute-start.12 = (bf16[512,512]{1,0:T(8,128)(2,1)}, bf16[512,512]{1,0:T(8,128)(2,1)}, u32[]{:S(2)}, u32[]{:S(2)}) collective-permute-start(bf16[512,512]{1,0:T(8,128)(2,1)} %refs_8_.4), channel_id=1, source_target_pairs={{0,1},{1,0},{2,3},{3,2},{4,5},{5,4},{6,7},{7,6},{8,9},{9,8},{10,11... | collective-permute-start | bytes 1572872 | tf_op jit(solution)/shard_map/ppermute | solution.py:493
  26.0 31.4 %collective-permute-start.13 = (bf16[512,512]{1,0:T(8,128)(2,1)}, bf16[512,512]{1,0:T(8,128)(2,1)}, u32[]{:S(2)}, u32[]{:S(2)}) collective-permute-start(bf16[512,512]{1,0:T(8,128)(2,1)} %refs_6_.1), channel_id=1, source_target_pairs={{0,1},{1,0},{2,3},{3,2},{4,5},{5,4},{6,7},{7,6},{8,9},{9,8},{10,11... | collective-permute-start | bytes 1572872 | tf_op jit(solution)/shard_map/ppermute | solution.py:493
  33.1 10.8 %copy-start.43 = (f32[1,768]{1,0:T(1,128)S(1)}, f32[1,768]{1,0:T(1,128)}, u32[]{:S(2)}) copy-start(f32[1,768]{1,0:T(1,128)} %copy-done.42) | copy-start | bytes 9220
  33.2 20.0 %collective-permute-start.11 = (bf16[128,512]{1,0:T(8,128)(2,1)}, bf16[128,512]{1,0:T(8,128)(2,1)S(1)}, u32[]{:S(2)}, u32[]{:S(2)}) collective-permute-start(bf16[128,512]{1,0:T(8,128)(2,1)} %collective-permute-done.10.refs_10_.wp_ref), channel_id=1, source_target_pairs={{0,1},{1,0},{2,3},{3,2},{4,5},{5,4},{6,7},{7,6},{8,9},{9,8},{10,11... | collective-permute-start | bytes 393224 | tf_op jit(solution)/shard_map/ppermute | solution.py:493
  34.7 13.9 %copy-start.28 = (f32[64,256]{1,0:T(8,128)S(1)}, f32[64,256]{1,0:T(8,128)}, u32[]{:S(2)}) copy-start(f32[64,256]{1,0:T(8,128)} %copy-done.27) | copy-start | bytes 196612
  34.7 13.9 %copy-start.38 = (f32[1,768]{1,0:T(1,128)S(1)}, f32[1,768]{1,0:T(1,128)}, u32[]{:S(2)}) copy-start(f32[1,768]{1,0:T(1,128)} %copy-done.37) | copy-start | bytes 9220
  40.0 13.1 %copy-start.18 = (bf16[128,512]{1,0:T(8,128)(2,1)S(1)}, bf16[128,512]{1,0:T(8,128)(2,1)}, u32[]{:S(2)}) copy-start(bf16[128,512]{1,0:T(8,128)(2,1)} %copy-done.17) | copy-start | bytes 393220
  40.1 13.1 %copy-start.35 = (f32[512]{0:T(512)S(1)}, f32[512]{0:T(512)}, u32[]{:S(2)}) copy-start(f32[512]{0:T(512)} %param.27) | copy-start | bytes 6148
  40.1 13.1 %copy-start.36 = (f32[512]{0:T(512)S(1)}, f32[512]{0:T(512)}, u32[]{:S(2)}) copy-start(f32[512]{0:T(512)} %param.28) | copy-start | bytes 6148
  40.1 13.1 %copy-start.46 = (f32[512]{0:T(512)S(1)}, f32[512]{0:T(512)}, u32[]{:S(2)}) copy-start(f32[512]{0:T(512)} %param.26) | copy-start | bytes 6148
  48.6 8.8 %copy-start.44 = (f32[1,768]{1,0:T(1,128)S(1)}, f32[1,768]{1,0:T(1,128)}, u32[]{:S(2)}) copy-start(f32[1,768]{1,0:T(1,128)} %copy-done.42) | copy-start | bytes 9220
  52.6 19.5 %collective-permute-start.16 = (bf16[512,512]{1,0:T(8,128)(2,1)}, bf16[512,512]{1,0:T(8,128)(2,1)S(1)}, u32[]{:S(2)}, u32[]{:S(2)}) collective-permute-start(bf16[512,512]{1,0:T(8,128)(2,1)} %collective-permute-done.14.w1_ref.refs_10_), channel_id=1, source_target_pairs={{0,1},{1,0},{2,3},{3,2},{4,5},{5,4},{6,7},{7,6},{8,9},{9,8},{10,11... | collective-permute-start | bytes 1572872 | tf_op jit(solution)/shard_map/ppermute | solution.py:493
  53.1 19.0 %collective-permute-start.17 = (bf16[512,512]{1,0:T(8,128)(2,1)}, bf16[512,512]{1,0:T(8,128)(2,1)S(1)}, u32[]{:S(2)}, u32[]{:S(2)}) collective-permute-start(bf16[512,512]{1,0:T(8,128)(2,1)} %collective-permute-done.15.w2_ref.refs_8_), channel_id=1, source_target_pairs={{0,1},{1,0},{2,3},{3,2},{4,5},{5,4},{6,7},{7,6},{8,9},{9,8},{10,11... | collective-permute-start | bytes 1572872 | tf_op jit(solution)/shard_map/ppermute | solution.py:493
  62.3 94.4 %collective-permute-start.37 = (bf16[1024,512]{1,0:T(8,128)(2,1)}, bf16[1024,512]{1,0:T(8,128)(2,1)}, u32[]{:S(2)}, u32[]{:S(2)}) collective-permute-start(bf16[1024,512]{1,0:T(8,128)(2,1)} %get-tuple-element.154), channel_id=1, source_target_pairs={{0,1},{1,0},{2,3},{3,2},{4,5},{5,4},{6,7},{7,6},{8,9},{9,8},{10,11... | collective-permute-start | bytes 3145736 | tf_op jit(solution)/shard_map/ppermute | solution.py:493
  75.1 41.6 %collective-permute-start.35 = (bf16[1024,512]{1,0:T(8,128)(2,1)S(1)}, bf16[1024,512]{1,0:T(8,128)(2,1)S(1)}, u32[]{:S(2)}, u32[]{:S(2)}) collective-permute-start(bf16[1024,512]{1,0:T(8,128)(2,1)S(1)} %get-tuple-element.153), channel_id=1, source_target_pairs={{0,1},{1,0},{2,3},{3,2},{4,5},{5,4},{6,7},{7,6},{8,9},{9,8},{10,11... | collective-permute-start | bytes 3145736 | tf_op jit(solution)/shard_map/ppermute | solution.py:493
  89.8 26.4 %collective-permute-start.18 = (bf16[512,512]{1,0:T(8,128)(2,1)S(1)}, bf16[512,512]{1,0:T(8,128)(2,1)S(1)}, u32[]{:S(2)}, u32[]{:S(2)}) collective-permute-start(bf16[512,512]{1,0:T(8,128)(2,1)S(1)} %get-tuple-element.127), channel_id=1, source_target_pairs={{0,1},{1,0},{2,3},{3,2},{4,5},{5,4},{6,7},{7,6},{8,9},{9,8},{10,11... | collective-permute-start | bytes 1572872 | tf_op jit(solution)/shard_map/ppermute | solution.py:493
  96.7 23.1 %collective-permute-start.20 = (bf16[512,512]{1,0:T(8,128)(2,1)S(1)}, bf16[512,512]{1,0:T(8,128)(2,1)S(1)}, u32[]{:S(2)}, u32[]{:S(2)}) collective-permute-start(bf16[512,512]{1,0:T(8,128)(2,1)S(1)} %get-tuple-element.128), channel_id=1, source_target_pairs={{0,1},{1,0},{2,3},{3,2},{4,5},{5,4},{6,7},{7,6},{8,9},{9,8},{10,11... | collective-permute-start | bytes 1572872 | tf_op jit(solution)/shard_map/ppermute | solution.py:493
  116.4 14.9 %collective-permute-start.19 = (bf16[512,512]{1,0:T(8,128)(2,1)S(1)}, bf16[512,512]{1,0:T(8,128)(2,1)S(1)}, u32[]{:S(2)}, u32[]{:S(2)}) collective-permute-start(bf16[512,512]{1,0:T(8,128)(2,1)S(1)} %add.44), channel_id=1, source_target_pairs={{0,2},{1,3},{2,0},{3,1},{4,6},{5,7},{6,4},{7,5},{8,10},{9,11},{10,... | collective-permute-start | bytes 1572872 | tf_op jit(solution)/shard_map/ppermute | solution.py:493
  116.8 15.6 %copy-start.24 = (f32[64,256]{1,0:T(8,128)S(1)}, f32[64,256]{1,0:T(8,128)}, u32[]{:S(2)}) copy-start(f32[64,256]{1,0:T(8,128)} %copy-done.23) | copy-start | bytes 196612
  116.8 15.8 %copy-start.49 = (s32[64,64]{0,1:T(8,128)S(1)}, s32[64,64]{0,1:T(8,128)}, u32[]{:S(2)}) copy-start(s32[64,64]{0,1:T(8,128)} %copy-done.48) | copy-start | bytes 49156
  118.0 39.2 %collective-permute-start.36 = (bf16[1024,512]{1,0:T(8,128)(2,1)}, bf16[1024,512]{1,0:T(8,128)(2,1)S(1)}, u32[]{:S(2)}, u32[]{:S(2)}) collective-permute-start(bf16[1024,512]{1,0:T(8,128)(2,1)} %add.53), channel_id=1, source_target_pairs={{0,2},{1,3},{2,0},{3,1},{4,6},{5,7},{6,4},{7,5},{8,10},{9,11},{10,... | collective-permute-start | bytes 3145736 | tf_op jit(solution)/shard_map/ppermute | solution.py:493
  132.5 24.7 %copy-start.11 = (bf16[1024,512]{1,0:T(8,128)(2,1)S(1)}, bf16[1024,512]{1,0:T(8,128)(2,1)}, u32[]{:S(2)}) copy-start(bf16[1024,512]{1,0:T(8,128)(2,1)} %copy-done.10) | copy-start | bytes 3145732
  134.6 34.4 %copy-start.45 = (f32[512]{0:T(512)S(1)}, f32[512]{0:T(512)}, u32[]{:S(2)}) copy-start(f32[512]{0:T(512)} %param.32) | copy-start | bytes 6148
  135.0 1.3 collective-permute-start.21
  135.1 3.2 %collective-permute-start.23 = (f32[4516]{0:T(1024)S(1)}, f32[4516]{0:T(1024)S(1)}, u32[]{:S(2)}, u32[]{:S(2)}) collective-permute-start(f32[4516]{0:T(1024)S(1)} %get-tuple-element.179), channel_id=1, source_target_pairs={{0,1},{1,0},{2,3},{3,2},{4,5},{5,4},{6,7},{7,6},{8,9},{9,8},{10,11... | collective-permute-start | bytes 54200 | tf_op jit(solution)/shard_map/ppermute | solution.py:493
  136.3 17.3 %collective-permute-start.22 = (f32[4516]{0:T(1024)S(1)}, f32[4516]{0:T(1024)S(1)}, u32[]{:S(2)}, u32[]{:S(2)}) collective-permute-start(f32[4516]{0:T(1024)S(1)} %add.45), channel_id=1, source_target_pairs={{0,2},{1,3},{2,0},{3,1},{4,6},{5,7},{6,4},{7,5},{8,10},{9,11},{10,... | collective-permute-start | bytes 54200 | tf_op jit(solution)/shard_map/ppermute | solution.py:493
  136.5 25.3 %collective-permute-start.27 = (bf16[128,512]{1,0:T(8,128)(2,1)}, bf16[128,512]{1,0:T(8,128)(2,1)S(1)}, u32[]{:S(2)}, u32[]{:S(2)}) collective-permute-start(bf16[128,512]{1,0:T(8,128)(2,1)} %get-tuple-element.144), channel_id=1, source_target_pairs={{0,4},{4,0},{8,12},{12,8},{16,20},{20,16},{24,28},{28,24},{1,5},{5... | collective-permute-start | bytes 393224 | tf_op jit(solution)/shard_map/ppermute | solution.py:574
  138.3 25.7 %collective-permute-start.28 = (bf16[128,512]{1,0:T(8,128)(2,1)}, bf16[128,512]{1,0:T(8,128)(2,1)S(1)}, u32[]{:S(2)}, u32[]{:S(2)}) collective-permute-start(bf16[128,512]{1,0:T(8,128)(2,1)} %get-tuple-element.145), channel_id=1, source_target_pairs={{0,8},{4,12},{8,0},{12,4},{16,24},{20,28},{24,16},{28,20},{1,9},{5... | collective-permute-start | bytes 393224 | tf_op jit(solution)/shard_map/ppermute | solution.py:574
  153.6 11.8 %collective-permute-start.29 = (bf16[128,512]{1,0:T(8,128)(2,1)}, bf16[128,512]{1,0:T(8,128)(2,1)}, u32[]{:S(2)}, u32[]{:S(2)}) collective-permute-start(bf16[128,512]{1,0:T(8,128)(2,1)} %get-tuple-element.146), channel_id=1, source_target_pairs={{0,12},{4,8},{8,4},{12,0},{16,28},{20,24},{24,20},{28,16},{1,13},{... | collective-permute-start | bytes 393224 | tf_op jit(solution)/shard_map/ppermute | solution.py:574
  156.7 4.4 %collective-permute-start.24 = (f32[4516]{0:T(1024)}, f32[4516]{0:T(1024)}, u32[]{:S(2)}, u32[]{:S(2)}) collective-permute-start(f32[4516]{0:T(1024)} %add_add_fusion), channel_id=1, source_target_pairs={{0,4},{4,0},{8,12},{12,8},{16,20},{20,16},{24,28},{28,24},{1,5},{5... | collective-permute-start | bytes 54200 | tf_op jit(solution)/shard_map/ppermute | solution.py:574
  159.6 18.3 %collective-permute-start.38 = (bf16[256,512]{1,0:T(8,128)(2,1)}, bf16[256,512]{1,0:T(8,128)(2,1)S(1)}, u32[]{:S(2)}, u32[]{:S(2)}) collective-permute-start(bf16[256,512]{1,0:T(8,128)(2,1)} %get-tuple-element.156), channel_id=1, source_target_pairs={{0,4},{4,0},{8,12},{12,8},{16,20},{20,16},{24,28},{28,24},{1,5},{5... | collective-permute-start | bytes 786440 | tf_op jit(solution)/shard_map/ppermute | solution.py:574
  161.1 16.8 %collective-permute-start.39 = (bf16[256,512]{1,0:T(8,128)(2,1)}, bf16[256,512]{1,0:T(8,128)(2,1)S(1)}, u32[]{:S(2)}, u32[]{:S(2)}) collective-permute-start(bf16[256,512]{1,0:T(8,128)(2,1)} %get-tuple-element.157), channel_id=1, source_target_pairs={{0,8},{4,12},{8,0},{12,4},{16,24},{20,28},{24,16},{28,20},{1,9},{5... | collective-permute-start | bytes 786440 | tf_op jit(solution)/shard_map/ppermute | solution.py:574
  161.8 16.1 %collective-permute-start.40 = (bf16[256,512]{1,0:T(8,128)(2,1)}, bf16[256,512]{1,0:T(8,128)(2,1)S(1)}, u32[]{:S(2)}, u32[]{:S(2)}) collective-permute-start(bf16[256,512]{1,0:T(8,128)(2,1)} %get-tuple-element.158), channel_id=1, source_target_pairs={{0,12},{4,8},{8,4},{12,0},{16,28},{20,24},{24,20},{28,16},{1,13},{... | collective-permute-start | bytes 786440 | tf_op jit(solution)/shard_map/ppermute | solution.py:574
  164.0 12.0 %collective-permute-start.25 = (f32[4516]{0:T(1024)S(1)}, f32[4516]{0:T(1024)S(1)}, u32[]{:S(2)}, u32[]{:S(2)}) collective-permute-start(f32[4516]{0:T(1024)S(1)} %add.48), channel_id=1, source_target_pairs={{0,8},{4,12},{8,0},{12,4},{16,24},{20,28},{24,16},{28,20},{1,9},{5... | collective-permute-start | bytes 54200 | tf_op jit(solution)/shard_map/ppermute | solution.py:574
  166.4 12.7 %collective-permute-start.30 = (bf16[64,512]{1,0:T(8,128)(2,1)S(1)}, bf16[64,512]{1,0:T(8,128)(2,1)S(1)}, u32[]{:S(2)}, u32[]{:S(2)}) collective-permute-start(bf16[64,512]{1,0:T(8,128)(2,1)S(1)} %get-tuple-element.148), channel_id=1, source_target_pairs={{0,16},{4,20},{8,24},{12,28},{16,0},{20,4},{24,8},{28,12},{1,17},{... | collective-permute-start | bytes 196616 | tf_op jit(solution)/shard_map/ppermute | solution.py:574
  174.6 16.1 %copy-start.13 = (bf16[1024,512]{1,0:T(8,128)(2,1)S(1)}, bf16[1024,512]{1,0:T(8,128)(2,1)}, u32[]{:S(2)}) copy-start(bf16[1024,512]{1,0:T(8,128)(2,1)} %copy-done.12) | copy-start | bytes 3145732
  175.7 13.8 %copy-start.47 = (bf16[784,512]{1,0:T(8,128)(2,1)S(1)}, bf16[784,512]{1,0:T(8,128)(2,1)}, u32[]{:S(2)}) copy-start(bf16[784,512]{1,0:T(8,128)(2,1)} %reshape.189) | copy-start | bytes 2408452
  176.0 15.9 %collective-permute-start.26 = (f32[4516]{0:T(1024)S(1)}, f32[4516]{0:T(1024)S(1)}, u32[]{:S(2)}, u32[]{:S(2)}) collective-permute-start(f32[4516]{0:T(1024)S(1)} %add.49), channel_id=1, source_target_pairs={{0,16},{4,20},{8,24},{12,28},{16,0},{20,4},{24,8},{28,12},{1,17},{... | collective-permute-start | bytes 54200 | tf_op jit(solution)/shard_map/ppermute | solution.py:574
  178.0 11.4 %collective-permute-start.41 = (bf16[128,512]{1,0:T(8,128)(2,1)S(1)}, bf16[128,512]{1,0:T(8,128)(2,1)S(1)}, u32[]{:S(2)}, u32[]{:S(2)}) collective-permute-start(bf16[128,512]{1,0:T(8,128)(2,1)S(1)} %get-tuple-element.160), channel_id=1, source_target_pairs={{0,16},{4,20},{8,24},{12,28},{16,0},{20,4},{24,8},{28,12},{1,17},{... | collective-permute-start | bytes 393224 | tf_op jit(solution)/shard_map/ppermute | solution.py:574
  179.1 12.7 %collective-permute-start.31 = (bf16[64,512]{1,0:T(8,128)(2,1)S(1)}, bf16[64,512]{1,0:T(8,128)(2,1)S(1)}, u32[]{:S(2)}, u32[]{:S(2)}) collective-permute-start(bf16[64,512]{1,0:T(8,128)(2,1)S(1)} %add_convert_fusion.1.refs_0_), channel_id=1, source_target_pairs={{0,16},{4,20},{8,24},{12,28},{16,0},{20,4},{24,8},{28,12},{1,17},{... | collective-permute-start | bytes 196616 | tf_op jit(solution)/shard_map/ppermute | solution.py:574
  189.5 6.5 %collective-permute-start.42 = (bf16[128,512]{1,0:T(8,128)(2,1)S(1)}, bf16[128,512]{1,0:T(8,128)(2,1)S(1)}, u32[]{:S(2)}, u32[]{:S(2)}) collective-permute-start(bf16[128,512]{1,0:T(8,128)(2,1)S(1)} %add_convert_fusion.refs_0_), channel_id=1, source_target_pairs={{0,16},{4,20},{8,24},{12,28},{16,0},{20,4},{24,8},{28,12},{1,17},{... | collective-permute-start | bytes 393224 | tf_op jit(solution)/shard_map/ppermute | solution.py:574
  190.6 24.8 %copy-start.1 = (f32[169,4]{0,1:T(4,128)S(1)}, f32[169,4]{0,1:T(4,128)}, u32[]{:S(2)}) copy-start(f32[169,4]{0,1:T(4,128)} %param.20) | copy-start | bytes 8116
  191.9 9.1 %collective-permute-start.34 = (bf16[128,512]{1,0:T(8,128)(2,1)S(1)}, bf16[128,512]{1,0:T(8,128)(2,1)S(1)}, u32[]{:S(2)}, u32[]{:S(2)}) collective-permute-start(bf16[128,512]{1,0:T(8,128)(2,1)S(1)} %merge.4.refs_0_), channel_id=1, source_target_pairs={{0,12},{4,8},{8,4},{12,0},{16,28},{20,24},{24,20},{28,16},{1,13},{... | collective-permute-start | bytes 393224 | tf_op jit(solution)/shard_map/ppermute | solution.py:574
  196.0 17.7 %collective-permute-start.45 = (bf16[256,512]{1,0:T(8,128)(2,1)S(1)}, bf16[256,512]{1,0:T(8,128)(2,1)S(1)}, u32[]{:S(2)}, u32[]{:S(2)}) collective-permute-start(bf16[256,512]{1,0:T(8,128)(2,1)S(1)} %merge.6.refs_0_), channel_id=1, source_target_pairs={{0,12},{4,8},{8,4},{12,0},{16,28},{20,24},{24,20},{28,16},{1,13},{... | collective-permute-start | bytes 786440 | tf_op jit(solution)/shard_map/ppermute | solution.py:574
  196.1 17.6 %collective-permute-start.44 = (bf16[256,512]{1,0:T(8,128)(2,1)S(1)}, bf16[256,512]{1,0:T(8,128)(2,1)S(1)}, u32[]{:S(2)}, u32[]{:S(2)}) collective-permute-start(bf16[256,512]{1,0:T(8,128)(2,1)S(1)} %merge.6.refs_0_), channel_id=1, source_target_pairs={{0,8},{4,12},{8,0},{12,4},{16,24},{20,28},{24,16},{28,20},{1,9},{5... | collective-permute-start | bytes 786440 | tf_op jit(solution)/shard_map/ppermute | solution.py:574
  198.6 15.1 %collective-permute-start.43 = (bf16[256,512]{1,0:T(8,128)(2,1)S(1)}, bf16[256,512]{1,0:T(8,128)(2,1)S(1)}, u32[]{:S(2)}, u32[]{:S(2)}) collective-permute-start(bf16[256,512]{1,0:T(8,128)(2,1)S(1)} %merge.6.refs_0_), channel_id=1, source_target_pairs={{0,4},{4,0},{8,12},{12,8},{16,20},{20,16},{24,28},{28,24},{1,5},{5... | collective-permute-start | bytes 786440 | tf_op jit(solution)/shard_map/ppermute | solution.py:574
  201.0 11.6 %collective-permute-start.33 = (bf16[128,512]{1,0:T(8,128)(2,1)S(1)}, bf16[128,512]{1,0:T(8,128)(2,1)S(1)}, u32[]{:S(2)}, u32[]{:S(2)}) collective-permute-start(bf16[128,512]{1,0:T(8,128)(2,1)S(1)} %merge.4.refs_0_), channel_id=1, source_target_pairs={{0,8},{4,12},{8,0},{12,4},{16,24},{20,28},{24,16},{28,20},{1,9},{5... | collective-permute-start | bytes 393224 | tf_op jit(solution)/shard_map/ppermute | solution.py:574
  201.0 11.5 %collective-permute-start.32 = (bf16[128,512]{1,0:T(8,128)(2,1)S(1)}, bf16[128,512]{1,0:T(8,128)(2,1)S(1)}, u32[]{:S(2)}, u32[]{:S(2)}) collective-permute-start(bf16[128,512]{1,0:T(8,128)(2,1)S(1)} %merge.4.refs_0_), channel_id=1, source_target_pairs={{0,4},{4,0},{8,12},{12,8},{16,20},{20,16},{24,28},{28,24},{1,5},{5... | collective-permute-start | bytes 393224 | tf_op jit(solution)/shard_map/ppermute | solution.py:574
  (34 other events, 97.7 us)
